TPU v7x, 32 devices: a whole 2x2x4 slice. The times are simulated.
32 devices in a mesh: seq: 8 (over z, y), inner: 4 (over x, core).
Axes of the slice: x: 2, y: 2, z: 4, core: 2. Of those that a mesh axis runs over, the one named last changes fastest.
Arguments:
- queries: bfloat16 [8, 16, 16384], P('inner', None, 'seq'), may hold values from -24 to 24
- key_states: bfloat16 [8, 16, 16384], P('inner', None, 'seq'), may hold values from -24 to 24
- value_states: bfloat16 [128, 25, 16384], P('inner', None, 'seq'), may hold values from -48 to 48
- fractional: float32 [3, 16384], P(None, 'seq'), may hold values from 0 to 1
- block_counts: int32 [64], replicated, may hold values from 64 to 256
- neighbors: int32 [64, 3], P('seq'), may hold values from 0 to 63, as said below
- integer_wave_vectors: int32 [3, 2048], replicated, may hold values from -7 to 7, as said below
- charge_weight: bfloat16 [128, 16], P('inner'), may hold values from -0.5 to 0.5
Outputs:
- attention: bfloat16 [128, 25, 16384], P('inner', None, 'seq')
- potential: float32 [16, 16384], P(None, 'seq')
- forces: float32 [3, 16384], P(None, 'seq')
Inputs may be any that keep to these rules, and one draw needn't show every extreme that they name: `neighbors`: row g lists 3 different blocks from g - 2 to g + 2 that lie in the grid, g itself among them. `integer_wave_vectors`: no column is all zeros.
All inputs are finite; a program needn't handle non-finite values.
Results may differ from a plain program's by a relative error of at most 0.006.
Values may be sent and summed in bfloat16 or wider, within the bound.
No kernel may reach another device: no remote copies, remote signals or barrier semaphores. Data moves between devices by JAX's collectives and lax.ppermute only.
A program may use at most 64 MiB of HBM per device.

v0:
```python
import functools
import math

import jax
import jax.numpy as jnp
from jax import lax
from jax.experimental import pallas as pl
from jax.experimental.pallas import tpu as pltpu
from jax.sharding import PartitionSpec as P

BS = 256
NNB = 3
REACH = 2
PAD = 32

ewald_scale = 40.0
ewald_damp = 0.02

BF = jnp.bfloat16
F32 = jnp.float32

SIN = (6.283185302511499, -41.34170040531678, 81.60513138577247, -76.70301535353673,
       42.02592698394968, -14.899846662448152, 3.2381375038938693)
COS = (0.9999999890590217, -19.73920449945376, 64.93911745989128, -85.45013953083522,
       60.167630950695504, -25.967599247822193, 6.5286581606558824)


def params(mib, sides=False):
    return pltpu.CompilerParams(vmem_limit_bytes=mib << 20, dimension_semantics=("arbitrary",))


def dot(a, b, dims):
    return lax.dot_general(a, b, (dims, ((), ())), preferred_element_type=F32)


def horner(coeffs, u):
    total = coeffs[-1]
    for c in coeffs[-2::-1]:
        total = total * u + c
    return total


def halves(x):
    high = x.astype(BF)
    return high, (x - high.astype(F32)).astype(BF)


def score_kernel(
    heads, head_dim, head_chan, blocks,
    lists, counts, place, q_ref, own_ref, left_ref, right_ref, cw_ref,
    p_ref, scale_ref, charge_ref, kaug, v0,
):
    g = pl.program_id(0)
    first = place[0] * blocks
    chans = heads * head_chan
    total = counts.shape[0]

    @pl.when(g == 0)
    def _():
        lane = lax.broadcasted_iota(jnp.int32, (16, BS), 1)
        row = lax.broadcasted_iota(jnp.int32, (16, BS), 0)
        for b in range(blocks + 2 * REACH):
            index = first + b - REACH
            inside = (index >= 0) & (index < total)
            live = jnp.where(inside, counts[jnp.clip(index, 0, total - 1)], 0)
            if b < REACH:
                src = left_ref[:, b * BS : (b + 1) * BS]
            elif b < REACH + blocks:
                src = own_ref[:, (b - REACH) * BS : (b - REACH + 1) * BS]
            else:
                src = right_ref[:, (b - REACH - blocks) * BS : (b - REACH - blocks + 1) * BS]
            bias = jnp.where((row == 0) & (lane >= live), -1e30, 0.0).astype(BF)
            for h in range(heads):
                kaug[b, h, 0:head_dim, :] = src[h * head_dim : (h + 1) * head_dim]
                kaug[b, h, head_dim : head_dim + 16, :] = bias
            v0[b] = src[heads * head_dim : heads * head_dim + chans]

    own_count = counts[first + g]
    live_q = lax.broadcasted_iota(jnp.int32, (1, BS), 1) < own_count
    ones = jnp.where(lax.broadcasted_iota(jnp.int32, (16, BS), 0) == 0, 1.0, 0.0).astype(BF)
    charge = None
    for h in range(heads):
        q = (q_ref[h * head_dim : (h + 1) * head_dim, :].astype(F32) * head_dim ** (-0.5)).astype(BF)
        qa = jnp.concatenate([q, ones], axis=0)
        listed = [lists[g, e] - (first - REACH) for e in range(NNB)]
        scores = [dot(kaug[b, h], qa, ((0,), (0,))) for b in listed]
        top = functools.reduce(jnp.maximum, [jnp.max(s, axis=0, keepdims=True) for s in scores])
        denominator = 0.0
        mixed = 0.0
        for e, b in enumerate(listed):
            w = jnp.exp(scores[e] - top)
            denominator = denominator + jnp.sum(w, axis=0, keepdims=True)
            w16 = w.astype(BF)
            p_ref[0, h, e * BS : (e + 1) * BS, :] = w16
            mixed = mixed + dot(v0[b, h * head_chan : (h + 1) * head_chan, :], w16, ((1,), (0,)))
        scale = jnp.where(live_q, 1.0 / denominator, 0.0)
        scale_ref[0, h : h + 1, :] = scale
        att0 = (mixed * scale).astype(BF)
        part = dot(cw_ref[h * head_chan : (h + 1) * head_chan, :], att0, ((0,), (0,)))
        charge = part if charge is None else charge + part
    charge_ref[...] = charge


def scores_call(lists, counts, place, q, own, left, right, cw, heads, head_dim, head_chan, blocks):
    rows = own.shape[0]
    nq = cw.shape[1]
    atoms = q.shape[1]
    band = blocks + 2 * REACH
    whole = lambda shape: pl.BlockSpec(shape, lambda g, *_: (0,) * len(shape))
    return pl.pallas_call(
        functools.partial(score_kernel, heads, head_dim, head_chan, blocks),
        grid_spec=pltpu.PrefetchScalarGridSpec(
            num_scalar_prefetch=3,
            grid=(blocks,),
            in_specs=[
                pl.BlockSpec((heads * head_dim, BS), lambda g, *_: (0, g)),
                whole(own.shape),
                whole(left.shape),
                whole(right.shape),
                whole(cw.shape),
            ],
            out_specs=[
                pl.BlockSpec((1, heads, NNB * BS, BS), lambda g, *_: (g, 0, 0, 0)),
                pl.BlockSpec((1, heads, BS), lambda g, *_: (g, 0, 0)),
                pl.BlockSpec((nq, BS), lambda g, *_: (0, g)),
            ],
            scratch_shapes=[
                pltpu.VMEM((band, heads, head_dim + 16, BS), BF),
                pltpu.VMEM((band, heads * head_chan, BS), BF),
            ],
        ),
        out_shape=[
            jax.ShapeDtypeStruct((blocks, heads, NNB * BS, BS), BF),
            jax.ShapeDtypeStruct((blocks, heads, BS), F32),
            jax.ShapeDtypeStruct((nq, atoms), F32),
        ],
        compiler_params=params(16),
        cost_estimate=pl.CostEstimate(
            flops=blocks * heads * NNB * BS * BS * 200, transcendentals=blocks * heads * NNB * BS * BS,
            bytes_accessed=blocks * heads * NNB * BS * BS * 2,
        ),
        name="scores",
    )(lists, counts, place, q, own, left, right, cw)


def inner_kernel(heads, head_chan, comps, lists, place, *refs):
    values, (p_ref, scale_ref, out_ref) = refs[:NNB], refs[NNB:]
    for h in range(heads):
        chans = slice(h * head_chan, (h + 1) * head_chan)
        acc = 0.0
        for e in range(NNB):
            v = values[e][chans].reshape(head_chan * PAD, BS)
            acc = acc + dot(v, p_ref[0, h, e * BS : (e + 1) * BS, :], ((1,), (0,)))
        acc = acc * scale_ref[0, h : h + 1, :]
        out_ref[chans] = acc.astype(BF).reshape(head_chan, PAD, BS)


def inner_call(lists, place, v, p, scale, heads, blocks):
    chans, comps, atoms = v.shape
    steps = blocks - 2 * REACH

    def value_map(e):
        return lambda i, lists, place: (0, 0, lists[i + REACH, e] - place[0] * blocks)

    return pl.pallas_call(
        functools.partial(inner_kernel, heads, chans // heads, comps),
        grid_spec=pltpu.PrefetchScalarGridSpec(
            num_scalar_prefetch=2,
            grid=(steps,),
            in_specs=[pl.BlockSpec((chans, PAD, BS), value_map(e)) for e in range(NNB)]
            + [
                pl.BlockSpec((1, heads, NNB * BS, BS), lambda i, *_: (i + REACH, 0, 0, 0)),
                pl.BlockSpec((1, heads, BS), lambda i, *_: (i + REACH, 0, 0)),
            ],
            out_specs=pl.BlockSpec((chans, PAD, BS), lambda i, *_: (0, 0, i + REACH)),
        ),
        out_shape=jax.ShapeDtypeStruct(v.shape, BF),
        compiler_params=params(24),
        cost_estimate=pl.CostEstimate(
            flops=steps * chans * PAD * NNB * BS * BS * 2, transcendentals=0,
            bytes_accessed=steps * chans * PAD * BS * 8,
        ),
        name="inner",
    )(lists, place, v, v, v, p, scale)


def edge_block(i, blocks):
    return jnp.where(i < REACH, i, i + blocks - 2 * REACH)


def edge_kernel(
    heads, head_chan, comps, blocks, row0,
    lists, place, own_ref, left_ref, right_ref, lsmall_ref, rsmall_ref, p_ref, scale_ref, prev_ref, out_ref, vb,
):
    i = pl.program_id(0)
    chans = heads * head_chan
    most = left_ref.shape[1]

    @pl.when(i == 0)
    def _():
        for b in range(blocks):
            vb[REACH + b] = own_ref[:, :, b * BS : (b + 1) * BS]
        for big, small, base in ((left_ref, lsmall_ref, 0), (right_ref, rsmall_ref, REACH + blocks)):
            for b in range(REACH):
                cols = slice(b * BS, (b + 1) * BS)
                vb[base + b, :, 0:most, :] = big[:, :, cols]
                tail = small[row0 : row0 + chans, cols].astype(F32)
                vb[base + b, :, most:PAD, :] = jnp.broadcast_to(
                    tail[:, None, :], (chans, PAD - most, BS)
                ).astype(BF)

    g = edge_block(i, blocks)
    offset = place[0] * blocks - REACH
    for h in range(heads):
        rows = slice(h * head_chan, (h + 1) * head_chan)
        acc = 0.0
        for e in range(NNB):
            v = vb[lists[g, e] - offset, rows].reshape(head_chan * PAD, BS)
            acc = acc + dot(v, p_ref[0, h, e * BS : (e + 1) * BS, :], ((1,), (0,)))
        acc = acc * scale_ref[0, h : h + 1, :]
        out_ref[rows] = acc.astype(BF).reshape(head_chan, PAD, BS)


def edge_call(lists, place, v, left, right, lsmall, rsmall, p, scale, prev, heads, head_dim, blocks):
    chans, comps, atoms = v.shape
    whole = lambda shape: pl.BlockSpec(shape, lambda g, *_: (0,) * len(shape), pipeline_mode=pl.Buffered(1))
    row0 = heads * head_dim + chans
    return pl.pallas_call(
        functools.partial(edge_kernel, heads, chans // heads, comps, blocks, row0),
        grid_spec=pltpu.PrefetchScalarGridSpec(
            num_scalar_prefetch=2,
            grid=(2 * REACH,),
            in_specs=[
                whole((chans, PAD, atoms)),
                whole(left.shape),
                whole(right.shape),
                whole(lsmall.shape),
                whole(rsmall.shape),
                pl.BlockSpec((1, heads, NNB * BS, BS), lambda i, *_: (edge_block(i, blocks), 0, 0, 0)),
                pl.BlockSpec((1, heads, BS), lambda i, *_: (edge_block(i, blocks), 0, 0)),
                pl.BlockSpec(memory_space=pl.ANY),
            ],
            out_specs=pl.BlockSpec((chans, PAD, BS), lambda i, *_: (0, 0, edge_block(i, blocks))),
            scratch_shapes=[pltpu.VMEM((blocks + 2 * REACH, chans, PAD, BS), BF)],
        ),
        out_shape=jax.ShapeDtypeStruct(v.shape, BF),
        input_output_aliases={9: 0},
        compiler_params=params(36),
        cost_estimate=pl.CostEstimate(
            flops=2 * REACH * chans * PAD * NNB * BS * BS * 2, transcendentals=0,
            bytes_accessed=2 * REACH * chans * PAD * BS * 8,
        ),
        name="edges",
    )(lists, place, v, left, right, lsmall, rsmall, p, scale, prev)


def table_kernel(place, n_ref, f_ref, out_ref, parts):
    @pl.when(pl.program_id(0) == 0)
    def _():
        f = f_ref[...]
        high, low = halves(f)
        rest = ((f - high.astype(F32)) - low.astype(F32)).astype(BF)
        parts[...] = jnp.concatenate([high, low, rest], axis=0)

    n = n_ref[...].astype(F32).astype(BF)
    turns = dot(jnp.concatenate([n, n, n], axis=0), parts[...], ((0,), (0,)))
    r = turns - jnp.round(turns)
    u = r * r
    out_ref[0] = horner(COS, u).astype(BF)
    out_ref[1] = (horner(SIN, u) * r).astype(BF)


def table_call(place, n, f, waves):
    step = 128
    atoms = f.shape[1]
    return pl.pallas_call(
        table_kernel,
        grid_spec=pltpu.PrefetchScalarGridSpec(
            num_scalar_prefetch=1,
            grid=(waves // step,),
            in_specs=[
                pl.BlockSpec((3, step), lambda i, place: (0, place[1] * (waves // step) + i)),
                pl.BlockSpec(f.shape, lambda i, place: (0, 0)),
            ],
            out_specs=pl.BlockSpec((2, step, atoms), lambda i, place: (0, i, 0)),
            scratch_shapes=[pltpu.VMEM((9, atoms), BF)],
        ),
        out_shape=jax.ShapeDtypeStruct((2, waves, atoms), BF),
        compiler_params=params(16),
        cost_estimate=pl.CostEstimate(
            flops=waves * atoms * 400, transcendentals=0, bytes_accessed=waves * atoms * 4
        ),
        name="table",
    )(place, n, f)


def structure_kernel(inv_root, c_ref, t_ref, out_ref):
    high, low = halves(c_ref[...])
    both = jnp.concatenate([high, low], axis=0)
    s = dot(t_ref[...], both, ((1,), (1,)))
    nq = c_ref.shape[0]
    out_ref[...] = (s[:, :nq] + s[:, nq:]).T * inv_root


def structure_call(c, table, inv_root):
    rows, atoms = table.shape
    step = min(256, rows)
    nq = c.shape[0]
    return pl.pallas_call(
        functools.partial(structure_kernel, inv_root),
        grid=(rows // step,),
        in_specs=[pl.BlockSpec((nq, atoms), lambda i: (0, 0)), pl.BlockSpec((step, atoms), lambda i: (i, 0))],
        out_specs=pl.BlockSpec((nq, step), lambda i: (0, i)),
        out_shape=jax.ShapeDtypeStruct((nq, rows), F32),
        compiler_params=params(12),
        cost_estimate=pl.CostEstimate(flops=rows * atoms * 512, transcendentals=0, bytes_accessed=rows * atoms * 2),
        name="structure",
    )(c, table)


def field_kernel(place, s_ref, n_ref, c_ref, t_ref, out_ref, coeff):
    nq = c_ref.shape[0]
    waves = n_ref.shape[1]

    @pl.when(pl.program_id(0) == 0)
    def _():
        n = n_ref[...].astype(F32)
        norm = n[0:1] * n[0:1] + n[1:2] * n[1:2] + n[2:3] * n[2:3]
        weight = ewald_scale * jnp.exp(-ewald_damp * norm) / norm
        real = s_ref[:, :waves] * weight
        imag = s_ref[:, waves:] * weight
        with_cos = jnp.concatenate([real] + [-imag * n[d : d + 1] for d in range(3)], axis=0)
        with_sin = jnp.concatenate([imag] + [real * n[d : d + 1] for d in range(3)], axis=0)
        for part, x in enumerate((with_cos, with_sin)):
            high, low = halves(x)
            cols = slice(part * waves, (part + 1) * waves)
            coeff[0 : 4 * nq, cols] = high
            coeff[4 * nq :, cols] = low

    both = dot(coeff[...], t_ref[...], ((1,), (0,)))
    sums = both[: 4 * nq] + both[4 * nq :]
    c = c_ref[...]
    out_ref[0:nq, :] = sums[:nq]
    forces = [
        jnp.sum(c * sums[(d + 1) * nq : (d + 2) * nq], axis=0, keepdims=True) for d in range(3)
    ]
    out_ref[nq : nq + 8, :] = jnp.concatenate(forces + [jnp.zeros((5, c.shape[1]), F32)], axis=0)


def field_call(place, s, n, c, table, waves):
    rows, atoms = table.shape
    step = 512
    nq = c.shape[0]
    return pl.pallas_call(
        field_kernel,
        grid_spec=pltpu.PrefetchScalarGridSpec(
            num_scalar_prefetch=1,
            grid=(atoms // step,),
            in_specs=[
                pl.BlockSpec((nq, rows), lambda i, place: (0, 0)),
                pl.BlockSpec((3, waves), lambda i, place: (0, place[1])),
                pl.BlockSpec((nq, step), lambda i, place: (0, i)),
                pl.BlockSpec((rows, step), lambda i, place: (0, i)),
            ],
            out_specs=pl.BlockSpec((nq + 8, step), lambda i, place: (0, i)),
            scratch_shapes=[pltpu.VMEM((8 * nq, rows), BF)],
        ),
        out_shape=jax.ShapeDtypeStruct((nq + 8, atoms), F32),
        compiler_params=params(12),
        cost_estimate=pl.CostEstimate(flops=rows * atoms * 512, transcendentals=0, bytes_accessed=rows * atoms * 2),
        name="fields",
    )(place, s, n, c, table)


def summed(x, axis):
    size = lax.axis_size(axis)
    if size & (size - 1):
        return lax.psum(x, axis)
    step = 1
    while step < size:
        x = x + lax.ppermute(x, axis, [(i, i ^ step) for i in range(size)])
        step *= 2
    return x


def local(
    queries,
    key_states,
    value_states,
    fractional,
    block_counts,
    neighbors,
    integer_wave_vectors,
    charge_weight,
):
    heads, head_dim, atoms = queries.shape
    chans, comps, _ = value_states.shape
    blocks = atoms // BS
    nq = charge_weight.shape[1]
    waves = integer_wave_vectors.shape[1] // lax.axis_size("inner")
    inv_root = 1.0 / math.sqrt(atoms * lax.axis_size("seq"))
    place = jnp.stack([lax.axis_index("seq"), lax.axis_index("inner")]).astype(jnp.int32)
    width = REACH * BS
    count = lax.axis_size("seq")
    up = [(i, i + 1) for i in range(count - 1)]
    down = [(i + 1, i) for i in range(count - 1)]

    small = jnp.concatenate(
        [
            key_states.reshape(heads * head_dim, atoms),
            value_states[:, 0, :],
            value_states[:, comps - 1, :],
        ],
        axis=0,
    )
    small_left = lax.ppermute(small[:, atoms - width :], "seq", up)
    small_right = lax.ppermute(small[:, :width], "seq", down)
    most = comps - 1
    big_left = lax.ppermute(value_states[:, :most, atoms - width :], "seq", up)
    big_right = lax.ppermute(value_states[:, :most, :width], "seq", down)

    table = table_call(place, integer_wave_vectors, fractional, waves).reshape(2 * waves, atoms)
    weights, scale, part = scores_call(
        neighbors, block_counts, place, queries.reshape(heads * head_dim, atoms),
        small, small_left, small_right, charge_weight, heads, head_dim, chans // heads, blocks,
    )
    charges = summed(part, "inner")
    structure = summed(structure_call(charges, table, inv_root), "seq")
    fields = summed(field_call(place, structure, integer_wave_vectors, charges, table, waves), "inner")

    attention = inner_call(neighbors, place, value_states, weights, scale, heads, blocks)
    attention = edge_call(
        neighbors, place, value_states, big_left, big_right, small_left, small_right,
        weights, scale, attention, heads, head_dim, blocks,
    )
    return (attention, fields[:nq], fields[nq : nq + 3])


def solution(mesh):
    placed = (
        P("inner", None, "seq"),
        P("inner", None, "seq"),
        P("inner", None, "seq"),
        P(None, "seq"),
        P(),
        P("seq", None),
        P(),
        P("inner", None),
    )
    return jax.shard_map(
        local,
        mesh=mesh,
        in_specs=placed,
        out_specs=(P("inner", None, "seq"), P(None, "seq"), P(None, "seq")),
        check_vma=False,
    )
```

profile of v0, /device:TPU:0, one launch (start us, length us, event | category | flops | bytes accessed | tf_op | source)
XLA Modules:
  0.0 96.8 jit_solution(8887554331420384130)
XLA Ops:
  0.6 1.0 %slice_bitcast_fusion.1 = (bf16[32,2048]{1,0:T(8,128)(2,1)S(1)}, bf16[32,2048]{1,0:T(8,128)(2,1)S(1)}) fusion(bf16[32,25,2048]{2,0,1:T(8,128)(2,1)} %param.10), kind=kLoop, calls=%fused_computation.2 | loop fusion | bytes 524288 | tf_op jit(solution)/shard_map/squeeze | solution.py:411
  1.6 0.9 pad_maximum_fusion.own_ref
  2.6 4.9 %collective-permute-start.2 = (bf16[96,512]{1,0:T(8,128)(2,1)S(1)}, bf16[96,512]{1,0:T(8,128)(2,1)S(1)}, u32[]{:S(2)}, u32[]{:S(2)}) collective-permute-start(bf16[96,512]{1,0:T(8,128)(2,1)S(1)} %get-tuple-element.17), channel_id=1, source_target_pairs={{0,4},{4,8},{8,12},{12,16},{16,20},{20,24},{24,28},{1,5},{5,9},{9,... | collective-permute-start | bytes 294920 | tf_op jit(solution)/shard_map/ppermute | solution.py:416
  7.5 1.3 %collective-permute-start.3 = (bf16[96,512]{1,0:T(8,128)(2,1)S(1)}, bf16[96,512]{1,0:T(8,128)(2,1)S(1)}, u32[]{:S(2)}, u32[]{:S(2)}) collective-permute-start(bf16[96,512]{1,0:T(8,128)(2,1)S(1)} %get-tuple-element.16), channel_id=1, source_target_pairs={{4,0},{8,4},{12,8},{16,12},{20,16},{24,20},{28,24},{5,1},{9,5},{13... | collective-permute-start | bytes 294920 | tf_op jit(solution)/shard_map/ppermute | solution.py:417
  8.8 0.8 copy.20.lists
  9.6 0.8 copy.15.cw_ref
  10.3 0.1 pad_add_fusion.place
  10.4 3.6 %collective-permute-done.3.right_ref.rsmall_ref = bf16[96,512]{1,0:T(8,128)(2,1)S(1)} collective-permute-done((bf16[96,512]{1,0:T(8,128)(2,1)S(1)}, bf16[96,512]{1,0:T(8,128)(2,1)S(1)}, u32[]{:S(2)}, u32[]{:S(2)}) %collective-permute-start.3) | collective-permute-done | bytes 98336 | tf_op jit(solution)/shard_map/ppermute | solution.py:417
  14.0 0.9 copy-done.2
  14.9 0.7 copy-done.3
  15.6 10.1 %scores.1 = (bf16[8,2,768,256]{3,2,1,0:T(8,128)(2,1)S(1)}, f32[8,2,256]{2,1,0:T(2,128)S(1)}, f32[16,2048]{1,0:T(8,128)S(1)}) custom-call(s32[8,3]{1,0:T(8,128)S(1)} %copy.20.lists, s32[64]{0:T(128)S(1)} %copy-done.3, s32[2]{0:T(128)S(1)} %pad_add_fusion.place, bf16[32,2048]{1,0:T(8,128)(2,1)S(1)} %bitcast.11, bf16[96,2048]{1,0:T(8,128)(2,1)S(1)} %pad_maximum_fusion.own_ref, ...), custom_call_target="tpu_custom_call" | custom-call | flops 629145600 | bytes 6291456 | tf_op jit(solution)/shard_map/scores/pallas_call | solution.py:110
  25.8 1.9 %copy.21.refs_0_.refs_1_.refs_2_.own_ref = bf16[32,25,2048]{2,1,0:T(8,128)(2,1)S(1)} copy(bf16[32,25,2048]{2,0,1:T(8,128)(2,1)S(1)} %copy-done.4) | data formatting | bytes 6553600 | tf_op args[2]
  27.7 1.6 %collective-permute-start.5 = (f32[16,2048]{1,0:T(8,128)S(1)}, f32[16,2048]{1,0:T(8,128)S(1)}, u32[]{:S(2)}, u32[]{:S(2)}) collective-permute-start(f32[16,2048]{1,0:T(8,128)S(1)} %add.21), channel_id=1, source_target_pairs={{0,2},{1,3},{2,0},{3,1},{4,6},{5,7},{6,4},{7,5},{8,10},{9,11},{10,... | collective-permute-start | bytes 393224 | tf_op jit(solution)/shard_map/ppermute | solution.py:381
  29.3 0.1 fusion
  29.4 4.4 %collective-permute-start = (bf16[32,24,512]{2,1,0:T(8,128)(2,1)S(1)}, bf16[32,24,512]{2,1,0:T(8,128)(2,1)S(1)}, u32[]{:S(2)}, u32[]{:S(2)}) collective-permute-start(bf16[32,24,512]{2,1,0:T(8,128)(2,1)S(1)} %get-tuple-element.13), channel_id=1, source_target_pairs={{0,4},{4,8},{8,12},{12,16},{16,20},{20,24},{24,28},{1,5},{5,9},{9,... | collective-permute-start | bytes 2359304 | tf_op jit(solution)/shard_map/ppermute | solution.py:419
  33.8 1.3 %collective-permute-start.1 = (bf16[32,24,512]{2,1,0:T(8,128)(2,1)S(1)}, bf16[32,24,512]{2,1,0:T(8,128)(2,1)S(1)}, u32[]{:S(2)}, u32[]{:S(2)}) collective-permute-start(bf16[32,24,512]{2,1,0:T(8,128)(2,1)S(1)} %get-tuple-element.12), channel_id=1, source_target_pairs={{4,0},{8,4},{12,8},{16,12},{20,16},{24,20},{28,24},{5,1},{9,5},{13... | collective-permute-start | bytes 2359304 | tf_op jit(solution)/shard_map/ppermute | solution.py:420
  35.1 5.6 %table.1 = bf16[2,512,2048]{2,1,0:T(8,128)(2,1)S(1)} custom-call(s32[2]{0:T(128)S(1)} %pad_add_fusion.place, s32[3,2048]{1,0:T(4,128)S(1)} %copy-done, f32[3,2048]{1,0:T(4,128)S(1)} %copy-done.1), custom_call_target="tpu_custom_call" | custom-call | flops 419430400 | bytes 4194304 | tf_op jit(solution)/shard_map/table/pallas_call | solution.py:276
  40.8 2.1 %structure.1 = f32[16,1024]{1,0:T(8,128)S(1)} custom-call(f32[16,2048]{1,0:T(8,128)S(1)} %add.22.c_ref, bf16[1024,2048]{1,0:T(8,128)(2,1)S(1)} %bitcast.9), custom_call_target="tpu_custom_call" | custom-call | flops 1073741824 | bytes 4194304 | tf_op jit(solution)/shard_map/structure/pallas_call | solution.py:309
  42.9 2.7 %collective-permute-start.6 = (f32[16,1024]{1,0:T(8,128)S(1)}, f32[16,1024]{1,0:T(8,128)S(1)}, u32[]{:S(2)}, u32[]{:S(2)}) collective-permute-start(f32[16,1024]{1,0:T(8,128)S(1)} %structure.1), channel_id=1, source_target_pairs={{0,4},{4,0},{8,12},{12,8},{16,20},{20,16},{24,28},{28,24},{1,5},{5... | collective-permute-start | bytes 196616 | tf_op jit(solution)/shard_map/ppermute | solution.py:381
  45.6 23.5 %collective-permute-done.6 = f32[16,1024]{1,0:T(8,128)S(1)} collective-permute-done((f32[16,1024]{1,0:T(8,128)S(1)}, f32[16,1024]{1,0:T(8,128)S(1)}, u32[]{:S(2)}, u32[]{:S(2)}) %collective-permute-start.6) | collective-permute-done | bytes 65568 | tf_op jit(solution)/shard_map/ppermute | solution.py:381
  69.2 2.6 %collective-permute-start.7 = (f32[16,1024]{1,0:T(8,128)S(1)}, f32[16,1024]{1,0:T(8,128)S(1)}, u32[]{:S(2)}, u32[]{:S(2)}) collective-permute-start(f32[16,1024]{1,0:T(8,128)S(1)} %add.23), channel_id=1, source_target_pairs={{0,8},{4,12},{8,0},{12,4},{16,24},{20,28},{24,16},{28,20},{1,9},{5... | collective-permute-start | bytes 196616 | tf_op jit(solution)/shard_map/ppermute | solution.py:381
  71.8 2.3 %collective-permute-done.7 = f32[16,1024]{1,0:T(8,128)S(1)} collective-permute-done((f32[16,1024]{1,0:T(8,128)S(1)}, f32[16,1024]{1,0:T(8,128)S(1)}, u32[]{:S(2)}, u32[]{:S(2)}) %collective-permute-start.7) | collective-permute-done | bytes 65568 | tf_op jit(solution)/shard_map/ppermute | solution.py:381
  74.1 3.1 %collective-permute-start.8 = (f32[16,1024]{1,0:T(8,128)S(1)}, f32[16,1024]{1,0:T(8,128)S(1)}, u32[]{:S(2)}, u32[]{:S(2)}) collective-permute-start(f32[16,1024]{1,0:T(8,128)S(1)} %add.24), channel_id=1, source_target_pairs={{0,16},{4,20},{8,24},{12,28},{16,0},{20,4},{24,8},{28,12},{1,17},{... | collective-permute-start | bytes 196616 | tf_op jit(solution)/shard_map/ppermute | solution.py:381
  77.2 2.2 %collective-permute-done.8 = f32[16,1024]{1,0:T(8,128)S(1)} collective-permute-done((f32[16,1024]{1,0:T(8,128)S(1)}, f32[16,1024]{1,0:T(8,128)S(1)}, u32[]{:S(2)}, u32[]{:S(2)}) %collective-permute-start.8) | collective-permute-done | bytes 65568 | tf_op jit(solution)/shard_map/ppermute | solution.py:381
  79.4 2.3 %fields.1 = f32[24,2048]{1,0:T(8,128)S(1)} custom-call(s32[2]{0:T(128)S(1)} %pad_add_fusion.place, f32[16,1024]{1,0:T(8,128)S(1)} %add.25.s_ref, s32[3,2048]{1,0:T(4,128)S(1)} %copy-done, f32[16,2048]{1,0:T(8,128)S(1)} %add.22.c_ref, bf16[1024,2048]{1,0:T(8,128)(2,1)S(1)} %bitcast.10), custom_call_target="tpu_custom_call" | custom-call | flops 1073741824 | bytes 4194304 | tf_op jit(solution)/shard_map/fields/pallas_call | solution.py:354
  81.9 1.4 %collective-permute-done.9 = f32[24,2048]{1,0:T(8,128)S(1)} collective-permute-done((f32[24,2048]{1,0:T(8,128)S(1)}, f32[24,2048]{1,0:T(8,128)S(1)}, u32[]{:S(2)}, u32[]{:S(2)}) %collective-permute-start.9) | collective-permute-done | bytes 196640 | tf_op jit(solution)/shard_map/ppermute | solution.py:381
  83.3 0.6 collective-permute-start.10
  83.9 4.2 %inner.1.prev_ref = bf16[32,25,2048]{2,1,0:T(8,128)(2,1)S(1)} custom-call(s32[8,3]{1,0:T(8,128)S(1)} %copy.20.lists, s32[2]{0:T(128)S(1)} %pad_add_fusion.place, bf16[32,25,2048]{2,1,0:T(8,128)(2,1)S(1)} %copy.21.refs_0_.refs_1_.refs_2_.own_ref, bf16[32,25,2048]{2,1,0:T(8,128)(2,1)S(1)} %copy.21.refs_0_.refs_1_.refs_2_.own_ref, ...), custom_call_target="tpu_custom_call" | custom-call | flops 1610612736 | bytes 8388608 | tf_op jit(solution)/shard_map/inner/pallas_call | solution.py:165
  88.1 3.7 %edges.1 = bf16[32,25,2048]{2,1,0:T(8,128)(2,1)S(1)} custom-call(s32[8,3]{1,0:T(8,128)S(1)} %copy.20.lists, s32[2]{0:T(128)S(1)} %pad_add_fusion.place, bf16[32,25,2048]{2,1,0:T(8,128)(2,1)S(1)} %copy.21.refs_0_.refs_1_.refs_2_.own_ref, bf16[32,24,512]{2,1,0:T(8,128)(2,1)S(1)} %collective-permute-done.left_ref, ...), custom_call_target="tpu_custom_call", output_to_operand_aliasing={{}: (9, {})} | custom-call | flops 1610612736 | bytes 8388608 | tf_op jit(solution)/shard_map/edges/pallas_call | solution.py:228
  91.9 3.6 %copy.22 = bf16[32,25,2048]{2,0,1:T(8,128)(2,1)} copy(bf16[32,25,2048]{2,1,0:T(8,128)(2,1)S(1)} %edges.1) | data formatting | bytes 6553600
  95.5 0.7 slice.36
  96.2 0.6 slice.37
  (24 shorter events, 0.3 us)
Async XLA Ops:
  2.6 7.8 %collective-permute-start.2 = (bf16[96,512]{1,0:T(8,128)(2,1)S(1)}, bf16[96,512]{1,0:T(8,128)(2,1)S(1)}, u32[]{:S(2)}, u32[]{:S(2)}) collective-permute-start(bf16[96,512]{1,0:T(8,128)(2,1)S(1)} %get-tuple-element.17), channel_id=1, source_target_pairs={{0,4},{4,8},{8,12},{12,16},{16,20},{20,24},{24,28},{1,5},{5,9},{9,... | collective-permute-start | bytes 294920 | tf_op jit(solution)/shard_map/ppermute | solution.py:416
  7.5 6.5 %collective-permute-start.3 = (bf16[96,512]{1,0:T(8,128)(2,1)S(1)}, bf16[96,512]{1,0:T(8,128)(2,1)S(1)}, u32[]{:S(2)}, u32[]{:S(2)}) collective-permute-start(bf16[96,512]{1,0:T(8,128)(2,1)S(1)} %get-tuple-element.16), channel_id=1, source_target_pairs={{4,0},{8,4},{12,8},{16,12},{20,16},{24,20},{28,24},{5,1},{9,5},{13... | collective-permute-start | bytes 294920 | tf_op jit(solution)/shard_map/ppermute | solution.py:417
  14.0 0.9 copy-start.2
  14.9 0.7 copy-start.3
  15.6 10.2 %copy-start.4 = (bf16[32,25,2048]{2,0,1:T(8,128)(2,1)S(1)}, bf16[32,25,2048]{2,0,1:T(8,128)(2,1)}, u32[]{:S(2)}) copy-start(bf16[32,25,2048]{2,0,1:T(8,128)(2,1)} %param.10) | copy-start | bytes 9830404
  25.7 9.5 %copy-start = (s32[3,2048]{1,0:T(4,128)S(1)}, s32[3,2048]{1,0:T(4,128)}, u32[]{:S(2)}) copy-start(s32[3,2048]{1,0:T(4,128)} %n_ref.3) | copy-start | bytes 73732
  25.7 9.5 %copy-start.1 = (f32[3,2048]{1,0:T(4,128)S(1)}, f32[3,2048]{1,0:T(4,128)}, u32[]{:S(2)}) copy-start(f32[3,2048]{1,0:T(4,128)} %f_ref.1) | copy-start | bytes 73732
  25.7 2.0 %collective-permute-start.4 = (f32[16,2048]{1,0:T(8,128)S(1)}, f32[16,2048]{1,0:T(8,128)S(1)}, u32[]{:S(2)}, u32[]{:S(2)}) collective-permute-start(f32[16,2048]{1,0:T(8,128)S(1)} %get-tuple-element.8), channel_id=1, source_target_pairs={{0,1},{1,0},{2,3},{3,2},{4,5},{5,4},{6,7},{7,6},{8,9},{9,8},{10,11... | collective-permute-start | bytes 393224 | tf_op jit(solution)/shard_map/ppermute | solution.py:381
  27.7 13.0 %collective-permute-start.5 = (f32[16,2048]{1,0:T(8,128)S(1)}, f32[16,2048]{1,0:T(8,128)S(1)}, u32[]{:S(2)}, u32[]{:S(2)}) collective-permute-start(f32[16,2048]{1,0:T(8,128)S(1)} %add.21), channel_id=1, source_target_pairs={{0,2},{1,3},{2,0},{3,1},{4,6},{5,7},{6,4},{7,5},{8,10},{9,11},{10,... | collective-permute-start | bytes 393224 | tf_op jit(solution)/shard_map/ppermute | solution.py:381
  29.4 58.7 %collective-permute-start = (bf16[32,24,512]{2,1,0:T(8,128)(2,1)S(1)}, bf16[32,24,512]{2,1,0:T(8,128)(2,1)S(1)}, u32[]{:S(2)}, u32[]{:S(2)}) collective-permute-start(bf16[32,24,512]{2,1,0:T(8,128)(2,1)S(1)} %get-tuple-element.13), channel_id=1, source_target_pairs={{0,4},{4,8},{8,12},{12,16},{16,20},{20,24},{24,28},{1,5},{5,9},{9,... | collective-permute-start | bytes 2359304 | tf_op jit(solution)/shard_map/ppermute | solution.py:419
  33.8 54.3 %collective-permute-start.1 = (bf16[32,24,512]{2,1,0:T(8,128)(2,1)S(1)}, bf16[32,24,512]{2,1,0:T(8,128)(2,1)S(1)}, u32[]{:S(2)}, u32[]{:S(2)}) collective-permute-start(bf16[32,24,512]{2,1,0:T(8,128)(2,1)S(1)} %get-tuple-element.12), channel_id=1, source_target_pairs={{4,0},{8,4},{12,8},{16,12},{20,16},{24,20},{28,24},{5,1},{9,5},{13... | collective-permute-start | bytes 2359304 | tf_op jit(solution)/shard_map/ppermute | solution.py:420
  42.9 26.3 %collective-permute-start.6 = (f32[16,1024]{1,0:T(8,128)S(1)}, f32[16,1024]{1,0:T(8,128)S(1)}, u32[]{:S(2)}, u32[]{:S(2)}) collective-permute-start(f32[16,1024]{1,0:T(8,128)S(1)} %structure.1), channel_id=1, source_target_pairs={{0,4},{4,0},{8,12},{12,8},{16,20},{20,16},{24,28},{28,24},{1,5},{5... | collective-permute-start | bytes 196616 | tf_op jit(solution)/shard_map/ppermute | solution.py:381
  69.2 4.9 %collective-permute-start.7 = (f32[16,1024]{1,0:T(8,128)S(1)}, f32[16,1024]{1,0:T(8,128)S(1)}, u32[]{:S(2)}, u32[]{:S(2)}) collective-permute-start(f32[16,1024]{1,0:T(8,128)S(1)} %add.23), channel_id=1, source_target_pairs={{0,8},{4,12},{8,0},{12,4},{16,24},{20,28},{24,16},{28,20},{1,9},{5... | collective-permute-start | bytes 196616 | tf_op jit(solution)/shard_map/ppermute | solution.py:381
  74.1 5.3 %collective-permute-start.8 = (f32[16,1024]{1,0:T(8,128)S(1)}, f32[16,1024]{1,0:T(8,128)S(1)}, u32[]{:S(2)}, u32[]{:S(2)}) collective-permute-start(f32[16,1024]{1,0:T(8,128)S(1)} %add.24), channel_id=1, source_target_pairs={{0,16},{4,20},{8,24},{12,28},{16,0},{20,4},{24,8},{28,12},{1,17},{... | collective-permute-start | bytes 196616 | tf_op jit(solution)/shard_map/ppermute | solution.py:381
  81.8 1.5 %collective-permute-start.9 = (f32[24,2048]{1,0:T(8,128)S(1)}, f32[24,2048]{1,0:T(8,128)S(1)}, u32[]{:S(2)}, u32[]{:S(2)}) collective-permute-start(f32[24,2048]{1,0:T(8,128)S(1)} %fields.1), channel_id=1, source_target_pairs={{0,1},{1,0},{2,3},{3,2},{4,5},{5,4},{6,7},{7,6},{8,9},{9,8},{10,11... | collective-permute-start | bytes 589832 | tf_op jit(solution)/shard_map/ppermute | solution.py:381
  83.3 12.1 %collective-permute-start.10 = (f32[24,2048]{1,0:T(8,128)S(1)}, f32[24,2048]{1,0:T(8,128)S(1)}, u32[]{:S(2)}, u32[]{:S(2)}) collective-permute-start(f32[24,2048]{1,0:T(8,128)S(1)} %add.26), channel_id=1, source_target_pairs={{0,2},{1,3},{2,0},{3,1},{4,6},{5,7},{6,4},{7,5},{8,10},{9,11},{10,... | collective-permute-start | bytes 589832 | tf_op jit(solution)/shard_map/ppermute | solution.py:381
where the time goes:
time: 97.1 us; the launch traced here: 96.8 us
  waiting for transfers between devices  33.1 us (34%)
  Pallas kernels  28.1 us (29%)
  starting transfers between devices  22.5 us (23%)
  local copies, waits for them, and re-layouts  11 us (11%)
  other arithmetic  1.12 us (1%)
    ppermute x7, waiting for transfers between devices, summed(): x = x + lax.ppermute(x, axis, [(i, i ^ step) for i in range(size)])  29.5 us
    ppermute x7, starting transfers between devices, summed(): x = x + lax.ppermute(x, axis, [(i, i ^ step) for i in range(size)])  10.7 us
    pallas_call x1, Pallas kernels, scores_call(): pl.pallas_call(functools.partial(score_kernel, heads, head_dim, head_chan...  10.1 us
    unnamed x14, local copies, waits for them, and re-layouts  8.56 us
    pallas_call x1, Pallas kernels, table_call(): pl.pallas_call(table_kernel, grid_spec=pltpu.PrefetchScalarGridSpec(num_s...  5.62 us
    ppermute x1, starting transfers between devices, local(): small_left = lax.ppermute(small[:, atoms - width:], 'seq', up)  4.9 us
    ppermute x1, starting transfers between devices, local(): big_left = lax.ppermute(value_states[:, :most, atoms - width:], 'seq', up)  4.37 us
    pallas_call x1, Pallas kernels, inner_call(): pl.pallas_call(functools.partial(inner_kernel, heads, chans // heads, com...  4.21 us
  transfers between devices with their start and end apart: 11, of which 5 were waited for; matrix products, arithmetic and copies ran while one was open for 8% of the time, Pallas kernels for 19%

commit v1 on v0

v1 whole, which is shorter than its diff:
```python
import functools
import math

import jax
import jax.numpy as jnp
from jax import lax
from jax.experimental import pallas as pl
from jax.experimental.pallas import tpu as pltpu
from jax.sharding import PartitionSpec as P


BS = 256
NNB = 3
REACH = 2

ewald_scale = 40.0
ewald_damp = 0.02

BF = jnp.bfloat16
F32 = jnp.float32

SIN = (6.283185302511499, -41.34170040531678, 81.60513138577247, -76.70301535353673,
       42.02592698394968, -14.899846662448152, 3.2381375038938693)
COS = (0.9999999890590217, -19.73920449945376, 64.93911745989128, -85.45013953083522,
       60.167630950695504, -25.967599247822193, 6.5286581606558824)


def params(mib):
    return pltpu.CompilerParams(vmem_limit_bytes=mib << 20, dimension_semantics=("arbitrary",))


def dot(a, b, dims):
    return lax.dot_general(a, b, (dims, ((), ())), preferred_element_type=F32)


def horner(coeffs, u):
    total = coeffs[-1]
    for c in coeffs[-2::-1]:
        total = total * u + c
    return total


def halves(x):
    high = x.astype(BF)
    return high, (x - high.astype(F32)).astype(BF)


def span(part, blocks):
    if part == "interior":
        return blocks - 2 * REACH, lambda i: i + REACH
    return 2 * REACH, lambda i: jnp.where(i < REACH, i, i + blocks - 2 * REACH)


def score_kernel(heads, head_dim, head_chan, blocks, part, lists, counts, place, *refs):
    q_ref, k_ref, v_ref, cw_ref = refs[:4]
    sides, (p_ref, scale_ref, charge_ref, kaug, v0) = refs[4:-5], refs[-5:]
    i = pl.program_id(0)
    first = place[0] * blocks
    total = counts.shape[0]

    @pl.when(i == 0)
    def _():
        lane = lax.broadcasted_iota(jnp.int32, (16, BS), 1)
        row = lax.broadcasted_iota(jnp.int32, (16, BS), 0)
        for b in range(blocks + 2 * REACH):
            own = REACH <= b < REACH + blocks
            if not own and part == "interior":
                continue
            index = first + b - REACH
            inside = (index >= 0) & (index < total)
            live = jnp.where(inside, counts[jnp.clip(index, 0, total - 1)], 0)
            if own:
                cols = slice((b - REACH) * BS, (b - REACH + 1) * BS)
                keys, v0[b] = k_ref[:, cols], v_ref[0, :, cols]
            else:
                side = sides[0] if b < REACH else sides[1]
                at = b if b < REACH else b - REACH - blocks
                cols = slice(at * BS, (at + 1) * BS)
                keys, v0[b] = side[0 : heads * head_dim, cols], side[heads * head_dim :, cols]
            bias = jnp.where((row == 0) & (lane >= live), -1e30, 0.0).astype(BF)
            for h in range(heads):
                kaug[b, h, 0:head_dim, :] = keys[h * head_dim : (h + 1) * head_dim]
                kaug[b, h, head_dim : head_dim + 16, :] = bias

    g = span(part, blocks)[1](i)
    own_count = counts[first + g]
    live_q = lax.broadcasted_iota(jnp.int32, (1, BS), 1) < own_count
    ones = jnp.where(lax.broadcasted_iota(jnp.int32, (16, BS), 0) == 0, 1.0, 0.0).astype(BF)
    listed = [lists[e, g] - (first - REACH) for e in range(NNB)]
    charge = None
    for h in range(heads):
        q = (q_ref[h * head_dim : (h + 1) * head_dim, :].astype(F32) * head_dim ** (-0.5)).astype(BF)
        qa = jnp.concatenate([q, ones], axis=0)
        scores = [dot(kaug[b, h], qa, ((0,), (0,))) for b in listed]
        top = functools.reduce(jnp.maximum, [jnp.max(s, axis=0, keepdims=True) for s in scores])
        denominator = 0.0
        mixed = 0.0
        for e, b in enumerate(listed):
            w = jnp.exp(scores[e] - top)
            denominator = denominator + jnp.sum(w, axis=0, keepdims=True)
            w16 = w.astype(BF)
            p_ref[0, h, e * BS : (e + 1) * BS, :] = w16
            mixed = mixed + dot(v0[b, h * head_chan : (h + 1) * head_chan, :], w16, ((1,), (0,)))
        scale = jnp.where(live_q, 1.0 / denominator, 0.0)
        scale_ref[0, h : h + 1, :] = scale
        att0 = (mixed * scale).astype(BF)
        term = dot(cw_ref[:, h * head_chan : (h + 1) * head_chan], att0, ((1,), (0,)))
        charge = term if charge is None else charge + term
    charge_ref[0] = charge


def scores_call(part, lists, counts, place, q, k, v, cw, sides, heads, head_dim):
    _, chans, atoms = v.shape
    blocks = atoms // BS
    nq = cw.shape[0]
    head_chan = chans // heads
    band = blocks + 2 * REACH
    steps, at = span(part, blocks)
    whole = lambda shape: pl.BlockSpec(shape, lambda g, *_: (0,) * len(shape))
    return pl.pallas_call(
        functools.partial(score_kernel, heads, head_dim, head_chan, blocks, part),
        grid_spec=pltpu.PrefetchScalarGridSpec(
            num_scalar_prefetch=3,
            grid=(steps,),
            in_specs=[
                pl.BlockSpec((heads * head_dim, BS), lambda i, *_: (0, at(i))),
                whole(k.shape),
                whole((1, chans, atoms)),
                whole(cw.shape),
            ]
            + [whole(s.shape) for s in sides],
            out_specs=[
                pl.BlockSpec((1, heads, NNB * BS, BS), lambda i, *_: (i, 0, 0, 0)),
                pl.BlockSpec((1, heads, BS), lambda i, *_: (i, 0, 0)),
                pl.BlockSpec((1, nq, BS), lambda i, *_: (i, 0, 0)),
            ],
            scratch_shapes=[
                pltpu.VMEM((band, heads, head_dim + 16, BS), BF),
                pltpu.VMEM((band, chans, BS), BF),
            ],
        ),
        out_shape=[
            jax.ShapeDtypeStruct((steps, heads, NNB * BS, BS), BF),
            jax.ShapeDtypeStruct((steps, heads, BS), F32),
            jax.ShapeDtypeStruct((steps, nq, BS), F32),
        ],
        compiler_params=params(12),
        cost_estimate=pl.CostEstimate(
            flops=steps * heads * NNB * BS * BS * 200, transcendentals=steps * heads * NNB * BS * BS,
            bytes_accessed=steps * heads * NNB * BS * BS * 2,
        ),
    )(lists, counts, place, q, k, v, cw, *sides)


def mix(heads, head_chan, listed, band_ref, p_ref, scale_ref, out_ref):
    comps = band_ref.shape[1]
    for h in range(heads):
        rows = slice(h * head_chan, (h + 1) * head_chan)
        acc = 0.0
        for e in range(NNB):
            v = band_ref[listed[e], :, rows, :].reshape(comps * head_chan, BS)
            acc = acc + dot(v, p_ref[0, h, e * BS : (e + 1) * BS, :], ((1,), (0,)))
        acc = acc * scale_ref[0, h : h + 1, :]
        out_ref[:, rows, :] = acc.astype(BF).reshape(comps, head_chan, BS)


def interior_kernel(heads, head_chan, blocks, lists, place, v_ref, p_ref, scale_ref, out_ref, band_ref):
    i = pl.program_id(0)

    @pl.when(i == 0)
    def _():
        for b in range(blocks):
            band_ref[REACH + b] = v_ref[:, :, b * BS : (b + 1) * BS]

    g = span("interior", blocks)[1](i)
    listed = [lists[e, g] - (place[0] * blocks - REACH) for e in range(NNB)]
    mix(heads, head_chan, listed, band_ref, p_ref, scale_ref, out_ref)


def interior_call(lists, place, v, p, scale, heads):
    comps, chans, atoms = v.shape
    blocks = atoms // BS
    steps, at = span("interior", blocks)
    band = (blocks + 2 * REACH, comps, chans, BS)
    return pl.pallas_call(
        functools.partial(interior_kernel, heads, chans // heads, blocks),
        grid_spec=pltpu.PrefetchScalarGridSpec(
            num_scalar_prefetch=2,
            grid=(steps,),
            in_specs=[
                pl.BlockSpec(v.shape, lambda i, *_: (0, 0, 0), pipeline_mode=pl.Buffered(1)),
                pl.BlockSpec((1, heads, NNB * BS, BS), lambda i, *_: (i, 0, 0, 0)),
                pl.BlockSpec((1, heads, BS), lambda i, *_: (i, 0, 0)),
            ],
            out_specs=[
                pl.BlockSpec((comps, chans, BS), lambda i, *_: (0, 0, at(i))),
                pl.BlockSpec(band, lambda i, *_: (0, 0, 0, 0), pipeline_mode=pl.Buffered(1)),
            ],
        ),
        out_shape=[jax.ShapeDtypeStruct(v.shape, BF), jax.ShapeDtypeStruct(band, BF)],
        compiler_params=params(20),
        cost_estimate=pl.CostEstimate(
            flops=steps * chans * comps * NNB * BS * BS * 2, transcendentals=0,
            bytes_accessed=steps * chans * comps * BS * 8,
        ),
        name="interior",
    )(lists, place, v, p, scale)


def edge_kernel(
    heads, head_dim, head_chan, blocks, lists, place, band_in, prev, p_ref, scale_ref, lsmall, rsmall, *refs
):
    halo, (out_ref, band_ref) = refs[:-2], refs[-2:]
    i = pl.program_id(0)

    @pl.when(i == 0)
    def _():
        for b in range(blocks):
            band_ref[REACH + b] = band_in[REACH + b]
        for side, (small, base) in enumerate(((lsmall, 0), (rsmall, REACH + blocks))):
            for b in range(REACH):
                cols = slice(b * BS, (b + 1) * BS)
                band_ref[base + b, 0] = small[heads * head_dim :, cols]
                at = 1
                for piece in halo[side::2]:
                    band_ref[base + b, at : at + piece.shape[0]] = piece[:, :, cols]
                    at += piece.shape[0]

    g = span("edges", blocks)[1](i)
    listed = [lists[e, g] - (place[0] * blocks - REACH) for e in range(NNB)]
    mix(heads, head_chan, listed, band_ref, p_ref, scale_ref, out_ref)


def edge_call(lists, place, v_shape, band, prev, p, scale, lsmall, rsmall, halo, heads, head_dim):
    comps, chans, atoms = v_shape
    blocks = atoms // BS
    steps, at = span("edges", blocks)
    whole = lambda shape: pl.BlockSpec(shape, lambda g, *_: (0,) * len(shape), pipeline_mode=pl.Buffered(1))
    return pl.pallas_call(
        functools.partial(edge_kernel, heads, head_dim, chans // heads, blocks),
        grid_spec=pltpu.PrefetchScalarGridSpec(
            num_scalar_prefetch=2,
            grid=(steps,),
            in_specs=[
                whole(band.shape),
                pl.BlockSpec(memory_space=pl.ANY),
                pl.BlockSpec((1, heads, NNB * BS, BS), lambda i, *_: (i, 0, 0, 0)),
                pl.BlockSpec((1, heads, BS), lambda i, *_: (i, 0, 0)),
                whole(lsmall.shape),
                whole(rsmall.shape),
            ]
            + [whole(x.shape) for x in halo],
            out_specs=pl.BlockSpec((comps, chans, BS), lambda i, *_: (0, 0, at(i))),
            scratch_shapes=[pltpu.VMEM(band.shape, BF)],
        ),
        out_shape=jax.ShapeDtypeStruct(v_shape, BF),
        input_output_aliases={3: 0},
        compiler_params=params(24),
        cost_estimate=pl.CostEstimate(
            flops=steps * chans * comps * NNB * BS * BS * 2, transcendentals=0,
            bytes_accessed=steps * chans * comps * BS * 8,
        ),
        name="edges",
    )(lists, place, band, prev, p, scale, lsmall, rsmall, *halo)


def table_kernel(place, n_ref, f_ref, out_ref, parts):
    @pl.when(pl.program_id(0) == 0)
    def _():
        f = f_ref[...]
        high, low = halves(f)
        rest = ((f - high.astype(F32)) - low.astype(F32)).astype(BF)
        parts[...] = jnp.concatenate([high, low, rest], axis=0)

    n = n_ref[...].astype(F32).astype(BF)
    turns = dot(jnp.concatenate([n, n, n], axis=0), parts[...], ((0,), (0,)))
    r = turns - jnp.round(turns)
    u = r * r
    out_ref[0] = horner(COS, u).astype(BF)
    out_ref[1] = (horner(SIN, u) * r).astype(BF)


def table_call(place, n, f, waves):
    step = 128
    atoms = f.shape[1]
    return pl.pallas_call(
        table_kernel,
        grid_spec=pltpu.PrefetchScalarGridSpec(
            num_scalar_prefetch=1,
            grid=(waves // step,),
            in_specs=[
                pl.BlockSpec((3, step), lambda i, place: (0, place[1] * (waves // step) + i)),
                pl.BlockSpec(f.shape, lambda i, place: (0, 0)),
            ],
            out_specs=pl.BlockSpec((2, step, atoms), lambda i, place: (0, i, 0)),
            scratch_shapes=[pltpu.VMEM((9, atoms), BF)],
        ),
        out_shape=jax.ShapeDtypeStruct((2, waves, atoms), BF),
        compiler_params=params(16),
        cost_estimate=pl.CostEstimate(
            flops=waves * atoms * 400, transcendentals=0, bytes_accessed=waves * atoms * 4
        ),
        name="table",
    )(place, n, f)


def structure_kernel(inv_root, c_ref, t_ref, out_ref):
    high, low = halves(c_ref[...])
    both = jnp.concatenate([high, low], axis=0)
    s = dot(t_ref[...], both, ((1,), (1,)))
    nq = c_ref.shape[0]
    out_ref[...] = (s[:, :nq] + s[:, nq:]).T * inv_root


def structure_call(c, table, inv_root):
    rows, atoms = table.shape
    step = min(256, rows)
    nq = c.shape[0]
    return pl.pallas_call(
        functools.partial(structure_kernel, inv_root),
        grid=(rows // step,),
        in_specs=[pl.BlockSpec((nq, atoms), lambda i: (0, 0)), pl.BlockSpec((step, atoms), lambda i: (i, 0))],
        out_specs=pl.BlockSpec((nq, step), lambda i: (0, i)),
        out_shape=jax.ShapeDtypeStruct((nq, rows), F32),
        compiler_params=params(12),
        cost_estimate=pl.CostEstimate(flops=rows * atoms * 512, transcendentals=0, bytes_accessed=rows * atoms * 2),
        name="structure",
    )(c, table)


def field_kernel(place, s_ref, n_ref, c_ref, t_ref, out_ref, coeff):
    nq = c_ref.shape[0]
    waves = n_ref.shape[1]

    @pl.when(pl.program_id(0) == 0)
    def _():
        n = n_ref[...].astype(F32)
        norm = n[0:1] * n[0:1] + n[1:2] * n[1:2] + n[2:3] * n[2:3]
        weight = ewald_scale * jnp.exp(-ewald_damp * norm) / norm
        real = s_ref[:, :waves] * weight
        imag = s_ref[:, waves:] * weight
        with_cos = jnp.concatenate([real] + [-imag * n[d : d + 1] for d in range(3)], axis=0)
        with_sin = jnp.concatenate([imag] + [real * n[d : d + 1] for d in range(3)], axis=0)
        for part, x in enumerate((with_cos, with_sin)):
            high, low = halves(x)
            cols = slice(part * waves, (part + 1) * waves)
            coeff[0 : 4 * nq, cols] = high
            coeff[4 * nq :, cols] = low

    both = dot(coeff[...], t_ref[...], ((1,), (0,)))
    sums = both[: 4 * nq] + both[4 * nq :]
    c = c_ref[...]
    out_ref[0:nq, :] = sums[:nq]
    forces = [
        jnp.sum(c * sums[(d + 1) * nq : (d + 2) * nq], axis=0, keepdims=True) for d in range(3)
    ]
    out_ref[nq : nq + 8, :] = jnp.concatenate(forces + [jnp.zeros((5, c.shape[1]), F32)], axis=0)


def field_call(place, s, n, c, table, waves):
    rows, atoms = table.shape
    step = 512
    nq = c.shape[0]
    return pl.pallas_call(
        field_kernel,
        grid_spec=pltpu.PrefetchScalarGridSpec(
            num_scalar_prefetch=1,
            grid=(atoms // step,),
            in_specs=[
                pl.BlockSpec((nq, rows), lambda i, place: (0, 0)),
                pl.BlockSpec((3, waves), lambda i, place: (0, place[1])),
                pl.BlockSpec((nq, step), lambda i, place: (0, i)),
                pl.BlockSpec((rows, step), lambda i, place: (0, i)),
            ],
            out_specs=pl.BlockSpec((nq + 8, step), lambda i, place: (0, i)),
            scratch_shapes=[pltpu.VMEM((8 * nq, rows), BF)],
        ),
        out_shape=jax.ShapeDtypeStruct((nq + 8, atoms), F32),
        compiler_params=params(12),
        cost_estimate=pl.CostEstimate(flops=rows * atoms * 512, transcendentals=0, bytes_accessed=rows * atoms * 2),
        name="fields",
    )(place, s, n, c, table)


def exchanged(x, axis, step):
    size = lax.axis_size(axis)
    if step >= size:
        return x
    return x + lax.ppermute(x, axis, [(i, i ^ step) for i in range(size)])


def summed(x, axis, step=1):
    size = lax.axis_size(axis)
    assert size & (size - 1) == 0
    while step < size:
        x = exchanged(x, axis, step)
        step *= 2
    return x


def whole_step(
    queries,
    key_states,
    value_states,
    fractional,
    block_counts,
    neighbors,
    integer_wave_vectors,
    charge_weight,
):
    heads, head_dim, atoms = queries.shape
    _, comps, _ = value_states.shape
    nq = charge_weight.shape[1]
    waves = integer_wave_vectors.shape[1] // lax.axis_size("inner")
    inv_root = 1.0 / math.sqrt(atoms * lax.axis_size("seq"))
    place = jnp.stack([lax.axis_index("seq"), lax.axis_index("inner")]).astype(jnp.int32)
    width = REACH * BS
    count = lax.axis_size("seq")
    up = [(i, i + 1) for i in range(count - 1)]
    down = [(i + 1, i) for i in range(count - 1)]

    keys = key_states.reshape(heads * head_dim, atoms)
    asked = queries.reshape(heads * head_dim, atoms)
    values = value_states.transpose(1, 0, 2)
    lists = neighbors.T
    weight = charge_weight.T
    tail, head = slice(atoms - width, atoms), slice(0, width)

    def shift(pick):
        left = lax.ppermute(pick(tail), "seq", up)
        right = lax.ppermute(pick(head), "seq", down)
        return left, right

    cut = 1 + (comps - 1) * 2 // 3
    sides = shift(lambda cols: jnp.concatenate([keys[:, cols], values[0, :, cols]], axis=0))
    halo_a = shift(lambda cols: values[1:cut, :, cols])

    p_in, scale_in, charge_in = scores_call(
        "interior", lists, block_counts, place, asked, keys, values, weight, (), heads, head_dim
    )
    p_out, scale_out, charge_out = scores_call(
        "edges", lists, block_counts, place, asked, keys, values, weight, sides, heads, head_dim
    )
    table = table_call(place, integer_wave_vectors, fractional, waves).reshape(2 * waves, atoms)
    part = jnp.concatenate([charge_out[:REACH], charge_in, charge_out[REACH:]], axis=0)
    part = part.transpose(1, 0, 2).reshape(nq, atoms)
    charges = summed(part, "inner")
    structure = structure_call(charges, table, inv_root)
    structure = exchanged(structure, "seq", 1)
    later, structure = lax.optimization_barrier((values, structure))
    halo_b = shift(lambda cols: later[cut:, :, cols])
    structure = summed(structure, "seq", 2)
    fields = summed(field_call(place, structure, integer_wave_vectors, charges, table, waves), "inner")

    attention, band = interior_call(lists, place, values, p_in, scale_in, heads)
    attention = edge_call(
        lists, place, values.shape, band, attention, p_out, scale_out, *sides, halo_a + halo_b, heads, head_dim
    )
    return (attention.transpose(1, 0, 2), fields[:nq], fields[nq : nq + 3])


def solution(mesh):
    placed = (
        P("inner", None, "seq"),
        P("inner", None, "seq"),
        P("inner", None, "seq"),
        P(None, "seq"),
        P(),
        P("seq", None),
        P(),
        P("inner", None),
    )
    return jax.shard_map(
        whole_step,
        mesh=mesh,
        in_specs=placed,
        out_specs=(P("inner", None, "seq"), P(None, "seq"), P(None, "seq")),
        check_vma=False,
    )
```

time: 97.1 us -> 89.9 us (0.926)
  waiting for transfers between devices: 33.1 us -> 21.9 us
  starting transfers between devices: 22.5 us -> 29.1 us
  local copies, waits for them, and re-layouts: 11 us -> 8.79 us
    ppermute x11 -> x13, waiting for transfers between devices: 33.1 us -> 21.9 us  [the longest x3 16 us: shift(): left = lax.ppermute(pick(tail), 'seq', up)]
    ppermute x11 -> x13, starting transfers between devices: 22.5 us -> 29.1 us  [the longest x3 14 us: shift(): left = lax.ppermute(pick(tail), 'seq', up)]
    unnamed x14 -> x20, local copies, waits for them, and re-layouts: 8.56 us -> 5.78 us
    slice x4 -> x6, local copies, waits for them, and re-layouts: 1.44 us -> 2.22 us  [the longest x2 1.28 us: whole_step(): return (attention.transpose(1, 0, 2), fields[:nq], fields[nq:nq + 3])]
    pallas_call x1 -> x2, Pallas kernels: 10.1 us -> 10.7 us  [scores_call(): pl.pallas_call(functools.partial(score_kernel, heads, head_dim, head_chan...]
  transfers between devices with their start and end apart: 11 -> 13, of which waited for: 5 -> 5; matrix products, arithmetic and copies ran while one was open for 8% -> 0% of each run, Pallas kernels for 19% -> 24%
where the time goes in v1:
time: 89.9 us; the launch traced here: 89.3 us
  starting transfers between devices  29.1 us (32%)
  Pallas kernels  28.5 us (32%)
  waiting for transfers between devices  21.9 us (24%)
  local copies, waits for them, and re-layouts  8.79 us (10%)
    ppermute x3, waiting for transfers between devices, shift(): left = lax.ppermute(pick(tail), 'seq', up)  16 us
    ppermute x3, starting transfers between devices, shift(): left = lax.ppermute(pick(tail), 'seq', up)  14 us
    ppermute x7, starting transfers between devices, exchanged(): return x + lax.ppermute(x, axis, [(i, i ^ step) for i in range(size)])  11.1 us
    pallas_call x2, Pallas kernels, scores_call(): pl.pallas_call(functools.partial(score_kernel, heads, head_dim, head_chan...  10.7 us
    ppermute x7, waiting for transfers between devices, exchanged(): return x + lax.ppermute(x, axis, [(i, i ^ step) for i in range(size)])  5.84 us
    unnamed x20, local copies, waits for them, and re-layouts  5.78 us
    pallas_call x1, Pallas kernels, table_call(): pl.pallas_call(table_kernel, grid_spec=pltpu.PrefetchScalarGridSpec(num_s...  5.62 us
    pallas_call x1, Pallas kernels, edge_call(): pl.pallas_call(functools.partial(edge_kernel, heads, head_dim, chans // h...  3.89 us
  transfers between devices with their start and end apart: 13, of which 5 were waited for; matrix products, arithmetic and copies ran while one was open for 0% of the time, Pallas kernels for 24%

profile of v1, /device:TPU:0, one launch (start us, length us, event | category | flops | bytes accessed | tf_op | source)
XLA Modules:
  0.0 89.3 jit_solution(11459899207643016698)
XLA Ops:
  0.6 0.8 fusion.2
  1.4 0.8 slice_bitcast_fusion
  2.2 4.9 %collective-permute-start = (bf16[64,512]{1,0:T(8,128)(2,1)S(1)}, bf16[64,512]{1,0:T(8,128)(2,1)S(1)}, u32[]{:S(2)}, u32[]{:S(2)}) collective-permute-start(bf16[64,512]{1,0:T(8,128)(2,1)S(1)} %pad_maximum_fusion), channel_id=1, source_target_pairs={{0,4},{4,8},{8,12},{12,16},{16,20},{20,24},{24,28},{1,5},{5,9},{9,... | collective-permute-start | bytes 196616 | tf_op jit(solution)/shard_map/ppermute | solution.py:430
  7.1 1.3 %collective-permute-start.1 = (bf16[64,512]{1,0:T(8,128)(2,1)S(1)}, bf16[64,512]{1,0:T(8,128)(2,1)S(1)}, u32[]{:S(2)}, u32[]{:S(2)}) collective-permute-start(bf16[64,512]{1,0:T(8,128)(2,1)S(1)} %pad_maximum_fusion.1), channel_id=1, source_target_pairs={{4,0},{8,4},{12,8},{16,12},{20,16},{24,20},{28,24},{5,1},{9,5},{13... | collective-permute-start | bytes 196616 | tf_op jit(solution)/shard_map/ppermute | solution.py:431
  8.5 1.9 %copy-done = bf16[32,25,2048]{2,0,1:T(8,128)(2,1)S(1)} copy-done((bf16[32,25,2048]{2,0,1:T(8,128)(2,1)S(1)}, bf16[32,25,2048]{2,0,1:T(8,128)(2,1)}, u32[]{:S(2)}) %copy-start) | copy-done | bytes 3276824
  10.4 0.9 %copy-done.2 = bf16[2,16,2048]{2,1,0:T(8,128)(2,1)S(1)} copy-done((bf16[2,16,2048]{2,1,0:T(8,128)(2,1)S(1)}, bf16[2,16,2048]{2,1,0:T(8,128)(2,1)}, u32[]{:S(2)}) %copy-start.2) | copy-done | bytes 131096
  11.3 0.9 %copy-done.3 = bf16[2,16,2048]{2,1,0:T(8,128)(2,1)S(1)} copy-done((bf16[2,16,2048]{2,1,0:T(8,128)(2,1)S(1)}, bf16[2,16,2048]{2,1,0:T(8,128)(2,1)}, u32[]{:S(2)}) %copy-start.3) | copy-done | bytes 131096
  12.2 0.7 copy-done.6
  12.9 0.7 copy-done.8
  13.6 0.7 copy-done.9
  14.3 5.3 %shard_map.103 = (bf16[4,2,768,256]{3,2,1,0:T(8,128)(2,1)S(1)}, f32[4,2,256]{2,1,0:T(2,128)S(1)}, f32[4,16,256]{2,1,0:T(8,128)S(1)}) custom-call(s32[3,8]{1,0:T(4,128)S(1)} %bitcast.30, s32[64]{0:T(128)S(1)} %copy-done.9, s32[2]{0:T(128)S(1)} %pad_add_fusion.place, bf16[32,2048]{1,0:T(8,128)(2,1)S(1)} %bitcast.28, bf16[32,2048]{1,0:T(8,128)(2,1)S(1)} %bitcast.26, ...), custom_call_target="tpu_custom_call" | custom-call | flops 314572800 | bytes 3145728 | tf_op jit(solution)/shard_map/pallas_call | solution.py:120
  19.6 5.4 %shard_map.104 = (bf16[4,2,768,256]{3,2,1,0:T(8,128)(2,1)S(1)}, f32[4,2,256]{2,1,0:T(2,128)S(1)}, f32[4,16,256]{2,1,0:T(8,128)S(1)}) custom-call(s32[3,8]{1,0:T(4,128)S(1)} %bitcast.31, s32[64]{0:T(128)S(1)} %copy-done.9, s32[2]{0:T(128)S(1)} %pad_add_fusion.place, bf16[32,2048]{1,0:T(8,128)(2,1)S(1)} %bitcast.29, bf16[32,2048]{1,0:T(8,128)(2,1)S(1)} %bitcast.27, ...), custom_call_target="tpu_custom_call" | custom-call | flops 314572800 | bytes 3145728 | tf_op jit(solution)/shard_map/pallas_call | solution.py:120
  25.1 1.3 %collective-permute-done.4 = f32[16,2048]{1,0:T(8,128)S(1)} collective-permute-done((f32[16,2048]{1,0:T(8,128)S(1)}, f32[16,2048]{1,0:T(8,128)S(1)}, u32[]{:S(2)}, u32[]{:S(2)}) %collective-permute-start.4) | collective-permute-done | bytes 131104 | tf_op jit(solution)/shard_map/ppermute | solution.py:389
  26.4 1.6 %collective-permute-start.5 = (f32[16,2048]{1,0:T(8,128)S(1)}, f32[16,2048]{1,0:T(8,128)S(1)}, u32[]{:S(2)}, u32[]{:S(2)}) collective-permute-start(f32[16,2048]{1,0:T(8,128)S(1)} %add.21), channel_id=1, source_target_pairs={{0,2},{1,3},{2,0},{3,1},{4,6},{5,7},{6,4},{7,5},{8,10},{9,11},{10,... | collective-permute-start | bytes 393224 | tf_op jit(solution)/shard_map/ppermute | solution.py:389
  28.0 5.6 %table.1 = bf16[2,512,2048]{2,1,0:T(8,128)(2,1)S(1)} custom-call(s32[2]{0:T(128)S(1)} %pad_add_fusion.place, s32[3,2048]{1,0:T(4,128)S(1)} %copy-done.4, f32[3,2048]{1,0:T(4,128)S(1)} %copy-done.5), custom_call_target="tpu_custom_call" | custom-call | flops 419430400 | bytes 4194304 | tf_op jit(solution)/shard_map/table/pallas_call | solution.py:286
  33.7 2.1 %structure.1 = f32[16,1024]{1,0:T(8,128)S(1)} custom-call(f32[16,2048]{1,0:T(8,128)S(1)} %add.22.c_ref, bf16[1024,2048]{1,0:T(8,128)(2,1)S(1)} %bitcast.23), custom_call_target="tpu_custom_call" | custom-call | flops 1073741824 | bytes 4194304 | tf_op jit(solution)/shard_map/structure/pallas_call | solution.py:319
  35.8 2.7 %collective-permute-start.6 = (f32[16,1024]{1,0:T(8,128)S(1)}, f32[16,1024]{1,0:T(8,128)S(1)}, u32[]{:S(2)}, u32[]{:S(2)}) collective-permute-start(f32[16,1024]{1,0:T(8,128)S(1)} %structure.1), channel_id=1, source_target_pairs={{0,4},{4,0},{8,12},{12,8},{16,20},{20,16},{24,28},{28,24},{1,5},{5... | collective-permute-start | bytes 196616 | tf_op jit(solution)/shard_map/ppermute | solution.py:389
  38.5 2.2 %collective-permute-done.6 = f32[16,1024]{1,0:T(8,128)S(1)} collective-permute-done((f32[16,1024]{1,0:T(8,128)S(1)}, f32[16,1024]{1,0:T(8,128)S(1)}, u32[]{:S(2)}, u32[]{:S(2)}) %collective-permute-start.6) | collective-permute-done | bytes 65568 | tf_op jit(solution)/shard_map/ppermute | solution.py:389
  40.8 3.0 %collective-permute-start.9 = (f32[16,1024]{1,0:T(8,128)S(1)}, f32[16,1024]{1,0:T(8,128)S(1)}, u32[]{:S(2)}, u32[]{:S(2)}) collective-permute-start(f32[16,1024]{1,0:T(8,128)S(1)} %add.23), channel_id=1, source_target_pairs={{0,8},{4,12},{8,0},{12,4},{16,24},{20,28},{24,16},{28,20},{1,9},{5... | collective-permute-start | bytes 196616 | tf_op jit(solution)/shard_map/ppermute | solution.py:389
  43.8 2.2 %collective-permute-done.9 = f32[16,1024]{1,0:T(8,128)S(1)} collective-permute-done((f32[16,1024]{1,0:T(8,128)S(1)}, f32[16,1024]{1,0:T(8,128)S(1)}, u32[]{:S(2)}, u32[]{:S(2)}) %collective-permute-start.9) | collective-permute-done | bytes 65568 | tf_op jit(solution)/shard_map/ppermute | solution.py:389
  46.1 3.1 %collective-permute-start.10 = (f32[16,1024]{1,0:T(8,128)S(1)}, f32[16,1024]{1,0:T(8,128)S(1)}, u32[]{:S(2)}, u32[]{:S(2)}) collective-permute-start(f32[16,1024]{1,0:T(8,128)S(1)} %add.24), channel_id=1, source_target_pairs={{0,16},{4,20},{8,24},{12,28},{16,0},{20,4},{24,8},{28,12},{1,17},{... | collective-permute-start | bytes 196616 | tf_op jit(solution)/shard_map/ppermute | solution.py:389
  49.3 1.3 %collective-permute-start.3 = (bf16[16,32,512]{2,1,0:T(8,128)(2,1)S(1)}, bf16[16,32,512]{2,1,0:T(8,128)(2,1)S(1)}, u32[]{:S(2)}, u32[]{:S(2)}) collective-permute-start(bf16[16,32,512]{2,1,0:T(8,128)(2,1)S(1)} %get-tuple-element.25), channel_id=1, source_target_pairs={{4,0},{8,4},{12,8},{16,12},{20,16},{24,20},{28,24},{5,1},{9,5},{13... | collective-permute-start | bytes 1572872 | tf_op jit(solution)/shard_map/ppermute | solution.py:431
  50.6 4.6 %collective-permute-start.2 = (bf16[16,32,512]{2,1,0:T(8,128)(2,1)S(1)}, bf16[16,32,512]{2,1,0:T(8,128)(2,1)S(1)}, u32[]{:S(2)}, u32[]{:S(2)}) collective-permute-start(bf16[16,32,512]{2,1,0:T(8,128)(2,1)S(1)} %get-tuple-element.26), channel_id=1, source_target_pairs={{0,4},{4,8},{8,12},{12,16},{16,20},{20,24},{24,28},{1,5},{5,9},{9,... | collective-permute-start | bytes 1572872 | tf_op jit(solution)/shard_map/ppermute | solution.py:430
  55.2 2.3 %fields.1 = f32[24,2048]{1,0:T(8,128)S(1)} custom-call(s32[2]{0:T(128)S(1)} %pad_add_fusion.place, f32[16,1024]{1,0:T(8,128)S(1)} %add.25.s_ref, s32[3,2048]{1,0:T(4,128)S(1)} %copy-done.4, f32[16,2048]{1,0:T(8,128)S(1)} %add.22.c_ref, bf16[1024,2048]{1,0:T(8,128)(2,1)S(1)} %bitcast.24), custom_call_target="tpu_custom_call" | custom-call | flops 1073741824 | bytes 4194304 | tf_op jit(solution)/shard_map/fields/pallas_call | solution.py:364
  57.7 1.3 %collective-permute-start.8 = (bf16[8,32,512]{2,1,0:T(8,128)(2,1)S(1)}, bf16[8,32,512]{2,1,0:T(8,128)(2,1)S(1)}, u32[]{:S(2)}, u32[]{:S(2)}) collective-permute-start(bf16[8,32,512]{2,1,0:T(8,128)(2,1)S(1)} %get-tuple-element.23), channel_id=1, source_target_pairs={{4,0},{8,4},{12,8},{16,12},{20,16},{24,20},{28,24},{5,1},{9,5},{13... | collective-permute-start | bytes 786440 | tf_op jit(solution)/shard_map/ppermute | solution.py:431
  59.0 4.6 %collective-permute-start.7 = (bf16[8,32,512]{2,1,0:T(8,128)(2,1)S(1)}, bf16[8,32,512]{2,1,0:T(8,128)(2,1)S(1)}, u32[]{:S(2)}, u32[]{:S(2)}) collective-permute-start(bf16[8,32,512]{2,1,0:T(8,128)(2,1)S(1)} %get-tuple-element.24), channel_id=1, source_target_pairs={{0,4},{4,8},{8,12},{12,16},{16,20},{20,24},{24,28},{1,5},{5,9},{9,... | collective-permute-start | bytes 786440 | tf_op jit(solution)/shard_map/ppermute | solution.py:430
  64.2 3.8 %interior.1 = (bf16[25,32,2048]{2,1,0:T(8,128)(2,1)}, bf16[12,25,32,256]{3,2,1,0:T(8,128)(2,1)S(1)}) custom-call(s32[3,8]{1,0:T(4,128)S(1)} %bitcast.32, s32[2]{0:T(128)S(1)} %pad_add_fusion.place, bf16[25,32,2048]{2,1,0:T(8,128)(2,1)S(1)} %bitcast.22, bf16[4,2,768,256]{3,2,1,0:T(8,128)(2,1)S(1)} %get-tuple-element.13.p_ref, ...), custom_call_target="tpu_custom_call" | custom-call | flops 1258291200 | bytes 6553600 | tf_op jit(solution)/shard_map/interior/pallas_call | solution.py:185
  68.1 10.5 %collective-permute-done.2.refs_0_ = bf16[16,32,512]{2,1,0:T(8,128)(2,1)S(1)} collective-permute-done((bf16[16,32,512]{2,1,0:T(8,128)(2,1)S(1)}, bf16[16,32,512]{2,1,0:T(8,128)(2,1)S(1)}, u32[]{:S(2)}, u32[]{:S(2)}) %collective-permute-start.2) | collective-permute-done | bytes 524320 | tf_op jit(solution)/shard_map/ppermute | solution.py:430
  78.6 5.5 %collective-permute-done.7.refs_2_ = bf16[8,32,512]{2,1,0:T(8,128)(2,1)S(1)} collective-permute-done((bf16[8,32,512]{2,1,0:T(8,128)(2,1)S(1)}, bf16[8,32,512]{2,1,0:T(8,128)(2,1)S(1)}, u32[]{:S(2)}, u32[]{:S(2)}) %collective-permute-start.7) | collective-permute-done | bytes 262176 | tf_op jit(solution)/shard_map/ppermute | solution.py:430
  84.1 3.9 %edges.1 = bf16[25,32,2048]{2,1,0:T(8,128)(2,1)} custom-call(s32[3,8]{1,0:T(4,128)S(1)} %bitcast.33, s32[2]{0:T(128)S(1)} %pad_add_fusion.place, bf16[12,25,32,256]{3,2,1,0:T(8,128)(2,1)S(1)} %get-tuple-element.15.band_in, bf16[25,32,2048]{2,1,0:T(8,128)(2,1)} %get-tuple-element.16.prev, ...), custom_call_target="tpu_custom_call", output_to_operand_aliasing={{}: (3, {})} | custom-call | flops 1258291200 | bytes 6553600 | tf_op jit(solution)/shard_map/edges/pallas_call | solution.py:239
  88.0 0.6 slice.55
  88.7 0.7 slice.54
  (40 shorter events, 1.2 us)
Async XLA Ops:
  2.2 17.4 %collective-permute-start = (bf16[64,512]{1,0:T(8,128)(2,1)S(1)}, bf16[64,512]{1,0:T(8,128)(2,1)S(1)}, u32[]{:S(2)}, u32[]{:S(2)}) collective-permute-start(bf16[64,512]{1,0:T(8,128)(2,1)S(1)} %pad_maximum_fusion), channel_id=1, source_target_pairs={{0,4},{4,8},{8,12},{12,16},{16,20},{20,24},{24,28},{1,5},{5,9},{9,... | collective-permute-start | bytes 196616 | tf_op jit(solution)/shard_map/ppermute | solution.py:430
  7.1 12.5 %collective-permute-start.1 = (bf16[64,512]{1,0:T(8,128)(2,1)S(1)}, bf16[64,512]{1,0:T(8,128)(2,1)S(1)}, u32[]{:S(2)}, u32[]{:S(2)}) collective-permute-start(bf16[64,512]{1,0:T(8,128)(2,1)S(1)} %pad_maximum_fusion.1), channel_id=1, source_target_pairs={{4,0},{8,4},{12,8},{16,12},{20,16},{24,20},{28,24},{5,1},{9,5},{13... | collective-permute-start | bytes 196616 | tf_op jit(solution)/shard_map/ppermute | solution.py:431
  8.5 1.9 %copy-start = (bf16[32,25,2048]{2,0,1:T(8,128)(2,1)S(1)}, bf16[32,25,2048]{2,0,1:T(8,128)(2,1)}, u32[]{:S(2)}) copy-start(bf16[32,25,2048]{2,0,1:T(8,128)(2,1)} %param.10) | copy-start | bytes 9830404
  10.4 0.9 %copy-start.2 = (bf16[2,16,2048]{2,1,0:T(8,128)(2,1)S(1)}, bf16[2,16,2048]{2,1,0:T(8,128)(2,1)}, u32[]{:S(2)}) copy-start(bf16[2,16,2048]{2,1,0:T(8,128)(2,1)} %param.9) | copy-start | bytes 393220
  11.3 0.9 %copy-start.3 = (bf16[2,16,2048]{2,1,0:T(8,128)(2,1)S(1)}, bf16[2,16,2048]{2,1,0:T(8,128)(2,1)}, u32[]{:S(2)}) copy-start(bf16[2,16,2048]{2,1,0:T(8,128)(2,1)} %param.8) | copy-start | bytes 393220
  12.2 0.7 copy-start.6
  12.9 0.7 copy-start.8
  13.6 0.7 copy-start.9
  14.3 13.7 %copy-start.4 = (s32[3,2048]{1,0:T(4,128)S(1)}, s32[3,2048]{1,0:T(4,128)}, u32[]{:S(2)}) copy-start(s32[3,2048]{1,0:T(4,128)} %n_ref.3) | copy-start | bytes 73732
  14.3 13.7 %copy-start.5 = (f32[3,2048]{1,0:T(4,128)S(1)}, f32[3,2048]{1,0:T(4,128)}, u32[]{:S(2)}) copy-start(f32[3,2048]{1,0:T(4,128)} %f_ref.1) | copy-start | bytes 73732
  25.0 1.4 %collective-permute-start.4 = (f32[16,2048]{1,0:T(8,128)S(1)}, f32[16,2048]{1,0:T(8,128)S(1)}, u32[]{:S(2)}, u32[]{:S(2)}) collective-permute-start(f32[16,2048]{1,0:T(8,128)S(1)} %bitcast.37), channel_id=1, source_target_pairs={{0,1},{1,0},{2,3},{3,2},{4,5},{5,4},{6,7},{7,6},{8,9},{9,8},{10,11... | collective-permute-start | bytes 393224 | tf_op jit(solution)/shard_map/ppermute | solution.py:389
  26.4 7.2 %collective-permute-start.5 = (f32[16,2048]{1,0:T(8,128)S(1)}, f32[16,2048]{1,0:T(8,128)S(1)}, u32[]{:S(2)}, u32[]{:S(2)}) collective-permute-start(f32[16,2048]{1,0:T(8,128)S(1)} %add.21), channel_id=1, source_target_pairs={{0,2},{1,3},{2,0},{3,1},{4,6},{5,7},{6,4},{7,5},{8,10},{9,11},{10,... | collective-permute-start | bytes 393224 | tf_op jit(solution)/shard_map/ppermute | solution.py:389
  33.6 15.5 %copy-start.1 = (bf16[32,25,2048]{2,0,1:T(8,128)(2,1)S(1)}, bf16[32,25,2048]{2,0,1:T(8,128)(2,1)}, u32[]{:S(2)}) copy-start(bf16[32,25,2048]{2,0,1:T(8,128)(2,1)} %param.10) | copy-start | bytes 9830404
  35.8 4.9 %collective-permute-start.6 = (f32[16,1024]{1,0:T(8,128)S(1)}, f32[16,1024]{1,0:T(8,128)S(1)}, u32[]{:S(2)}, u32[]{:S(2)}) collective-permute-start(f32[16,1024]{1,0:T(8,128)S(1)} %structure.1), channel_id=1, source_target_pairs={{0,4},{4,0},{8,12},{12,8},{16,20},{20,16},{24,28},{28,24},{1,5},{5... | collective-permute-start | bytes 196616 | tf_op jit(solution)/shard_map/ppermute | solution.py:389
  40.8 5.3 %collective-permute-start.9 = (f32[16,1024]{1,0:T(8,128)S(1)}, f32[16,1024]{1,0:T(8,128)S(1)}, u32[]{:S(2)}, u32[]{:S(2)}) collective-permute-start(f32[16,1024]{1,0:T(8,128)S(1)} %add.23), channel_id=1, source_target_pairs={{0,8},{4,12},{8,0},{12,4},{16,24},{20,28},{24,16},{28,20},{1,9},{5... | collective-permute-start | bytes 196616 | tf_op jit(solution)/shard_map/ppermute | solution.py:389
  46.1 9.1 %collective-permute-start.10 = (f32[16,1024]{1,0:T(8,128)S(1)}, f32[16,1024]{1,0:T(8,128)S(1)}, u32[]{:S(2)}, u32[]{:S(2)}) collective-permute-start(f32[16,1024]{1,0:T(8,128)S(1)} %add.24), channel_id=1, source_target_pairs={{0,16},{4,20},{8,24},{12,28},{16,0},{20,4},{24,8},{28,12},{1,17},{... | collective-permute-start | bytes 196616 | tf_op jit(solution)/shard_map/ppermute | solution.py:389
  49.3 14.9 %copy-start.7 = (s32[8,3]{0,1:T(4,128)S(1)}, s32[8,3]{0,1:T(4,128)}, u32[]{:S(2)}) copy-start(s32[8,3]{0,1:T(4,128)} %param.13) | copy-start | bytes 292
  49.3 18.8 %collective-permute-start.3 = (bf16[16,32,512]{2,1,0:T(8,128)(2,1)S(1)}, bf16[16,32,512]{2,1,0:T(8,128)(2,1)S(1)}, u32[]{:S(2)}, u32[]{:S(2)}) collective-permute-start(bf16[16,32,512]{2,1,0:T(8,128)(2,1)S(1)} %get-tuple-element.25), channel_id=1, source_target_pairs={{4,0},{8,4},{12,8},{16,12},{20,16},{24,20},{28,24},{5,1},{9,5},{13... | collective-permute-start | bytes 1572872 | tf_op jit(solution)/shard_map/ppermute | solution.py:431
  50.6 28.0 %collective-permute-start.2 = (bf16[16,32,512]{2,1,0:T(8,128)(2,1)S(1)}, bf16[16,32,512]{2,1,0:T(8,128)(2,1)S(1)}, u32[]{:S(2)}, u32[]{:S(2)}) collective-permute-start(bf16[16,32,512]{2,1,0:T(8,128)(2,1)S(1)} %get-tuple-element.26), channel_id=1, source_target_pairs={{0,4},{4,8},{8,12},{12,16},{16,20},{20,24},{24,28},{1,5},{5,9},{9,... | collective-permute-start | bytes 1572872 | tf_op jit(solution)/shard_map/ppermute | solution.py:430
  57.6 6.0 %collective-permute-start.11 = (f32[24,2048]{1,0:T(8,128)S(1)}, f32[24,2048]{1,0:T(8,128)S(1)}, u32[]{:S(2)}, u32[]{:S(2)}) collective-permute-start(f32[24,2048]{1,0:T(8,128)S(1)} %fields.1), channel_id=1, source_target_pairs={{0,1},{1,0},{2,3},{3,2},{4,5},{5,4},{6,7},{7,6},{8,9},{9,8},{10,11... | collective-permute-start | bytes 589832 | tf_op jit(solution)/shard_map/ppermute | solution.py:389
  57.7 20.9 %collective-permute-start.8 = (bf16[8,32,512]{2,1,0:T(8,128)(2,1)S(1)}, bf16[8,32,512]{2,1,0:T(8,128)(2,1)S(1)}, u32[]{:S(2)}, u32[]{:S(2)}) collective-permute-start(bf16[8,32,512]{2,1,0:T(8,128)(2,1)S(1)} %get-tuple-element.23), channel_id=1, source_target_pairs={{4,0},{8,4},{12,8},{16,12},{20,16},{24,20},{28,24},{5,1},{9,5},{13... | collective-permute-start | bytes 786440 | tf_op jit(solution)/shard_map/ppermute | solution.py:431
  59.0 25.1 %collective-permute-start.7 = (bf16[8,32,512]{2,1,0:T(8,128)(2,1)S(1)}, bf16[8,32,512]{2,1,0:T(8,128)(2,1)S(1)}, u32[]{:S(2)}, u32[]{:S(2)}) collective-permute-start(bf16[8,32,512]{2,1,0:T(8,128)(2,1)S(1)} %get-tuple-element.24), channel_id=1, source_target_pairs={{0,4},{4,8},{8,12},{12,16},{16,20},{20,24},{24,28},{1,5},{5,9},{9,... | collective-permute-start | bytes 786440 | tf_op jit(solution)/shard_map/ppermute | solution.py:430
  63.6 24.4 %collective-permute-start.12 = (f32[24,2048]{1,0:T(8,128)S(1)}, f32[24,2048]{1,0:T(8,128)S(1)}, u32[]{:S(2)}, u32[]{:S(2)}) collective-permute-start(f32[24,2048]{1,0:T(8,128)S(1)} %add.26), channel_id=1, source_target_pairs={{0,2},{1,3},{2,0},{3,1},{4,6},{5,7},{6,4},{7,5},{8,10},{9,11},{10,... | collective-permute-start | bytes 589832 | tf_op jit(solution)/shard_map/ppermute | solution.py:389

commit v2 on v1

v2 whole, which is shorter than its diff:
```python
import functools
import math

import jax
import jax.numpy as jnp
from jax import lax
from jax.experimental import pallas as pl
from jax.experimental.pallas import tpu as pltpu
from jax.sharding import PartitionSpec as P


BS = 256
NNB = 3
REACH = 2

ewald_scale = 40.0
ewald_damp = 0.02

BF = jnp.bfloat16
F32 = jnp.float32

SIN = (6.283185302511499, -41.34170040531678, 81.60513138577247, -76.70301535353673,
       42.02592698394968, -14.899846662448152, 3.2381375038938693)
COS = (0.9999999890590217, -19.73920449945376, 64.93911745989128, -85.45013953083522,
       60.167630950695504, -25.967599247822193, 6.5286581606558824)


def params(mib):
    return pltpu.CompilerParams(vmem_limit_bytes=mib << 20, dimension_semantics=("arbitrary",))


def dot(a, b, dims):
    return lax.dot_general(a, b, (dims, ((), ())), preferred_element_type=F32)


def horner(coeffs, u):
    total = coeffs[-1]
    for c in coeffs[-2::-1]:
        total = total * u + c
    return total


def halves(x):
    high = x.astype(BF)
    return high, (x - high.astype(F32)).astype(BF)


def load_kernel(chans, rows, width, place, *refs):
    (k, v, others), (near, far, near_big, far_big, v0, *copies) = (refs[0], refs[1], refs[2:7]), refs[7:-1]
    sems = refs[-1]
    atoms = v.shape[2]
    even = place[0] % 2 == 0
    last = atoms - width
    near_cols = pl.ds(pl.multiple_of(jnp.where(even, last, 0), 128), width)
    far_cols = pl.ds(pl.multiple_of(jnp.where(even, 0, last), 128), width)
    moves = []
    for piece, cols in ((far, far_cols), (near, near_cols)):
        moves.append((k.at[:, cols], piece.at[pl.ds(0, rows)]))
        moves.append((v.at[0, :, cols], piece.at[pl.ds(rows, chans)]))
    moves.append((k, copies[0]))
    moves.append((v.at[0], v0))
    moves += list(zip(others, copies[1:]))
    for piece, cols in ((far_big, far_cols), (near_big, near_cols)):
        moves.append((v.at[pl.ds(1, piece.shape[0]), :, cols], piece))
    started = [pltpu.make_async_copy(src, dst, sems.at[i]) for i, (src, dst) in enumerate(moves)]
    for copy in started:
        copy.start()
    for copy in started:
        copy.wait()


def load_call(place, k, v, others, width):
    comps, chans, atoms = v.shape
    rows = k.shape[0]
    shape = jax.ShapeDtypeStruct
    outs = [shape((rows + chans, width), BF)] * 2 + [shape((comps - 1, chans, width), BF)] * 2
    outs += [shape((chans, atoms), BF)] + [shape(x.shape, x.dtype) for x in (k, *others)]
    return pl.pallas_call(
        functools.partial(load_kernel, chans, rows, width),
        grid_spec=pltpu.PrefetchScalarGridSpec(
            num_scalar_prefetch=1,
            grid=(1,),
            in_specs=[pl.BlockSpec(memory_space=pltpu.HBM)] * (2 + len(others)),
            out_specs=[pl.BlockSpec(memory_space=pl.ANY)] * len(outs),
            scratch_shapes=[pltpu.SemaphoreType.DMA((8 + len(others),))],
        ),
        out_shape=outs,
        compiler_params=params(2),
        cost_estimate=pl.CostEstimate(flops=0, transcendentals=0, bytes_accessed=4 * comps * chans * width),
        name="load",
    )(place, *[pltpu.with_memory_space_constraint(x, pltpu.HBM) for x in (k, v, *others)])


def on_left(place, far):
    even = place[0] % 2 == 0
    return even if far else jnp.logical_not(even)


def edge_block(step, place, blocks):
    left = (step < REACH) == (place[0] % 2 == 0)
    return step % REACH + jnp.where(left, 0, blocks - REACH)


def score_kernel(heads, head_dim, head_chan, blocks, part, lists, counts, place, *refs):
    q_ref, k_ref, v_ref, cw_ref = refs[:4]
    sides, (p_ref, scale_ref, charge_ref, kaug, v0) = refs[4:-5], refs[-5:]
    i = pl.program_id(0)
    first = place[0] * blocks
    total = counts.shape[0]

    @pl.when(i == 0)
    def _():
        lane = lax.broadcasted_iota(jnp.int32, (16, BS), 1)
        row = lax.broadcasted_iota(jnp.int32, (16, BS), 0)

        def fill(b, keys, values):
            index = first + b - REACH
            inside = (index >= 0) & (index < total)
            live = jnp.where(inside, counts[jnp.clip(index, 0, total - 1)], 0)
            bias = jnp.where((row == 0) & (lane >= live), -1e30, 0.0).astype(BF)
            v0[b] = values
            for h in range(heads):
                kaug[b, h, 0:head_dim, :] = keys[h * head_dim : (h + 1) * head_dim]
                kaug[b, h, head_dim : head_dim + 16, :] = bias

        for b in range(blocks):
            cols = slice(b * BS, (b + 1) * BS)
            fill(b + REACH, k_ref[:, cols], v_ref[:, cols])
        for far, side in zip((True, False), sides[:2]):
            base = jnp.where(on_left(place, far), 0, blocks + REACH)
            for b in range(REACH):
                cols = slice(b * BS, (b + 1) * BS)
                fill(base + b, side[0 : heads * head_dim, cols], side[heads * head_dim :, cols])

    g = i + REACH if part == "interior" else edge_block(i, place, blocks)
    own_count = counts[first + g]
    live_q = lax.broadcasted_iota(jnp.int32, (1, BS), 1) < own_count
    ones = jnp.where(lax.broadcasted_iota(jnp.int32, (16, BS), 0) == 0, 1.0, 0.0).astype(BF)
    listed = [lists[e, g] - (first - REACH) for e in range(NNB)]
    charge = None
    for h in range(heads):
        q = (q_ref[h * head_dim : (h + 1) * head_dim, :].astype(F32) * head_dim ** (-0.5)).astype(BF)
        qa = jnp.concatenate([q, ones], axis=0)
        scores = [dot(kaug[b, h], qa, ((0,), (0,))) for b in listed]
        top = functools.reduce(jnp.maximum, [jnp.max(s, axis=0, keepdims=True) for s in scores])
        denominator = 0.0
        mixed = 0.0
        for e, b in enumerate(listed):
            w = jnp.exp(scores[e] - top)
            denominator = denominator + jnp.sum(w, axis=0, keepdims=True)
            w16 = w.astype(BF)
            p_ref[0, h, e * BS : (e + 1) * BS, :] = w16
            mixed = mixed + dot(v0[b, h * head_chan : (h + 1) * head_chan, :], w16, ((1,), (0,)))
        scale = jnp.where(live_q, 1.0 / denominator, 0.0)
        scale_ref[0, h : h + 1, :] = scale
        att0 = (mixed * scale).astype(BF)
        term = dot(cw_ref[:, h * head_chan : (h + 1) * head_chan], att0, ((1,), (0,)))
        charge = term if charge is None else charge + term
    charge_ref[...] = charge


def scores_call(part, lists, counts, place, q, k, v0, cw, sides, heads, head_dim):
    chans, atoms = v0.shape
    blocks = atoms // BS
    nq = cw.shape[0]
    head_chan = chans // heads
    band = blocks + 2 * REACH
    steps = blocks - 2 * REACH if part == "interior" else 2 * REACH

    def at(i, lists, counts, place):
        return i + REACH if part == "interior" else edge_block(i, place, blocks)

    whole = lambda shape: pl.BlockSpec(shape, lambda g, *_: (0,) * len(shape), pipeline_mode=pl.Buffered(1))
    any_space = pl.BlockSpec(memory_space=pl.ANY)
    return pl.pallas_call(
        functools.partial(score_kernel, heads, head_dim, head_chan, blocks, part),
        grid_spec=pltpu.PrefetchScalarGridSpec(
            num_scalar_prefetch=3,
            grid=(steps,),
            in_specs=[
                pl.BlockSpec((heads * head_dim, BS), lambda i, *s: (0, at(i, *s))),
                whole(k.shape),
                whole(v0.shape),
                whole(cw.shape),
            ]
            + [whole(s.shape) for s in sides[:2]] + [any_space] * len(sides[2:]),
            out_specs=[
                pl.BlockSpec((1, heads, NNB * BS, BS), lambda i, *_: (i, 0, 0, 0)),
                pl.BlockSpec((1, heads, BS), lambda i, *_: (i, 0, 0)),
                pl.BlockSpec((nq, BS), lambda i, *s: (0, at(i, *s))),
            ],
            scratch_shapes=[
                pltpu.VMEM((band, heads, head_dim + 16, BS), BF),
                pltpu.VMEM((band, chans, BS), BF),
            ],
        ),
        out_shape=[
            jax.ShapeDtypeStruct((steps, heads, NNB * BS, BS), BF),
            jax.ShapeDtypeStruct((steps, heads, BS), F32),
            jax.ShapeDtypeStruct((nq, atoms), F32),
        ],
        input_output_aliases={9: 2} if sides else {},
        compiler_params=params(10),
        cost_estimate=pl.CostEstimate(
            flops=steps * heads * NNB * BS * BS * 200, transcendentals=steps * heads * NNB * BS * BS,
            bytes_accessed=steps * heads * NNB * BS * BS * 2,
        ),
    )(lists, counts, place, q, k, v0, cw, *sides)


def mix_kernel(heads, head_dim, head_chan, blocks, part, lists, place, v_ref, p_ref, scale_ref, *refs):
    halo, out_ref = refs[: 2 if part in ("far", "near") else 0], refs[-2 if part in ("far", "near") else -1]
    comps = v_ref.shape[0]
    i = pl.program_id(0)
    offset = place[0] * blocks
    if halo:
        small, big = halo
        band = refs[-1]
        span = 3 * REACH
        left = on_left(place, part == "far")
        begin = jnp.where(left, 0, blocks + 2 * REACH - span)

        @pl.when(i == 0)
        def _():
            own = jnp.where(left, REACH, 0)
            first = jnp.where(left, 0, blocks - 2 * REACH)
            for b in range(2 * REACH):
                band[own + b] = v_ref[:, :, pl.ds(pl.multiple_of((first + b) * BS, BS), BS)]
            other = jnp.where(left, 0, 2 * REACH)
            for b in range(REACH):
                cols = slice(b * BS, (b + 1) * BS)
                band[other + b, 0] = small[heads * head_dim :, cols]
                band[other + b, 1:] = big[:, :, cols]

        g = edge_block(i if part == "far" else i + REACH, place, blocks)
        listed = [lists[e, g] - offset + REACH - begin for e in range(NNB)]
        pick = lambda b, rows: band[b, :, rows, :]
    else:
        g = i + (REACH if part == "low" else blocks // 2)
        listed = [lists[e, g] - offset for e in range(NNB)]
        pick = lambda b, rows: v_ref[:, rows, pl.ds(pl.multiple_of(b * BS, BS), BS)]
    for h in range(heads):
        rows = slice(h * head_chan, (h + 1) * head_chan)
        acc = 0.0
        for e in range(NNB):
            v = pick(listed[e], rows).reshape(comps * head_chan, BS)
            acc = acc + dot(v, p_ref[0, h, e * BS : (e + 1) * BS, :], ((1,), (0,)))
        acc = acc * scale_ref[0, h : h + 1, :]
        out_ref[:, rows, :] = acc.astype(BF).reshape(comps, head_chan, BS)


def mix_call(part, lists, place, v, p, scale, halo, prev, heads, head_dim):
    comps, chans, atoms = v.shape
    blocks = atoms // BS
    half = blocks // 2 - REACH
    steps = REACH if halo else half
    skip = {"low": 0, "high": half, "far": 0, "near": REACH}[part]

    def at(i, lists, place):
        if part in ("low", "high"):
            return i + REACH + skip
        return edge_block(i + skip, place, blocks)

    whole = lambda shape: pl.BlockSpec(shape, lambda g, *_: (0,) * len(shape), pipeline_mode=pl.Buffered(1))
    extra = list(halo) + ([] if prev is None else [prev])
    return pl.pallas_call(
        functools.partial(mix_kernel, heads, head_dim, chans // heads, blocks, part),
        grid_spec=pltpu.PrefetchScalarGridSpec(
            num_scalar_prefetch=2,
            grid=(steps,),
            in_specs=[
                whole(v.shape),
                pl.BlockSpec((1, heads, NNB * BS, BS), lambda i, *_: (i + skip, 0, 0, 0)),
                pl.BlockSpec((1, heads, BS), lambda i, *_: (i + skip, 0, 0)),
            ]
            + [whole(x.shape) for x in halo]
            + ([] if prev is None else [pl.BlockSpec(memory_space=pl.ANY)]),
            out_specs=pl.BlockSpec((comps, chans, BS), lambda i, *s: (0, 0, at(i, *s))),
            scratch_shapes=[pltpu.VMEM((3 * REACH, comps, chans, BS), BF)] if halo else [],
        ),
        out_shape=jax.ShapeDtypeStruct(v.shape, BF),
        input_output_aliases={} if prev is None else {4 + len(extra): 0},
        compiler_params=params(16),
        cost_estimate=pl.CostEstimate(
            flops=steps * chans * comps * NNB * BS * BS * 2, transcendentals=0,
            bytes_accessed=steps * chans * comps * BS * 8,
        ),
    )(lists, place, v, p, scale, *extra)


def table_kernel(place, n_ref, f_ref, out_ref, parts):
    @pl.when(pl.program_id(0) == 0)
    def _():
        f = f_ref[...]
        high, low = halves(f)
        rest = ((f - high.astype(F32)) - low.astype(F32)).astype(BF)
        parts[...] = jnp.concatenate([high, low, rest], axis=0)

    n = n_ref[...].astype(F32).astype(BF)
    turns = dot(jnp.concatenate([n, n, n], axis=0), parts[...], ((0,), (0,)))
    r = turns - jnp.round(turns)
    u = r * r
    out_ref[0] = horner(COS, u).astype(BF)
    out_ref[1] = (horner(SIN, u) * r).astype(BF)


def table_call(place, n, f, waves):
    step = 128
    atoms = f.shape[1]
    return pl.pallas_call(
        table_kernel,
        grid_spec=pltpu.PrefetchScalarGridSpec(
            num_scalar_prefetch=1,
            grid=(waves // step,),
            in_specs=[
                pl.BlockSpec((3, step), lambda i, place: (0, place[1] * (waves // step) + i)),
                pl.BlockSpec(f.shape, lambda i, place: (0, 0)),
            ],
            out_specs=pl.BlockSpec((2, step, atoms), lambda i, place: (0, i, 0)),
            scratch_shapes=[pltpu.VMEM((9, atoms), BF)],
        ),
        out_shape=jax.ShapeDtypeStruct((2, waves, atoms), BF),
        compiler_params=params(16),
        cost_estimate=pl.CostEstimate(
            flops=waves * atoms * 400, transcendentals=0, bytes_accessed=waves * atoms * 4
        ),
        name="table",
    )(place, n, f)


def structure_kernel(inv_root, c_ref, t_ref, out_ref):
    high, low = halves(c_ref[...])
    both = jnp.concatenate([high, low], axis=0)
    s = dot(t_ref[...], both, ((1,), (1,)))
    nq = c_ref.shape[0]
    out_ref[...] = (s[:, :nq] + s[:, nq:]).T * inv_root


def structure_call(c, table, inv_root):
    rows, atoms = table.shape
    step = min(256, rows)
    nq = c.shape[0]
    return pl.pallas_call(
        functools.partial(structure_kernel, inv_root),
        grid=(rows // step,),
        in_specs=[pl.BlockSpec((nq, atoms), lambda i: (0, 0)), pl.BlockSpec((step, atoms), lambda i: (i, 0))],
        out_specs=pl.BlockSpec((nq, step), lambda i: (0, i)),
        out_shape=jax.ShapeDtypeStruct((nq, rows), F32),
        compiler_params=params(12),
        cost_estimate=pl.CostEstimate(flops=rows * atoms * 512, transcendentals=0, bytes_accessed=rows * atoms * 2),
        name="structure",
    )(c, table)


def field_kernel(place, s_ref, n_ref, c_ref, t_ref, out_ref, coeff):
    nq = c_ref.shape[0]
    waves = n_ref.shape[1]

    @pl.when(pl.program_id(0) == 0)
    def _():
        n = n_ref[...].astype(F32)
        norm = n[0:1] * n[0:1] + n[1:2] * n[1:2] + n[2:3] * n[2:3]
        weight = ewald_scale * jnp.exp(-ewald_damp * norm) / norm
        real = s_ref[:, :waves] * weight
        imag = s_ref[:, waves:] * weight
        with_cos = jnp.concatenate([real] + [-imag * n[d : d + 1] for d in range(3)], axis=0)
        with_sin = jnp.concatenate([imag] + [real * n[d : d + 1] for d in range(3)], axis=0)
        for part, x in enumerate((with_cos, with_sin)):
            high, low = halves(x)
            cols = slice(part * waves, (part + 1) * waves)
            coeff[0 : 4 * nq, cols] = high
            coeff[4 * nq :, cols] = low

    both = dot(coeff[...], t_ref[...], ((1,), (0,)))
    sums = both[: 4 * nq] + both[4 * nq :]
    c = c_ref[...]
    out_ref[0:nq, :] = sums[:nq]
    forces = [
        jnp.sum(c * sums[(d + 1) * nq : (d + 2) * nq], axis=0, keepdims=True) for d in range(3)
    ]
    out_ref[nq : nq + 8, :] = jnp.concatenate(forces + [jnp.zeros((5, c.shape[1]), F32)], axis=0)


def field_call(place, s, n, c, table, waves):
    rows, atoms = table.shape
    step = 512
    nq = c.shape[0]
    return pl.pallas_call(
        field_kernel,
        grid_spec=pltpu.PrefetchScalarGridSpec(
            num_scalar_prefetch=1,
            grid=(atoms // step,),
            in_specs=[
                pl.BlockSpec((nq, rows), lambda i, place: (0, 0)),
                pl.BlockSpec((3, waves), lambda i, place: (0, place[1])),
                pl.BlockSpec((nq, step), lambda i, place: (0, i)),
                pl.BlockSpec((rows, step), lambda i, place: (0, i)),
            ],
            out_specs=pl.BlockSpec((nq + 8, step), lambda i, place: (0, i)),
            scratch_shapes=[pltpu.VMEM((8 * nq, rows), BF)],
        ),
        out_shape=jax.ShapeDtypeStruct((nq + 8, atoms), F32),
        compiler_params=params(12),
        cost_estimate=pl.CostEstimate(flops=rows * atoms * 512, transcendentals=0, bytes_accessed=rows * atoms * 2),
        name="fields",
    )(place, s, n, c, table)


def exchanged(x, axis, step):
    size = lax.axis_size(axis)
    if step >= size:
        return x
    return x + lax.ppermute(x, axis, [(i, i ^ step) for i in range(size)])


def summed(x, axis, step=1):
    size = lax.axis_size(axis)
    assert size & (size - 1) == 0
    while step < size:
        x = exchanged(x, axis, step)
        step *= 2
    return x


def whole_step(
    queries,
    key_states,
    value_states,
    fractional,
    block_counts,
    neighbors,
    integer_wave_vectors,
    charge_weight,
):
    heads, head_dim, atoms = queries.shape
    nq = charge_weight.shape[1]
    waves = integer_wave_vectors.shape[1] // lax.axis_size("inner")
    inv_root = 1.0 / math.sqrt(atoms * lax.axis_size("seq"))
    place = jnp.stack([lax.axis_index("seq"), lax.axis_index("inner")]).astype(jnp.int32)
    width = REACH * BS
    count = lax.axis_size("seq")
    near_pairs = [(i, i ^ 1) for i in range(count)]
    far_pairs = [(i, i + 1 if i % 2 else i - 1) for i in range(1, count - 1)]

    def swap(x, pairs):
        return lax.ppermute(x, "seq", pairs)

    values = value_states.transpose(1, 0, 2)
    near, far, near_big, far_big, v0, keys, asked, weight, counts, lists, vectors = load_call(
        place, key_states.reshape(heads * head_dim, atoms), values,
        (queries.reshape(heads * head_dim, atoms), charge_weight.T, block_counts, neighbors.T, integer_wave_vectors),
        width,
    )
    far = swap(far, far_pairs)
    near = swap(near, near_pairs)
    far_big = swap(far_big, far_pairs)
    near_big = swap(near_big, near_pairs)

    p_in, scale_in, part = scores_call(
        "interior", lists, counts, place, asked, keys, v0, weight, (), heads, head_dim
    )
    p_out, scale_out, part = scores_call(
        "edges", lists, counts, place, asked, keys, v0, weight, (far, near, part), heads, head_dim
    )
    table = table_call(place, vectors, fractional, waves).reshape(2 * waves, atoms)
    charges = summed(part, "inner")
    structure = structure_call(charges, table, inv_root)
    structure = exchanged(summed(structure, "seq", 2), "seq", 1)
    fields = field_call(place, structure, vectors, charges, table, waves)
    fields = summed(fields, "inner")

    mix = functools.partial(mix_call, heads=heads, head_dim=head_dim)
    attention = mix("low", lists, place, values, p_in, scale_in, (), None)
    attention = mix("high", lists, place, values, p_in, scale_in, (), attention)
    attention = mix("far", lists, place, values, p_out, scale_out, (far, far_big), attention)
    attention = mix("near", lists, place, values, p_out, scale_out, (near, near_big), attention)
    return (attention.transpose(1, 0, 2), fields[:nq], fields[nq : nq + 3])


def solution(mesh):
    placed = (
        P("inner", None, "seq"),
        P("inner", None, "seq"),
        P("inner", None, "seq"),
        P(None, "seq"),
        P(),
        P("seq", None),
        P(),
        P("inner", None),
    )
    return jax.shard_map(
        whole_step,
        mesh=mesh,
        in_specs=placed,
        out_specs=(P("inner", None, "seq"), P(None, "seq"), P(None, "seq")),
        check_vma=False,
    )
```

time: 89.9 us -> 78.3 us (0.87)
  starting transfers between devices: 29.1 us -> 19.6 us
  local copies, waits for them, and re-layouts: 8.79 us -> 1.3 us
  Pallas kernels: 28.5 us -> 33.2 us
    ppermute x7, waiting for transfers between devices: 5.84 us -> 22.3 us  [exchanged(): return x + lax.ppermute(x, axis, [(i, i ^ step) for i in range(size)])]
    ppermute x6 -> x4, waiting for transfers between devices: 16 us -> 0.02 us  [swap(): return lax.ppermute(x, 'seq', pairs)]
    ppermute x6 -> x4, starting transfers between devices: 17.9 us -> 11.5 us  [swap(): return lax.ppermute(x, 'seq', pairs)]
    unnamed x20 -> x4, local copies, waits for them, and re-layouts: 5.78 us -> 0.01 us
    pallas_call x2 -> x5, Pallas kernels: 7.74 us -> 12.4 us  [the longest x4 10 us: mix_call(): pl.pallas_call(functools.partial(mix_kernel, heads, head_dim, chans // he...]
    ppermute x7, starting transfers between devices: 11.1 us -> 8.16 us  [exchanged(): return x + lax.ppermute(x, axis, [(i, i ^ step) for i in range(size)])]
    slice x4 -> x0, local copies, waits for them, and re-layouts: 0.94 us -> none  [the longest x1 0.78 us: whole_step(): keys[:, cols]]
  transfers between devices with their start and end apart: 13 -> 11, of which waited for: 5 -> 5; matrix products, arithmetic and copies ran while one was open for 0% -> 0% of each run, Pallas kernels for 24% -> 33%
where the time goes in v2:
time: 78.3 us; the launch traced here: 77.4 us
  Pallas kernels  33.2 us (42%)
  waiting for transfers between devices  22.3 us (28%)
  starting transfers between devices  19.6 us (25%)
  local copies, waits for them, and re-layouts  1.3 us (2%)
    ppermute x7, waiting for transfers between devices, exchanged(): return x + lax.ppermute(x, axis, [(i, i ^ step) for i in range(size)])  22.3 us
    ppermute x4, starting transfers between devices, swap(): return lax.ppermute(x, 'seq', pairs)  11.5 us
    pallas_call x2, Pallas kernels, scores_call(): pl.pallas_call(functools.partial(score_kernel, heads, head_dim, head_chan...  10.8 us
    pallas_call x4, Pallas kernels, mix_call(): pl.pallas_call(functools.partial(mix_kernel, heads, head_dim, chans // he...  10 us
    ppermute x7, starting transfers between devices, exchanged(): return x + lax.ppermute(x, axis, [(i, i ^ step) for i in range(size)])  8.16 us
    pallas_call x1, Pallas kernels, table_call(): pl.pallas_call(table_kernel, grid_spec=pltpu.PrefetchScalarGridSpec(num_s...  5.62 us
    pallas_call x1, Pallas kernels, load_call(): pl.pallas_call(functools.partial(load_kernel, chans, rows, width), grid_s...  2.34 us
    pallas_call x1, Pallas kernels, field_call(): pl.pallas_call(field_kernel, grid_spec=pltpu.PrefetchScalarGridSpec(num_s...  2.34 us
  transfers between devices with their start and end apart: 11, of which 5 were waited for; matrix products, arithmetic and copies ran while one was open for 0% of the time, Pallas kernels for 33%

profile of v2, /device:TPU:0, one launch (start us, length us, event | category | flops | bytes accessed | tf_op | source)
XLA Modules:
  0.0 77.4 jit_solution(6400744615393594754)
XLA Ops:
  0.6 0.1 pad_add_fusion.place
  0.7 2.3 %load.1 = (bf16[64,512]{1,0:T(8,128)(2,1)S(1)}, bf16[64,512]{1,0:T(8,128)(2,1)S(1)}, bf16[24,32,512]{2,1,0:T(8,128)(2,1)S(1)}, bf16[24,32,512]{2,1,0:T(8,128)(2,...) custom-call(s32[2]{0:T(128)S(1)} %pad_add_fusion.place, ...), custom_call_target="tpu_custom_call" | custom-call | bytes 1638400 | tf_op jit(solution)/shard_map/load/pallas_call | solution.py:78
  3.1 0.0 copy-start.1
  3.1 0.7 collective-permute-start
  3.7 5.8 %collective-permute-start.1 = (bf16[64,512]{1,0:T(8,128)(2,1)S(1)}, bf16[64,512]{1,0:T(8,128)(2,1)S(1)}, u32[]{:S(2)}, u32[]{:S(2)}) collective-permute-start(bf16[64,512]{1,0:T(8,128)(2,1)S(1)} %get-tuple-element.27), channel_id=1, source_target_pairs={{0,4},{4,0},{8,12},{12,8},{16,20},{20,16},{24,28},{28,24},{1,5},{5... | collective-permute-start | bytes 196616 | tf_op jit(solution)/shard_map/ppermute | solution.py:446
  9.6 5.3 %shard_map.103 = (bf16[4,2,768,256]{3,2,1,0:T(8,128)(2,1)S(1)}, f32[4,2,256]{2,1,0:T(2,128)S(1)}, f32[16,2048]{1,0:T(8,128)S(1)}) custom-call(s32[3,8]{1,0:T(4,128)S(1)} %get-tuple-element.20.lists, s32[64]{0:T(128)S(1)} %get-tuple-element.21.counts, s32[2]{0:T(128)S(1)} %pad_add_fusion.place, bf16[32,2048]{1,0:T(8,128)(2,1)S(1)} %get-tuple-element.22.refs_0_, ...), custom_call_target="tpu_custom_call" | custom-call | flops 314572800 | bytes 3145728 | tf_op jit(solution)/shard_map/pallas_call | solution.py:175
  14.9 0.0 collective-permute-done.1.refs_5_.refs_0_
  14.9 5.4 %shard_map.104 = (bf16[4,2,768,256]{3,2,1,0:T(8,128)(2,1)S(1)}, f32[4,2,256]{2,1,0:T(2,128)S(1)}, f32[16,2048]{1,0:T(8,128)S(1)}) custom-call(s32[3,8]{1,0:T(4,128)S(1)} %get-tuple-element.20.lists, s32[64]{0:T(128)S(1)} %get-tuple-element.21.counts, s32[2]{0:T(128)S(1)} %pad_add_fusion.place, ...), custom_call_target="tpu_custom_call", output_to_operand_aliasing={{2}: (9, {})} | custom-call | flops 314572800 | bytes 3145728 | tf_op jit(solution)/shard_map/pallas_call | solution.py:175
  20.4 0.0 collective-permute-start.4
  20.4 1.3 %collective-permute-done.4 = f32[16,2048]{1,0:T(8,128)S(1)} collective-permute-done((f32[16,2048]{1,0:T(8,128)S(1)}, f32[16,2048]{1,0:T(8,128)S(1)}, u32[]{:S(2)}, u32[]{:S(2)}) %collective-permute-start.4) | collective-permute-done | bytes 131104 | tf_op jit(solution)/shard_map/ppermute | solution.py:413
  21.8 1.6 %collective-permute-start.5 = (f32[16,2048]{1,0:T(8,128)S(1)}, f32[16,2048]{1,0:T(8,128)S(1)}, u32[]{:S(2)}, u32[]{:S(2)}) collective-permute-start(f32[16,2048]{1,0:T(8,128)S(1)} %add.21), channel_id=1, source_target_pairs={{0,2},{1,3},{2,0},{3,1},{4,6},{5,7},{6,4},{7,5},{8,10},{9,11},{10,... | collective-permute-start | bytes 393224 | tf_op jit(solution)/shard_map/ppermute | solution.py:413
  23.3 0.7 collective-permute-start.3
  24.0 4.3 %collective-permute-start.2 = (bf16[24,32,512]{2,1,0:T(8,128)(2,1)S(1)}, bf16[24,32,512]{2,1,0:T(8,128)(2,1)S(1)}, u32[]{:S(2)}, u32[]{:S(2)}) collective-permute-start(bf16[24,32,512]{2,1,0:T(8,128)(2,1)S(1)} %get-tuple-element.31), channel_id=1, source_target_pairs={{0,4},{4,0},{8,12},{12,8},{16,20},{20,16},{24,28},{28,24},{1,5},{5... | collective-permute-start | bytes 2359304 | tf_op jit(solution)/shard_map/ppermute | solution.py:446
  28.3 5.6 %table.1 = bf16[2,512,2048]{2,1,0:T(8,128)(2,1)S(1)} custom-call(s32[2]{0:T(128)S(1)} %pad_add_fusion.place, s32[3,2048]{1,0:T(4,128)S(1)} %get-tuple-element.36.n_ref, f32[3,2048]{1,0:T(4,128)S(1)} %copy-done.1), custom_call_target="tpu_custom_call" | custom-call | flops 419430400 | bytes 4194304 | tf_op jit(solution)/shard_map/table/pallas_call | solution.py:310
  34.0 2.1 %structure.1 = f32[16,1024]{1,0:T(8,128)S(1)} custom-call(f32[16,2048]{1,0:T(8,128)S(1)} %add.22.c_ref, bf16[1024,2048]{1,0:T(8,128)(2,1)S(1)} %bitcast.14), custom_call_target="tpu_custom_call" | custom-call | flops 1073741824 | bytes 4194304 | tf_op jit(solution)/shard_map/structure/pallas_call | solution.py:343
  36.1 0.0 copy-start
  36.1 1.6 %collective-permute-start.6 = (f32[16,1024]{1,0:T(8,128)S(1)}, f32[16,1024]{1,0:T(8,128)S(1)}, u32[]{:S(2)}, u32[]{:S(2)}) collective-permute-start(f32[16,1024]{1,0:T(8,128)S(1)} %structure.1), channel_id=1, source_target_pairs={{0,8},{4,12},{8,0},{12,4},{16,24},{20,28},{24,16},{28,20},{1,9},{5... | collective-permute-start | bytes 196616 | tf_op jit(solution)/shard_map/ppermute | solution.py:413
  37.8 8.0 %collective-permute-done.6 = f32[16,1024]{1,0:T(8,128)S(1)} collective-permute-done((f32[16,1024]{1,0:T(8,128)S(1)}, f32[16,1024]{1,0:T(8,128)S(1)}, u32[]{:S(2)}, u32[]{:S(2)}) %collective-permute-start.6) | collective-permute-done | bytes 65568 | tf_op jit(solution)/shard_map/ppermute | solution.py:413
  45.8 2.8 %collective-permute-start.7 = (f32[16,1024]{1,0:T(8,128)S(1)}, f32[16,1024]{1,0:T(8,128)S(1)}, u32[]{:S(2)}, u32[]{:S(2)}) collective-permute-start(f32[16,1024]{1,0:T(8,128)S(1)} %add.23), channel_id=1, source_target_pairs={{0,16},{4,20},{8,24},{12,28},{16,0},{20,4},{24,8},{28,12},{1,17},{... | collective-permute-start | bytes 196616 | tf_op jit(solution)/shard_map/ppermute | solution.py:413
  48.6 2.4 %collective-permute-done.7 = f32[16,1024]{1,0:T(8,128)S(1)} collective-permute-done((f32[16,1024]{1,0:T(8,128)S(1)}, f32[16,1024]{1,0:T(8,128)S(1)}, u32[]{:S(2)}, u32[]{:S(2)}) %collective-permute-start.7) | collective-permute-done | bytes 65568 | tf_op jit(solution)/shard_map/ppermute | solution.py:413
  51.0 1.4 %collective-permute-start.8 = (f32[16,1024]{1,0:T(8,128)S(1)}, f32[16,1024]{1,0:T(8,128)S(1)}, u32[]{:S(2)}, u32[]{:S(2)}) collective-permute-start(f32[16,1024]{1,0:T(8,128)S(1)} %add.24), channel_id=1, source_target_pairs={{0,4},{4,0},{8,12},{12,8},{16,20},{20,16},{24,28},{28,24},{1,5},{5... | collective-permute-start | bytes 196616 | tf_op jit(solution)/shard_map/ppermute | solution.py:413
  52.5 9.1 %collective-permute-done.8 = f32[16,1024]{1,0:T(8,128)S(1)} collective-permute-done((f32[16,1024]{1,0:T(8,128)S(1)}, f32[16,1024]{1,0:T(8,128)S(1)}, u32[]{:S(2)}, u32[]{:S(2)}) %collective-permute-start.8) | collective-permute-done | bytes 65568 | tf_op jit(solution)/shard_map/ppermute | solution.py:413
  61.6 2.3 %fields.1 = f32[24,2048]{1,0:T(8,128)S(1)} custom-call(s32[2]{0:T(128)S(1)} %pad_add_fusion.place, f32[16,1024]{1,0:T(8,128)S(1)} %add.25.s_ref, s32[3,2048]{1,0:T(4,128)S(1)} %get-tuple-element.36.n_ref, f32[16,2048]{1,0:T(8,128)S(1)} %add.22.c_ref, bf16[1024,2048]{1,0:T(8,128)(2,1)S(1)} %bitcast.15), custom_call_target="tpu_custom_call" | custom-call | flops 1073741824 | bytes 4194304 | tf_op jit(solution)/shard_map/fields/pallas_call | solution.py:388
  63.9 0.1 collective-permute-start.9
  64.0 1.4 %collective-permute-done.9 = f32[24,2048]{1,0:T(8,128)S(1)} collective-permute-done((f32[24,2048]{1,0:T(8,128)S(1)}, f32[24,2048]{1,0:T(8,128)S(1)}, u32[]{:S(2)}, u32[]{:S(2)}) %collective-permute-start.9) | collective-permute-done | bytes 196640 | tf_op jit(solution)/shard_map/ppermute | solution.py:413
  65.5 0.6 collective-permute-start.10
  66.1 2.3 %shard_map.105.refs_0_ = bf16[25,32,2048]{2,1,0:T(8,128)(2,1)} custom-call(s32[3,8]{1,0:T(4,128)S(1)} %get-tuple-element.20.lists, s32[2]{0:T(128)S(1)} %pad_add_fusion.place, bf16[25,32,2048]{2,1,0:T(8,128)(2,1)S(1)} %bitcast.10, bf16[4,2,768,256]{3,2,1,0:T(8,128)(2,1)S(1)} %get-tuple-element.33.p_ref, f32[4,2,256]{2,1,0:T(2,128)S(1)} %get-tuple-element.34.scale_ref), custom_call_target="tpu_custom_call" | custom-call | flops 629145600 | bytes 3276800 | tf_op jit(solution)/shard_map/pallas_call | solution.py:266
  68.4 2.3 %shard_map.106.refs_2_ = bf16[25,32,2048]{2,1,0:T(8,128)(2,1)} custom-call(s32[3,8]{1,0:T(4,128)S(1)} %get-tuple-element.20.lists, s32[2]{0:T(128)S(1)} %pad_add_fusion.place, bf16[25,32,2048]{2,1,0:T(8,128)(2,1)S(1)} %bitcast.11, bf16[4,2,768,256]{3,2,1,0:T(8,128)(2,1)S(1)} %get-tuple-element.33.p_ref, ...), custom_call_target="tpu_custom_call", output_to_operand_aliasing={{}: (5, {})} | custom-call | flops 629145600 | bytes 3276800 | tf_op jit(solution)/shard_map/pallas_call | solution.py:266
  70.8 2.7 %shard_map.107.refs_2_ = bf16[25,32,2048]{2,1,0:T(8,128)(2,1)} custom-call(s32[3,8]{1,0:T(4,128)S(1)} %get-tuple-element.20.lists, s32[2]{0:T(128)S(1)} %pad_add_fusion.place, bf16[25,32,2048]{2,1,0:T(8,128)(2,1)S(1)} %bitcast.12, bf16[4,2,768,256]{3,2,1,0:T(8,128)(2,1)S(1)} %get-tuple-element.29.p_ref, ...), custom_call_target="tpu_custom_call", output_to_operand_aliasing={{}: (7, {})} | custom-call | flops 629145600 | bytes 3276800 | tf_op jit(solution)/shard_map/pallas_call | solution.py:266
  73.4 2.7 %shard_map.108 = bf16[25,32,2048]{2,1,0:T(8,128)(2,1)} custom-call(s32[3,8]{1,0:T(4,128)S(1)} %get-tuple-element.20.lists, s32[2]{0:T(128)S(1)} %pad_add_fusion.place, bf16[25,32,2048]{2,1,0:T(8,128)(2,1)S(1)} %bitcast.13, bf16[4,2,768,256]{3,2,1,0:T(8,128)(2,1)S(1)} %get-tuple-element.29.p_ref, ...), custom_call_target="tpu_custom_call", output_to_operand_aliasing={{}: (7, {})} | custom-call | flops 629145600 | bytes 3276800 | tf_op jit(solution)/shard_map/pallas_call | solution.py:266
  76.2 0.6 slice.9
  76.8 0.7 slice.8
  (14 shorter events, 0.1 us)
Async XLA Ops:
  3.1 25.3 %copy-start.1 = (f32[3,2048]{1,0:T(4,128)S(1)}, f32[3,2048]{1,0:T(4,128)}, u32[]{:S(2)}) copy-start(f32[3,2048]{1,0:T(4,128)} %f_ref.1) | copy-start | bytes 73732
  3.1 11.8 %collective-permute-start = (bf16[64,512]{1,0:T(8,128)(2,1)S(1)}, bf16[64,512]{1,0:T(8,128)(2,1)S(1)}, u32[]{:S(2)}, u32[]{:S(2)}) collective-permute-start(bf16[64,512]{1,0:T(8,128)(2,1)S(1)} %get-tuple-element.26), channel_id=1, source_target_pairs={{4,8},{8,4},{12,16},{16,12},{20,24},{24,20},{5,9},{9,5},{13,17},{1... | collective-permute-start | bytes 196616 | tf_op jit(solution)/shard_map/ppermute | solution.py:446
  3.7 11.2 %collective-permute-start.1 = (bf16[64,512]{1,0:T(8,128)(2,1)S(1)}, bf16[64,512]{1,0:T(8,128)(2,1)S(1)}, u32[]{:S(2)}, u32[]{:S(2)}) collective-permute-start(bf16[64,512]{1,0:T(8,128)(2,1)S(1)} %get-tuple-element.27), channel_id=1, source_target_pairs={{0,4},{4,0},{8,12},{12,8},{16,20},{20,16},{24,28},{28,24},{1,5},{5... | collective-permute-start | bytes 196616 | tf_op jit(solution)/shard_map/ppermute | solution.py:446
  20.4 1.4 %collective-permute-start.4 = (f32[16,2048]{1,0:T(8,128)S(1)}, f32[16,2048]{1,0:T(8,128)S(1)}, u32[]{:S(2)}, u32[]{:S(2)}) collective-permute-start(f32[16,2048]{1,0:T(8,128)S(1)} %get-tuple-element.35), channel_id=1, source_target_pairs={{0,1},{1,0},{2,3},{3,2},{4,5},{5,4},{6,7},{7,6},{8,9},{9,8},{10,11... | collective-permute-start | bytes 393224 | tf_op jit(solution)/shard_map/ppermute | solution.py:413
  21.8 12.2 %collective-permute-start.5 = (f32[16,2048]{1,0:T(8,128)S(1)}, f32[16,2048]{1,0:T(8,128)S(1)}, u32[]{:S(2)}, u32[]{:S(2)}) collective-permute-start(f32[16,2048]{1,0:T(8,128)S(1)} %add.21), channel_id=1, source_target_pairs={{0,2},{1,3},{2,0},{3,1},{4,6},{5,7},{6,4},{7,5},{8,10},{9,11},{10,... | collective-permute-start | bytes 393224 | tf_op jit(solution)/shard_map/ppermute | solution.py:413
  23.3 47.5 %collective-permute-start.3 = (bf16[24,32,512]{2,1,0:T(8,128)(2,1)S(1)}, bf16[24,32,512]{2,1,0:T(8,128)(2,1)S(1)}, u32[]{:S(2)}, u32[]{:S(2)}) collective-permute-start(bf16[24,32,512]{2,1,0:T(8,128)(2,1)S(1)} %get-tuple-element.32), channel_id=1, source_target_pairs={{4,8},{8,4},{12,16},{16,12},{20,24},{24,20},{5,9},{9,5},{13,17},{1... | collective-permute-start | bytes 2359304 | tf_op jit(solution)/shard_map/ppermute | solution.py:446
  24.0 49.4 %collective-permute-start.2 = (bf16[24,32,512]{2,1,0:T(8,128)(2,1)S(1)}, bf16[24,32,512]{2,1,0:T(8,128)(2,1)S(1)}, u32[]{:S(2)}, u32[]{:S(2)}) collective-permute-start(bf16[24,32,512]{2,1,0:T(8,128)(2,1)S(1)} %get-tuple-element.31), channel_id=1, source_target_pairs={{0,4},{4,0},{8,12},{12,8},{16,20},{20,16},{24,28},{28,24},{1,5},{5... | collective-permute-start | bytes 2359304 | tf_op jit(solution)/shard_map/ppermute | solution.py:446
  36.1 30.0 %copy-start = (bf16[32,25,2048]{2,0,1:T(8,128)(2,1)S(1)}, bf16[32,25,2048]{2,0,1:T(8,128)(2,1)}, u32[]{:S(2)}) copy-start(bf16[32,25,2048]{2,0,1:T(8,128)(2,1)} %param.10) | copy-start | bytes 9830404
  36.1 9.7 %collective-permute-start.6 = (f32[16,1024]{1,0:T(8,128)S(1)}, f32[16,1024]{1,0:T(8,128)S(1)}, u32[]{:S(2)}, u32[]{:S(2)}) collective-permute-start(f32[16,1024]{1,0:T(8,128)S(1)} %structure.1), channel_id=1, source_target_pairs={{0,8},{4,12},{8,0},{12,4},{16,24},{20,28},{24,16},{28,20},{1,9},{5... | collective-permute-start | bytes 196616 | tf_op jit(solution)/shard_map/ppermute | solution.py:413
  45.8 5.2 %collective-permute-start.7 = (f32[16,1024]{1,0:T(8,128)S(1)}, f32[16,1024]{1,0:T(8,128)S(1)}, u32[]{:S(2)}, u32[]{:S(2)}) collective-permute-start(f32[16,1024]{1,0:T(8,128)S(1)} %add.23), channel_id=1, source_target_pairs={{0,16},{4,20},{8,24},{12,28},{16,0},{20,4},{24,8},{28,12},{1,17},{... | collective-permute-start | bytes 196616 | tf_op jit(solution)/shard_map/ppermute | solution.py:413
  51.0 10.5 %collective-permute-start.8 = (f32[16,1024]{1,0:T(8,128)S(1)}, f32[16,1024]{1,0:T(8,128)S(1)}, u32[]{:S(2)}, u32[]{:S(2)}) collective-permute-start(f32[16,1024]{1,0:T(8,128)S(1)} %add.24), channel_id=1, source_target_pairs={{0,4},{4,0},{8,12},{12,8},{16,20},{20,16},{24,28},{28,24},{1,5},{5... | collective-permute-start | bytes 196616 | tf_op jit(solution)/shard_map/ppermute | solution.py:413
  63.9 1.5 %collective-permute-start.9 = (f32[24,2048]{1,0:T(8,128)S(1)}, f32[24,2048]{1,0:T(8,128)S(1)}, u32[]{:S(2)}, u32[]{:S(2)}) collective-permute-start(f32[24,2048]{1,0:T(8,128)S(1)} %fields.1), channel_id=1, source_target_pairs={{0,1},{1,0},{2,3},{3,2},{4,5},{5,4},{6,7},{7,6},{8,9},{9,8},{10,11... | collective-permute-start | bytes 589832 | tf_op jit(solution)/shard_map/ppermute | solution.py:413
  65.5 10.7 %collective-permute-start.10 = (f32[24,2048]{1,0:T(8,128)S(1)}, f32[24,2048]{1,0:T(8,128)S(1)}, u32[]{:S(2)}, u32[]{:S(2)}) collective-permute-start(f32[24,2048]{1,0:T(8,128)S(1)} %add.26), channel_id=1, source_target_pairs={{0,2},{1,3},{2,0},{3,1},{4,6},{5,7},{6,4},{7,5},{8,10},{9,11},{10,... | collective-permute-start | bytes 589832 | tf_op jit(solution)/shard_map/ppermute | solution.py:413

commit v3 on v2

--- a/solution.py
+++ b/solution.py
@@ -12,6 +12,8 @@
 BS = 256
 NNB = 3
 REACH = 2
+KMAX = 7
+LOG2E = 1.4426950408889634
 
 ewald_scale = 40.0
 ewald_damp = 0.02
@@ -43,6 +45,11 @@
 def halves(x):
     high = x.astype(BF)
     return high, (x - high.astype(F32)).astype(BF)
+
+
+def thirds(x):
+    high, low = halves(x)
+    return high, low, ((x - high.astype(F32)) - low.astype(F32)).astype(BF)
 
 
 def load_kernel(chans, rows, width, place, *refs):
@@ -120,8 +127,9 @@
             bias = jnp.where((row == 0) & (lane >= live), -1e30, 0.0).astype(BF)
             v0[b] = values
             for h in range(heads):
-                kaug[b, h, 0:head_dim, :] = keys[h * head_dim : (h + 1) * head_dim]
-                kaug[b, h, head_dim : head_dim + 16, :] = bias
+                for copy in range(3):
+                    kaug[b, h, copy * head_dim : (copy + 1) * head_dim, :] = keys[h * head_dim : (h + 1) * head_dim]
+                kaug[b, h, 3 * head_dim : 3 * head_dim + 16, :] = bias
 
         for b in range(blocks):
             cols = slice(b * BS, (b + 1) * BS)
@@ -135,25 +143,26 @@
     g = i + REACH if part == "interior" else edge_block(i, place, blocks)
     own_count = counts[first + g]
     live_q = lax.broadcasted_iota(jnp.int32, (1, BS), 1) < own_count
-    ones = jnp.where(lax.broadcasted_iota(jnp.int32, (16, BS), 0) == 0, 1.0, 0.0).astype(BF)
+    top_row = jnp.where(lax.broadcasted_iota(jnp.int32, (16, BS), 0) == 0, 1.0, 0.0).astype(BF)
     listed = [lists[e, g] - (first - REACH) for e in range(NNB)]
+    scores = []
+    for h in range(heads):
+        q = q_ref[h * head_dim : (h + 1) * head_dim, :].astype(F32) * (head_dim ** (-0.5) * LOG2E)
+        qa = jnp.concatenate([*thirds(q), top_row], axis=0)
+        scores.append([dot(kaug[b, h], qa, ((0,), (0,))) for b in listed])
     charge = None
     for h in range(heads):
-        q = (q_ref[h * head_dim : (h + 1) * head_dim, :].astype(F32) * head_dim ** (-0.5)).astype(BF)
-        qa = jnp.concatenate([q, ones], axis=0)
-        scores = [dot(kaug[b, h], qa, ((0,), (0,))) for b in listed]
-        top = functools.reduce(jnp.maximum, [jnp.max(s, axis=0, keepdims=True) for s in scores])
-        denominator = 0.0
+        top = functools.reduce(jnp.maximum, [jnp.max(s, axis=0, keepdims=True) for s in scores[h]])
         mixed = 0.0
         for e, b in enumerate(listed):
-            w = jnp.exp(scores[e] - top)
-            denominator = denominator + jnp.sum(w, axis=0, keepdims=True)
-            w16 = w.astype(BF)
-            p_ref[0, h, e * BS : (e + 1) * BS, :] = w16
-            mixed = mixed + dot(v0[b, h * head_chan : (h + 1) * head_chan, :], w16, ((1,), (0,)))
+            w16 = jnp.exp2(scores[h][e] - top).astype(BF)
+            p_ref[i, h, e * BS : (e + 1) * BS, :] = w16
+            v = jnp.concatenate([v0[b, h * head_chan : (h + 1) * head_chan, :], top_row], axis=0)
+            mixed = mixed + dot(v, w16, ((1,), (0,)))
+        denominator = mixed[head_chan : head_chan + 1]
         scale = jnp.where(live_q, 1.0 / denominator, 0.0)
-        scale_ref[0, h : h + 1, :] = scale
-        att0 = (mixed * scale).astype(BF)
+        scale_ref[i, h : h + 1, :] = scale
+        att0 = (mixed[:head_chan] * scale).astype(BF)
         term = dot(cw_ref[:, h * head_chan : (h + 1) * head_chan], att0, ((1,), (0,)))
         charge = term if charge is None else charge + term
     charge_ref[...] = charge
@@ -185,12 +194,12 @@
             ]
             + [whole(s.shape) for s in sides[:2]] + [any_space] * len(sides[2:]),
             out_specs=[
-                pl.BlockSpec((1, heads, NNB * BS, BS), lambda i, *_: (i, 0, 0, 0)),
-                pl.BlockSpec((1, heads, BS), lambda i, *_: (i, 0, 0)),
+                whole((steps, heads, NNB * BS, BS)),
+                whole((steps, heads, BS)),
                 pl.BlockSpec((nq, BS), lambda i, *s: (0, at(i, *s))),
             ],
             scratch_shapes=[
-                pltpu.VMEM((band, heads, head_dim + 16, BS), BF),
+                pltpu.VMEM((band, heads, 3 * head_dim + 16, BS), BF),
                 pltpu.VMEM((band, chans, BS), BF),
             ],
         ),
@@ -208,7 +217,7 @@
     )(lists, counts, place, q, k, v0, cw, *sides)
 
 
-def mix_kernel(heads, head_dim, head_chan, blocks, part, lists, place, v_ref, p_ref, scale_ref, *refs):
+def mix_kernel(heads, head_dim, head_chan, blocks, part, skip, lists, place, v_ref, p_ref, scale_ref, *refs):
     halo, out_ref = refs[: 2 if part in ("far", "near") else 0], refs[-2 if part in ("far", "near") else -1]
     comps = v_ref.shape[0]
     i = pl.program_id(0)
@@ -244,8 +253,8 @@
         acc = 0.0
         for e in range(NNB):
             v = pick(listed[e], rows).reshape(comps * head_chan, BS)
-            acc = acc + dot(v, p_ref[0, h, e * BS : (e + 1) * BS, :], ((1,), (0,)))
-        acc = acc * scale_ref[0, h : h + 1, :]
+            acc = acc + dot(v, p_ref[i + skip, h, e * BS : (e + 1) * BS, :], ((1,), (0,)))
+        acc = acc * scale_ref[i + skip, h : h + 1, :]
         out_ref[:, rows, :] = acc.astype(BF).reshape(comps, head_chan, BS)
 
 
@@ -264,14 +273,14 @@
     whole = lambda shape: pl.BlockSpec(shape, lambda g, *_: (0,) * len(shape), pipeline_mode=pl.Buffered(1))
     extra = list(halo) + ([] if prev is None else [prev])
     return pl.pallas_call(
-        functools.partial(mix_kernel, heads, head_dim, chans // heads, blocks, part),
+        functools.partial(mix_kernel, heads, head_dim, chans // heads, blocks, part, skip),
         grid_spec=pltpu.PrefetchScalarGridSpec(
             num_scalar_prefetch=2,
             grid=(steps,),
             in_specs=[
                 whole(v.shape),
-                pl.BlockSpec((1, heads, NNB * BS, BS), lambda i, *_: (i + skip, 0, 0, 0)),
-                pl.BlockSpec((1, heads, BS), lambda i, *_: (i + skip, 0, 0)),
+                whole(p.shape),
+                whole(scale.shape),
             ]
             + [whole(x.shape) for x in halo]
             + ([] if prev is None else [pl.BlockSpec(memory_space=pl.ANY)]),
@@ -288,42 +297,94 @@
     )(lists, place, v, p, scale, *extra)
 
 
-def table_kernel(place, n_ref, f_ref, out_ref, parts):
+SPREAD = 2 * KMAX + 1
+WIDE = 16
+
+
+def wave(turns):
+    r = turns - jnp.round(turns)
+    u = r * r
+    return horner(COS, u), horner(SIN, u) * r
+
+
+def grid_points(base, planes):
+    rows = planes * SPREAD * WIDE
+    place = lax.broadcasted_iota(jnp.int32, (1, rows), 1).astype(F32)
+    pair = jnp.floor((place + 0.5) * (1.0 / WIDE))
+    n3 = place - pair * WIDE - KMAX
+    plane = jnp.floor((pair + 0.5) * (1.0 / SPREAD))
+    return plane + base.astype(F32), pair - plane * SPREAD - KMAX, n3
+
+
+def grid_weights(n, base, planes):
+    pairs = planes * SPREAD
+    high = -(-pairs // 16) * 16
+    flip = jnp.where(n[0:1] < 0, -1, 1)
+    pair = (n[0:1] * flip - base) * SPREAD + n[1:2] * flip + KMAX
+    mine = (n[0:1] * flip >= base) & (n[0:1] * flip < base + planes)
+    third = n[2:3] * flip + KMAX
+    count = n.shape[1]
+    is_pair = (lax.broadcasted_iota(jnp.int32, (high, count), 0) == pair) & mine
+    is_third = lax.broadcasted_iota(jnp.int32, (WIDE, count), 0) == third
+    one_hot = lambda x: jnp.where(x, 1.0, 0.0).astype(BF)
+    found = dot(one_hot(is_pair), one_hot(is_third), ((1,), (1,)))
+    rows = pairs * WIDE
+    row = lax.broadcasted_iota(jnp.int32, (WIDE, rows), 0)
+    spread = one_hot((lax.broadcasted_iota(jnp.int32, (WIDE, rows), 1) & (WIDE - 1)) == row)
+    wide = sum(dot(part, spread, ((1,), (0,))) for part in thirds(found))
+    own = lax.broadcasted_iota(jnp.int32, (high, rows), 1) >> (WIDE.bit_length() - 1)
+    times = jnp.sum(jnp.where(own == lax.broadcasted_iota(jnp.int32, (high, rows), 0), wide, 0.0), axis=0, keepdims=True)
+    n1, n2, n3 = grid_points(base, planes)
+    norm = n1 * n1 + n2 * n2 + n3 * n3
+    safe = jnp.maximum(norm, 1.0)
+    return jnp.where(norm > 0, times * (ewald_scale * jnp.exp(-ewald_damp * safe) / safe), 0.0)
+
+
+def table_kernel(planes, place, n_ref, f_ref, out_ref, weight_ref, pairs):
+    base = place[1] * planes
+
     @pl.when(pl.program_id(0) == 0)
     def _():
-        f = f_ref[...]
-        high, low = halves(f)
-        rest = ((f - high.astype(F32)) - low.astype(F32)).astype(BF)
-        parts[...] = jnp.concatenate([high, low, rest], axis=0)
-
-    n = n_ref[...].astype(F32).astype(BF)
-    turns = dot(jnp.concatenate([n, n, n], axis=0), parts[...], ((0,), (0,)))
-    r = turns - jnp.round(turns)
-    u = r * r
-    out_ref[0] = horner(COS, u).astype(BF)
-    out_ref[1] = (horner(SIN, u) * r).astype(BF)
-
-
-def table_call(place, n, f, waves):
-    step = 128
+        weight_ref[...] = grid_weights(n_ref[...], base, planes)
+
+    atoms = f_ref.shape[1]
+    wide = lax.broadcasted_iota(jnp.int32, (WIDE, atoms), 0)
+    steps = (wide - KMAX).astype(F32)
+    second = wave(steps * f_ref[1:2, :])
+    third = wave(steps * f_ref[2:3, :])
+    for plane in range(planes):
+        first = wave((base + plane).astype(F32) * f_ref[0:1, :])
+        pairs[0, plane] = first[0] * second[0] - first[1] * second[1]
+        pairs[1, plane] = first[1] * second[0] + first[0] * second[1]
+        for m in range(SPREAD):
+            real, imag = pairs[0, plane, m : m + 1, :], pairs[1, plane, m : m + 1, :]
+            at = slice((plane * SPREAD + m) * WIDE, (plane * SPREAD + m + 1) * WIDE)
+            out_ref[0, at, :] = (real * third[0] - imag * third[1]).astype(BF)
+            out_ref[1, at, :] = (imag * third[0] + real * third[1]).astype(BF)
+
+
+def table_call(place, n, f, planes):
+    rows = planes * SPREAD * WIDE
     atoms = f.shape[1]
-    return pl.pallas_call(
-        table_kernel,
+    step = 256
+    return pl.pallas_call(
+        functools.partial(table_kernel, planes),
         grid_spec=pltpu.PrefetchScalarGridSpec(
             num_scalar_prefetch=1,
-            grid=(waves // step,),
+            grid=(atoms // step,),
             in_specs=[
-                pl.BlockSpec((3, step), lambda i, place: (0, place[1] * (waves // step) + i)),
-                pl.BlockSpec(f.shape, lambda i, place: (0, 0)),
+                pl.BlockSpec(n.shape, lambda i, place: (0, 0), pipeline_mode=pl.Buffered(1)),
+                pl.BlockSpec((3, step), lambda i, place: (0, i)),
             ],
-            out_specs=pl.BlockSpec((2, step, atoms), lambda i, place: (0, i, 0)),
-            scratch_shapes=[pltpu.VMEM((9, atoms), BF)],
-        ),
-        out_shape=jax.ShapeDtypeStruct((2, waves, atoms), BF),
-        compiler_params=params(16),
-        cost_estimate=pl.CostEstimate(
-            flops=waves * atoms * 400, transcendentals=0, bytes_accessed=waves * atoms * 4
-        ),
+            out_specs=[
+                pl.BlockSpec((2, rows, step), lambda i, place: (0, 0, i)),
+                pl.BlockSpec((1, rows), lambda i, place: (0, 0)),
+            ],
+            scratch_shapes=[pltpu.VMEM((2, planes, WIDE, step), F32)],
+        ),
+        out_shape=[jax.ShapeDtypeStruct((2, rows, atoms), BF), jax.ShapeDtypeStruct((1, rows), F32)],
+        compiler_params=params(12),
+        cost_estimate=pl.CostEstimate(flops=rows * atoms * 40, transcendentals=0, bytes_accessed=rows * atoms * 4),
         name="table",
     )(place, n, f)
 
@@ -338,7 +399,7 @@
 
 def structure_call(c, table, inv_root):
     rows, atoms = table.shape
-    step = min(256, rows)
+    step = rows
     nq = c.shape[0]
     return pl.pallas_call(
         functools.partial(structure_kernel, inv_root),
@@ -352,26 +413,23 @@
     )(c, table)
 
 
-def field_kernel(place, s_ref, n_ref, c_ref, t_ref, out_ref, coeff):
+def field_kernel(planes, place, s_ref, weight_ref, c_ref, t_ref, out_ref, coeff):
     nq = c_ref.shape[0]
-    waves = n_ref.shape[1]
+    waves = weight_ref.shape[1]
 
     @pl.when(pl.program_id(0) == 0)
     def _():
-        n = n_ref[...].astype(F32)
-        norm = n[0:1] * n[0:1] + n[1:2] * n[1:2] + n[2:3] * n[2:3]
-        weight = ewald_scale * jnp.exp(-ewald_damp * norm) / norm
-        real = s_ref[:, :waves] * weight
-        imag = s_ref[:, waves:] * weight
-        with_cos = jnp.concatenate([real] + [-imag * n[d : d + 1] for d in range(3)], axis=0)
-        with_sin = jnp.concatenate([imag] + [real * n[d : d + 1] for d in range(3)], axis=0)
+        n = grid_points(place[1] * planes, planes)
+        real = s_ref[:, :waves] * weight_ref[...]
+        imag = s_ref[:, waves:] * weight_ref[...]
+        with_cos = jnp.concatenate([real] + [-imag * n[d] for d in range(3)], axis=0)
+        with_sin = jnp.concatenate([imag] + [real * n[d] for d in range(3)], axis=0)
         for part, x in enumerate((with_cos, with_sin)):
             high, low = halves(x)
-            cols = slice(part * waves, (part + 1) * waves)
-            coeff[0 : 4 * nq, cols] = high
-            coeff[4 * nq :, cols] = low
-
-    both = dot(coeff[...], t_ref[...], ((1,), (0,)))
+            coeff[part, 0 : 4 * nq] = high
+            coeff[part, 4 * nq :] = low
+
+    both = dot(coeff[0], t_ref[0], ((1,), (0,))) + dot(coeff[1], t_ref[1], ((1,), (0,)))
     sums = both[: 4 * nq] + both[4 * nq :]
     c = c_ref[...]
     out_ref[0:nq, :] = sums[:nq]
@@ -381,29 +439,45 @@
     out_ref[nq : nq + 8, :] = jnp.concatenate(forces + [jnp.zeros((5, c.shape[1]), F32)], axis=0)
 
 
-def field_call(place, s, n, c, table, waves):
-    rows, atoms = table.shape
+def field_call(place, s, weight, c, table, planes):
+    _, rows, atoms = table.shape
     step = 512
     nq = c.shape[0]
     return pl.pallas_call(
-        field_kernel,
+        functools.partial(field_kernel, planes),
         grid_spec=pltpu.PrefetchScalarGridSpec(
             num_scalar_prefetch=1,
             grid=(atoms // step,),
             in_specs=[
-                pl.BlockSpec((nq, rows), lambda i, place: (0, 0)),
-                pl.BlockSpec((3, waves), lambda i, place: (0, place[1])),
+                pl.BlockSpec(s.shape, lambda i, place: (0, 0)),
+                pl.BlockSpec(weight.shape, lambda i, place: (0, 0)),
                 pl.BlockSpec((nq, step), lambda i, place: (0, i)),
-                pl.BlockSpec((rows, step), lambda i, place: (0, i)),
+                pl.BlockSpec((2, rows, step), lambda i, place: (0, 0, i)),
             ],
             out_specs=pl.BlockSpec((nq + 8, step), lambda i, place: (0, i)),
-            scratch_shapes=[pltpu.VMEM((8 * nq, rows), BF)],
+            scratch_shapes=[pltpu.VMEM((2, 8 * nq, rows), BF)],
         ),
         out_shape=jax.ShapeDtypeStruct((nq + 8, atoms), F32),
         compiler_params=params(12),
         cost_estimate=pl.CostEstimate(flops=rows * atoms * 512, transcendentals=0, bytes_accessed=rows * atoms * 2),
         name="fields",
-    )(place, s, n, c, table)
+    )(place, s, weight, c, table)
+
+
+def finish_kernel(mine_ref, theirs_ref, potential_ref, force_ref):
+    nq = potential_ref.shape[0]
+    potential_ref[...] = mine_ref[0:nq] + theirs_ref[0:nq]
+    force_ref[...] = (mine_ref[nq : nq + 8] + theirs_ref[nq : nq + 8])[:3]
+
+
+def finish_call(mine, theirs, nq):
+    atoms = mine.shape[1]
+    return pl.pallas_call(
+        finish_kernel,
+        out_shape=[jax.ShapeDtypeStruct((nq, atoms), F32), jax.ShapeDtypeStruct((3, atoms), F32)],
+        compiler_params=pltpu.CompilerParams(vmem_limit_bytes=4 << 20),
+        name="finish",
+    )(mine, theirs)
 
 
 def exchanged(x, axis, step):
@@ -413,10 +487,10 @@
     return x + lax.ppermute(x, axis, [(i, i ^ step) for i in range(size)])
 
 
-def summed(x, axis, step=1):
+def summed(x, axis, step=1, stop=None):
     size = lax.axis_size(axis)
     assert size & (size - 1) == 0
-    while step < size:
+    while step < (stop or size):
         x = exchanged(x, axis, step)
         step *= 2
     return x
@@ -434,7 +508,8 @@
 ):
     heads, head_dim, atoms = queries.shape
     nq = charge_weight.shape[1]
-    waves = integer_wave_vectors.shape[1] // lax.axis_size("inner")
+    planes = (KMAX + 1) // lax.axis_size("inner")
+    assert planes * lax.axis_size("inner") == KMAX + 1
     inv_root = 1.0 / math.sqrt(atoms * lax.axis_size("seq"))
     place = jnp.stack([lax.axis_index("seq"), lax.axis_index("inner")]).astype(jnp.int32)
     width = REACH * BS
@@ -462,19 +537,22 @@
     p_out, scale_out, part = scores_call(
         "edges", lists, counts, place, asked, keys, v0, weight, (far, near, part), heads, head_dim
     )
-    table = table_call(place, vectors, fractional, waves).reshape(2 * waves, atoms)
+    table, wave_weight = table_call(place, vectors, fractional, planes)
     charges = summed(part, "inner")
-    structure = structure_call(charges, table, inv_root)
-    structure = exchanged(summed(structure, "seq", 2), "seq", 1)
-    fields = field_call(place, structure, vectors, charges, table, waves)
-    fields = summed(fields, "inner")
+    structure = structure_call(charges, table.reshape(-1, atoms), inv_root)
+    structure = summed(structure, "seq")
+    fields = field_call(place, structure, wave_weight, charges, table, planes)
+    last = lax.axis_size("inner") // 2
+    fields = summed(fields, "inner", stop=last)
+    others = lax.ppermute(fields, "inner", [(i, i ^ last) for i in range(2 * last)])
+    potential, forces = finish_call(fields, others, nq)
 
     mix = functools.partial(mix_call, heads=heads, head_dim=head_dim)
     attention = mix("low", lists, place, values, p_in, scale_in, (), None)
     attention = mix("high", lists, place, values, p_in, scale_in, (), attention)
     attention = mix("far", lists, place, values, p_out, scale_out, (far, far_big), attention)
     attention = mix("near", lists, place, values, p_out, scale_out, (near, near_big), attention)
-    return (attention.transpose(1, 0, 2), fields[:nq], fields[nq : nq + 3])
+    return (attention.transpose(1, 0, 2), potential, forces)
 
 
 def solution(mesh):

time: 78.3 us -> 85.2 us (1.088)
  waiting for transfers between devices: 22.3 us -> 33.4 us
  Pallas kernels: 33.2 us -> 28.6 us
  starting transfers between devices: 19.6 us -> 22.1 us
  local copies, waits for them, and re-layouts: 1.3 us -> 0.01 us
    ppermute x7 -> x6, waiting for transfers between devices: 22.3 us -> 33.4 us  [exchanged(): return x + lax.ppermute(x, axis, [(i, i ^ step) for i in range(size)])]
    pallas_call x2 -> x3, Pallas kernels: 7.96 us -> 5.91 us  [the longest x1 2.8 us: table_call(): pl.pallas_call(functools.partial(table_kernel, planes), grid_spec=pltpu.P...]
    pallas_call x2, Pallas kernels: 10.8 us -> 8.94 us  [scores_call(): pl.pallas_call(functools.partial(score_kernel, heads, head_dim, head_chan...]
    ppermute x7 -> x6, starting transfers between devices: 8.16 us -> 9.72 us  [exchanged(): return x + lax.ppermute(x, axis, [(i, i ^ step) for i in range(size)])]
    ppermute x0 -> x1, starting transfers between devices: none -> 1.53 us  [whole_step(): lax.ppermute(fields, 'inner', [(i, i ^ last) for i in range(2 * last)])]
    slice x2 -> x0, local copies, waits for them, and re-layouts: 1.28 us -> none  [whole_step(): return (attention.transpose(1, 0, 2), fields[:nq], fields[nq:nq + 3])]
  transfers between devices with their start and end apart: 11 -> 11, of which waited for: 5 -> 5; matrix products, arithmetic and copies ran while one was open for 0% -> 0% of each run, Pallas kernels for 33% -> 25%
where the time goes in v3:
time: 85.2 us; the launch traced here: 85 us
  waiting for transfers between devices  33.4 us (39%)
  Pallas kernels  28.6 us (34%)
  starting transfers between devices  22.1 us (26%)
    ppermute x6, waiting for transfers between devices, exchanged(): return x + lax.ppermute(x, axis, [(i, i ^ step) for i in range(size)])  33.4 us
    ppermute x4, starting transfers between devices, swap(): return lax.ppermute(x, 'seq', pairs)  10.8 us
    pallas_call x4, Pallas kernels, mix_call(): pl.pallas_call(functools.partial(mix_kernel, heads, head_dim, chans // he...  10 us
    ppermute x6, starting transfers between devices, exchanged(): return x + lax.ppermute(x, axis, [(i, i ^ step) for i in range(size)])  9.72 us
    pallas_call x2, Pallas kernels, scores_call(): pl.pallas_call(functools.partial(score_kernel, heads, head_dim, head_chan...  8.94 us
    pallas_call x1, Pallas kernels, table_call(): pl.pallas_call(functools.partial(table_kernel, planes), grid_spec=pltpu.P...  2.8 us
    pallas_call x1, Pallas kernels, field_call(): pl.pallas_call(functools.partial(field_kernel, planes), grid_spec=pltpu.P...  2.43 us
    pallas_call x1, Pallas kernels, load_call(): pl.pallas_call(functools.partial(load_kernel, chans, rows, width), grid_s...  2.34 us
  transfers between devices with their start and end apart: 11, of which 5 were waited for; matrix products, arithmetic and copies ran while one was open for 0% of the time, Pallas kernels for 25%

profile of v3, /device:TPU:0, one launch (start us, length us, event | category | flops | bytes accessed | tf_op | source)
XLA Modules:
  0.0 85.0 jit_solution(11880713859145343510)
XLA Ops:
  0.6 0.1 pad_add_fusion.place
  0.7 2.3 %load.1 = (bf16[64,512]{1,0:T(8,128)(2,1)S(1)}, bf16[64,512]{1,0:T(8,128)(2,1)S(1)}, bf16[24,32,512]{2,1,0:T(8,128)(2,1)S(1)}, bf16[24,32,512]{2,1,0:T(8,128)(2,...) custom-call(s32[2]{0:T(128)S(1)} %pad_add_fusion.place, ...), custom_call_target="tpu_custom_call" | custom-call | bytes 1638400 | tf_op jit(solution)/shard_map/load/pallas_call | solution.py:85
  3.1 0.0 copy-start.1
  3.1 0.7 collective-permute-start
  3.7 5.8 %collective-permute-start.1 = (bf16[64,512]{1,0:T(8,128)(2,1)S(1)}, bf16[64,512]{1,0:T(8,128)(2,1)S(1)}, u32[]{:S(2)}, u32[]{:S(2)}) collective-permute-start(bf16[64,512]{1,0:T(8,128)(2,1)S(1)} %get-tuple-element.31), channel_id=1, source_target_pairs={{0,4},{4,0},{8,12},{12,8},{16,20},{20,16},{24,28},{28,24},{1,5},{5... | collective-permute-start | bytes 196616 | tf_op jit(solution)/shard_map/ppermute | solution.py:521
  9.6 4.4 %shard_map.103 = (bf16[4,2,768,256]{3,2,1,0:T(8,128)(2,1)S(1)}, f32[4,2,256]{2,1,0:T(2,128)S(1)}, f32[16,2048]{1,0:T(8,128)S(1)}) custom-call(s32[3,8]{1,0:T(4,128)S(1)} %get-tuple-element.24.lists, s32[64]{0:T(128)S(1)} %get-tuple-element.25.counts, s32[2]{0:T(128)S(1)} %pad_add_fusion.place, bf16[32,2048]{1,0:T(8,128)(2,1)S(1)} %get-tuple-element.26.refs_0_, ...), custom_call_target="tpu_custom_call" | custom-call | flops 314572800 | bytes 3145728 | tf_op jit(solution)/shard_map/pallas_call | solution.py:184
  14.0 0.0 collective-permute-done.1.refs_5_.refs_0_
  14.0 4.5 %shard_map.104 = (bf16[4,2,768,256]{3,2,1,0:T(8,128)(2,1)S(1)}, f32[4,2,256]{2,1,0:T(2,128)S(1)}, f32[16,2048]{1,0:T(8,128)S(1)}) custom-call(s32[3,8]{1,0:T(4,128)S(1)} %get-tuple-element.24.lists, s32[64]{0:T(128)S(1)} %get-tuple-element.25.counts, s32[2]{0:T(128)S(1)} %pad_add_fusion.place, ...), custom_call_target="tpu_custom_call", output_to_operand_aliasing={{2}: (9, {})} | custom-call | flops 314572800 | bytes 3145728 | tf_op jit(solution)/shard_map/pallas_call | solution.py:184
  18.5 0.0 collective-permute-start.4
  18.6 0.7 collective-permute-start.3
  19.3 0.6 collective-permute-done.4
  19.9 1.5 %collective-permute-start.5 = (f32[16,2048]{1,0:T(8,128)S(1)}, f32[16,2048]{1,0:T(8,128)S(1)}, u32[]{:S(2)}, u32[]{:S(2)}) collective-permute-start(f32[16,2048]{1,0:T(8,128)S(1)} %add.18), channel_id=1, source_target_pairs={{0,2},{1,3},{2,0},{3,1},{4,6},{5,7},{6,4},{7,5},{8,10},{9,11},{10,... | collective-permute-start | bytes 393224 | tf_op jit(solution)/shard_map/ppermute | solution.py:487
  21.5 3.6 %collective-permute-start.2 = (bf16[24,32,512]{2,1,0:T(8,128)(2,1)S(1)}, bf16[24,32,512]{2,1,0:T(8,128)(2,1)S(1)}, u32[]{:S(2)}, u32[]{:S(2)}) collective-permute-start(bf16[24,32,512]{2,1,0:T(8,128)(2,1)S(1)} %get-tuple-element.35), channel_id=1, source_target_pairs={{0,4},{4,0},{8,12},{12,8},{16,20},{20,16},{24,28},{28,24},{1,5},{5... | collective-permute-start | bytes 2359304 | tf_op jit(solution)/shard_map/ppermute | solution.py:521
  25.1 2.8 %table.1 = (bf16[2,480,2048]{2,1,0:T(8,128)(2,1)S(1)}, f32[1,480]{1,0:T(1,128)S(1)}) custom-call(s32[2]{0:T(128)S(1)} %pad_add_fusion.place, s32[3,2048]{1,0:T(4,128)S(1)} %get-tuple-element.40.n_ref, f32[3,2048]{1,0:T(4,128)S(1)} %copy-done.1), custom_call_target="tpu_custom_call" | custom-call | flops 39321600 | bytes 3932160 | tf_op jit(solution)/shard_map/table/pallas_call | solution.py:370
  27.9 0.0 collective-permute-done.5
  27.9 1.4 %structure.1 = f32[16,960]{1,0:T(8,128)S(1)} custom-call(f32[16,2048]{1,0:T(8,128)S(1)} %add.19.c_ref, bf16[960,2048]{1,0:T(8,128)(2,1)S(1)} %bitcast.14), custom_call_target="tpu_custom_call" | custom-call | flops 1006632960 | bytes 3932160 | tf_op jit(solution)/shard_map/structure/pallas_call | solution.py:404
  29.3 1.3 %collective-permute-start.6 = (f32[16,960]{1,0:T(8,128)S(1)}, f32[16,960]{1,0:T(8,128)S(1)}, u32[]{:S(2)}, u32[]{:S(2)}) collective-permute-start(f32[16,960]{1,0:T(8,128)S(1)} %structure.1), channel_id=1, source_target_pairs={{0,4},{4,0},{8,12},{12,8},{16,20},{20,16},{24,28},{28,24},{1,5},{5... | collective-permute-start | bytes 184328 | tf_op jit(solution)/shard_map/ppermute | solution.py:487
  30.7 26.8 %collective-permute-done.6 = f32[16,960]{1,0:T(8,128)S(1)} collective-permute-done((f32[16,960]{1,0:T(8,128)S(1)}, f32[16,960]{1,0:T(8,128)S(1)}, u32[]{:S(2)}, u32[]{:S(2)}) %collective-permute-start.6) | collective-permute-done | bytes 61472 | tf_op jit(solution)/shard_map/ppermute | solution.py:487
  57.5 3.7 %collective-permute-start.7 = (f32[16,960]{1,0:T(8,128)S(1)}, f32[16,960]{1,0:T(8,128)S(1)}, u32[]{:S(2)}, u32[]{:S(2)}) collective-permute-start(f32[16,960]{1,0:T(8,128)S(1)} %add.20), channel_id=1, source_target_pairs={{0,8},{4,12},{8,0},{12,4},{16,24},{20,28},{24,16},{28,20},{1,9},{5... | collective-permute-start | bytes 184328 | tf_op jit(solution)/shard_map/ppermute | solution.py:487
  61.2 2.3 %collective-permute-done.7 = f32[16,960]{1,0:T(8,128)S(1)} collective-permute-done((f32[16,960]{1,0:T(8,128)S(1)}, f32[16,960]{1,0:T(8,128)S(1)}, u32[]{:S(2)}, u32[]{:S(2)}) %collective-permute-start.7) | collective-permute-done | bytes 61472 | tf_op jit(solution)/shard_map/ppermute | solution.py:487
  63.5 3.0 %collective-permute-start.8 = (f32[16,960]{1,0:T(8,128)S(1)}, f32[16,960]{1,0:T(8,128)S(1)}, u32[]{:S(2)}, u32[]{:S(2)}) collective-permute-start(f32[16,960]{1,0:T(8,128)S(1)} %add.21), channel_id=1, source_target_pairs={{0,16},{4,20},{8,24},{12,28},{16,0},{20,4},{24,8},{28,12},{1,17},{... | collective-permute-start | bytes 184328 | tf_op jit(solution)/shard_map/ppermute | solution.py:487
  66.5 2.2 %collective-permute-done.8 = f32[16,960]{1,0:T(8,128)S(1)} collective-permute-done((f32[16,960]{1,0:T(8,128)S(1)}, f32[16,960]{1,0:T(8,128)S(1)}, u32[]{:S(2)}, u32[]{:S(2)}) %collective-permute-start.8) | collective-permute-done | bytes 61472 | tf_op jit(solution)/shard_map/ppermute | solution.py:487
  68.8 2.4 %fields.1 = f32[24,2048]{1,0:T(8,128)S(1)} custom-call(s32[2]{0:T(128)S(1)} %pad_add_fusion.place, f32[16,960]{1,0:T(8,128)S(1)} %add.22.s_ref, f32[1,480]{1,0:T(1,128)S(1)} %get-tuple-element.42.weight_ref, f32[16,2048]{1,0:T(8,128)S(1)} %add.19.c_ref, bf16[2,480,2048]{2,1,0:T(8,128)(2,1)S(1)} %get-tuple-element.41.t_ref), custom_call_target="tpu_custom_call" | custom-call | flops 503316480 | bytes 1966080 | tf_op jit(solution)/shard_map/fields/pallas_call | solution.py:446
  71.2 0.1 collective-permute-start.9
  71.3 1.4 %collective-permute-done.9 = f32[24,2048]{1,0:T(8,128)S(1)} collective-permute-done((f32[24,2048]{1,0:T(8,128)S(1)}, f32[24,2048]{1,0:T(8,128)S(1)}, u32[]{:S(2)}, u32[]{:S(2)}) %collective-permute-start.9) | collective-permute-done | bytes 196640 | tf_op jit(solution)/shard_map/ppermute | solution.py:487
  72.8 1.5 %collective-permute-start.10 = (f32[24,2048]{1,0:T(8,128)S(1)}, f32[24,2048]{1,0:T(8,128)S(1)}, u32[]{:S(2)}, u32[]{:S(2)}) collective-permute-start(f32[24,2048]{1,0:T(8,128)S(1)} %add.23.mine_ref), channel_id=1, source_target_pairs={{0,2},{1,3},{2,0},{3,1},{4,6},{5,7},{6,4},{7,5},{8,10},{9,11},{10,... | collective-permute-start | bytes 589832 | tf_op jit(solution)/shard_map/ppermute | solution.py:547
  74.3 2.3 %shard_map.105.refs_0_ = bf16[25,32,2048]{2,1,0:T(8,128)(2,1)} custom-call(s32[3,8]{1,0:T(4,128)S(1)} %get-tuple-element.24.lists, s32[2]{0:T(128)S(1)} %pad_add_fusion.place, bf16[25,32,2048]{2,1,0:T(8,128)(2,1)S(1)} %bitcast.10, bf16[4,2,768,256]{3,2,1,0:T(8,128)(2,1)S(1)} %get-tuple-element.37.p_ref, f32[4,2,256]{2,1,0:T(2,128)S(1)} %get-tuple-element.38.scale_ref), custom_call_target="tpu_custom_call" | custom-call | flops 629145600 | bytes 3276800 | tf_op jit(solution)/shard_map/pallas_call | solution.py:275
  76.6 2.3 %shard_map.106.refs_2_ = bf16[25,32,2048]{2,1,0:T(8,128)(2,1)} custom-call(s32[3,8]{1,0:T(4,128)S(1)} %get-tuple-element.24.lists, s32[2]{0:T(128)S(1)} %pad_add_fusion.place, bf16[25,32,2048]{2,1,0:T(8,128)(2,1)S(1)} %bitcast.11, bf16[4,2,768,256]{3,2,1,0:T(8,128)(2,1)S(1)} %get-tuple-element.37.p_ref, ...), custom_call_target="tpu_custom_call", output_to_operand_aliasing={{}: (5, {})} | custom-call | flops 629145600 | bytes 3276800 | tf_op jit(solution)/shard_map/pallas_call | solution.py:275
  79.0 0.0 collective-permute-done.3.refs_1_
  79.0 2.7 %shard_map.107.refs_2_ = bf16[25,32,2048]{2,1,0:T(8,128)(2,1)} custom-call(s32[3,8]{1,0:T(4,128)S(1)} %get-tuple-element.24.lists, s32[2]{0:T(128)S(1)} %pad_add_fusion.place, bf16[25,32,2048]{2,1,0:T(8,128)(2,1)S(1)} %bitcast.12, bf16[4,2,768,256]{3,2,1,0:T(8,128)(2,1)S(1)} %get-tuple-element.33.p_ref, ...), custom_call_target="tpu_custom_call", output_to_operand_aliasing={{}: (7, {})} | custom-call | flops 629145600 | bytes 3276800 | tf_op jit(solution)/shard_map/pallas_call | solution.py:275
  81.6 2.7 %shard_map.108 = bf16[25,32,2048]{2,1,0:T(8,128)(2,1)} custom-call(s32[3,8]{1,0:T(4,128)S(1)} %get-tuple-element.24.lists, s32[2]{0:T(128)S(1)} %pad_add_fusion.place, bf16[25,32,2048]{2,1,0:T(8,128)(2,1)S(1)} %bitcast.13, bf16[4,2,768,256]{3,2,1,0:T(8,128)(2,1)S(1)} %get-tuple-element.33.p_ref, ...), custom_call_target="tpu_custom_call", output_to_operand_aliasing={{}: (7, {})} | custom-call | flops 629145600 | bytes 3276800 | tf_op jit(solution)/shard_map/pallas_call | solution.py:275
  84.3 0.7 finish.1
  (12 shorter events, 0.1 us)
Async XLA Ops:
  3.1 22.0 %copy-start.1 = (f32[3,2048]{1,0:T(4,128)S(1)}, f32[3,2048]{1,0:T(4,128)}, u32[]{:S(2)}) copy-start(f32[3,2048]{1,0:T(4,128)} %f_ref.1) | copy-start | bytes 73732
  3.1 10.9 %collective-permute-start = (bf16[64,512]{1,0:T(8,128)(2,1)S(1)}, bf16[64,512]{1,0:T(8,128)(2,1)S(1)}, u32[]{:S(2)}, u32[]{:S(2)}) collective-permute-start(bf16[64,512]{1,0:T(8,128)(2,1)S(1)} %get-tuple-element.30), channel_id=1, source_target_pairs={{4,8},{8,4},{12,16},{16,12},{20,24},{24,20},{5,9},{9,5},{13,17},{1... | collective-permute-start | bytes 196616 | tf_op jit(solution)/shard_map/ppermute | solution.py:521
  3.7 10.2 %collective-permute-start.1 = (bf16[64,512]{1,0:T(8,128)(2,1)S(1)}, bf16[64,512]{1,0:T(8,128)(2,1)S(1)}, u32[]{:S(2)}, u32[]{:S(2)}) collective-permute-start(bf16[64,512]{1,0:T(8,128)(2,1)S(1)} %get-tuple-element.31), channel_id=1, source_target_pairs={{0,4},{4,0},{8,12},{12,8},{16,20},{20,16},{24,28},{28,24},{1,5},{5... | collective-permute-start | bytes 196616 | tf_op jit(solution)/shard_map/ppermute | solution.py:521
  18.5 1.4 %collective-permute-start.4 = (f32[16,2048]{1,0:T(8,128)S(1)}, f32[16,2048]{1,0:T(8,128)S(1)}, u32[]{:S(2)}, u32[]{:S(2)}) collective-permute-start(f32[16,2048]{1,0:T(8,128)S(1)} %get-tuple-element.39), channel_id=1, source_target_pairs={{0,1},{1,0},{2,3},{3,2},{4,5},{5,4},{6,7},{7,6},{8,9},{9,8},{10,11... | collective-permute-start | bytes 393224 | tf_op jit(solution)/shard_map/ppermute | solution.py:487
  18.6 60.4 %collective-permute-start.3 = (bf16[24,32,512]{2,1,0:T(8,128)(2,1)S(1)}, bf16[24,32,512]{2,1,0:T(8,128)(2,1)S(1)}, u32[]{:S(2)}, u32[]{:S(2)}) collective-permute-start(bf16[24,32,512]{2,1,0:T(8,128)(2,1)S(1)} %get-tuple-element.36), channel_id=1, source_target_pairs={{4,8},{8,4},{12,16},{16,12},{20,24},{24,20},{5,9},{9,5},{13,17},{1... | collective-permute-start | bytes 2359304 | tf_op jit(solution)/shard_map/ppermute | solution.py:521
  19.9 8.0 %collective-permute-start.5 = (f32[16,2048]{1,0:T(8,128)S(1)}, f32[16,2048]{1,0:T(8,128)S(1)}, u32[]{:S(2)}, u32[]{:S(2)}) collective-permute-start(f32[16,2048]{1,0:T(8,128)S(1)} %add.18), channel_id=1, source_target_pairs={{0,2},{1,3},{2,0},{3,1},{4,6},{5,7},{6,4},{7,5},{8,10},{9,11},{10,... | collective-permute-start | bytes 393224 | tf_op jit(solution)/shard_map/ppermute | solution.py:487
  21.5 60.2 %collective-permute-start.2 = (bf16[24,32,512]{2,1,0:T(8,128)(2,1)S(1)}, bf16[24,32,512]{2,1,0:T(8,128)(2,1)S(1)}, u32[]{:S(2)}, u32[]{:S(2)}) collective-permute-start(bf16[24,32,512]{2,1,0:T(8,128)(2,1)S(1)} %get-tuple-element.35), channel_id=1, source_target_pairs={{0,4},{4,0},{8,12},{12,8},{16,20},{20,16},{24,28},{28,24},{1,5},{5... | collective-permute-start | bytes 2359304 | tf_op jit(solution)/shard_map/ppermute | solution.py:521
  29.3 45.0 %copy-start = (bf16[32,25,2048]{2,0,1:T(8,128)(2,1)S(1)}, bf16[32,25,2048]{2,0,1:T(8,128)(2,1)}, u32[]{:S(2)}) copy-start(bf16[32,25,2048]{2,0,1:T(8,128)(2,1)} %param.10) | copy-start | bytes 9830404
  29.3 28.1 %collective-permute-start.6 = (f32[16,960]{1,0:T(8,128)S(1)}, f32[16,960]{1,0:T(8,128)S(1)}, u32[]{:S(2)}, u32[]{:S(2)}) collective-permute-start(f32[16,960]{1,0:T(8,128)S(1)} %structure.1), channel_id=1, source_target_pairs={{0,4},{4,0},{8,12},{12,8},{16,20},{20,16},{24,28},{28,24},{1,5},{5... | collective-permute-start | bytes 184328 | tf_op jit(solution)/shard_map/ppermute | solution.py:487
  57.5 6.0 %collective-permute-start.7 = (f32[16,960]{1,0:T(8,128)S(1)}, f32[16,960]{1,0:T(8,128)S(1)}, u32[]{:S(2)}, u32[]{:S(2)}) collective-permute-start(f32[16,960]{1,0:T(8,128)S(1)} %add.20), channel_id=1, source_target_pairs={{0,8},{4,12},{8,0},{12,4},{16,24},{20,28},{24,16},{28,20},{1,9},{5... | collective-permute-start | bytes 184328 | tf_op jit(solution)/shard_map/ppermute | solution.py:487
  63.5 5.3 %collective-permute-start.8 = (f32[16,960]{1,0:T(8,128)S(1)}, f32[16,960]{1,0:T(8,128)S(1)}, u32[]{:S(2)}, u32[]{:S(2)}) collective-permute-start(f32[16,960]{1,0:T(8,128)S(1)} %add.21), channel_id=1, source_target_pairs={{0,16},{4,20},{8,24},{12,28},{16,0},{20,4},{24,8},{28,12},{1,17},{... | collective-permute-start | bytes 184328 | tf_op jit(solution)/shard_map/ppermute | solution.py:487
  71.2 1.5 %collective-permute-start.9 = (f32[24,2048]{1,0:T(8,128)S(1)}, f32[24,2048]{1,0:T(8,128)S(1)}, u32[]{:S(2)}, u32[]{:S(2)}) collective-permute-start(f32[24,2048]{1,0:T(8,128)S(1)} %fields.1), channel_id=1, source_target_pairs={{0,1},{1,0},{2,3},{3,2},{4,5},{5,4},{6,7},{7,6},{8,9},{9,8},{10,11... | collective-permute-start | bytes 589832 | tf_op jit(solution)/shard_map/ppermute | solution.py:487
  72.8 11.5 %collective-permute-start.10 = (f32[24,2048]{1,0:T(8,128)S(1)}, f32[24,2048]{1,0:T(8,128)S(1)}, u32[]{:S(2)}, u32[]{:S(2)}) collective-permute-start(f32[24,2048]{1,0:T(8,128)S(1)} %add.23.mine_ref), channel_id=1, source_target_pairs={{0,2},{1,3},{2,0},{3,1},{4,6},{5,7},{6,4},{7,5},{8,10},{9,11},{10,... | collective-permute-start | bytes 589832 | tf_op jit(solution)/shard_map/ppermute | solution.py:547

commit v4 on v3

--- a/solution.py
+++ b/solution.py
@@ -111,61 +111,74 @@
 def score_kernel(heads, head_dim, head_chan, blocks, part, lists, counts, place, *refs):
     q_ref, k_ref, v_ref, cw_ref = refs[:4]
     sides, (p_ref, scale_ref, charge_ref, kaug, v0) = refs[4:-5], refs[-5:]
-    i = pl.program_id(0)
     first = place[0] * blocks
     total = counts.shape[0]
-
-    @pl.when(i == 0)
-    def _():
-        lane = lax.broadcasted_iota(jnp.int32, (16, BS), 1)
-        row = lax.broadcasted_iota(jnp.int32, (16, BS), 0)
-
-        def fill(b, keys, values):
-            index = first + b - REACH
-            inside = (index >= 0) & (index < total)
-            live = jnp.where(inside, counts[jnp.clip(index, 0, total - 1)], 0)
-            bias = jnp.where((row == 0) & (lane >= live), -1e30, 0.0).astype(BF)
-            v0[b] = values
-            for h in range(heads):
-                for copy in range(3):
-                    kaug[b, h, copy * head_dim : (copy + 1) * head_dim, :] = keys[h * head_dim : (h + 1) * head_dim]
-                kaug[b, h, 3 * head_dim : 3 * head_dim + 16, :] = bias
-
-        for b in range(blocks):
-            cols = slice(b * BS, (b + 1) * BS)
-            fill(b + REACH, k_ref[:, cols], v_ref[:, cols])
+    lane = lax.broadcasted_iota(jnp.int32, (16, BS), 1)
+    row = lax.broadcasted_iota(jnp.int32, (16, BS), 0)
+    top_row = jnp.where(row == 0, 1.0, 0.0).astype(BF)
+
+    def fill(b, keys, values):
+        index = first + b - REACH
+        inside = (index >= 0) & (index < total)
+        live = jnp.where(inside, counts[jnp.clip(index, 0, total - 1)], 0)
+        bias = jnp.where((row == 0) & (lane >= live), -1e30, 0.0).astype(BF)
+        for h in range(heads):
+            for copy in range(3):
+                kaug[b, h, copy * head_dim : (copy + 1) * head_dim, :] = keys[h * head_dim : (h + 1) * head_dim]
+            kaug[b, h, 3 * head_dim : 3 * head_dim + 16, :] = bias
+            v0[b, h, 0:head_chan] = values[h * head_chan : (h + 1) * head_chan]
+            v0[b, h, head_chan : head_chan + 16] = top_row
+
+    for b in range(blocks):
+        cols = slice(b * BS, (b + 1) * BS)
+        fill(b + REACH, k_ref[:, cols], v_ref[:, cols])
+    if sides:
         for far, side in zip((True, False), sides[:2]):
             base = jnp.where(on_left(place, far), 0, blocks + REACH)
             for b in range(REACH):
                 cols = slice(b * BS, (b + 1) * BS)
                 fill(base + b, side[0 : heads * head_dim, cols], side[heads * head_dim :, cols])
-
-    g = i + REACH if part == "interior" else edge_block(i, place, blocks)
-    own_count = counts[first + g]
-    live_q = lax.broadcasted_iota(jnp.int32, (1, BS), 1) < own_count
-    top_row = jnp.where(lax.broadcasted_iota(jnp.int32, (16, BS), 0) == 0, 1.0, 0.0).astype(BF)
-    listed = [lists[e, g] - (first - REACH) for e in range(NNB)]
-    scores = []
-    for h in range(heads):
-        q = q_ref[h * head_dim : (h + 1) * head_dim, :].astype(F32) * (head_dim ** (-0.5) * LOG2E)
+        inner = slice(REACH * BS, (blocks - REACH) * BS)
+        charge_ref[:, inner] = sides[2][:, inner]
+    else:
+        charge_ref[...] = jnp.zeros_like(charge_ref)
+
+    def block_of(i):
+        return i + REACH if part == "interior" else edge_block(i, place, blocks)
+
+    def columns(g):
+        return pl.ds(pl.multiple_of(g * BS, BS), BS)
+
+    def scores_of(i, h):
+        g = block_of(i)
+        listed = [lists[e, g] - (first - REACH) for e in range(NNB)]
+        q = q_ref[h * head_dim : (h + 1) * head_dim, columns(g)].astype(F32) * (head_dim ** (-0.5) * LOG2E)
         qa = jnp.concatenate([*thirds(q), top_row], axis=0)
-        scores.append([dot(kaug[b, h], qa, ((0,), (0,))) for b in listed])
+        return listed, [dot(kaug[b, h], qa, ((0,), (0,))) for b in listed]
+
+    steps = p_ref.shape[0]
+    pairs = [(i, h) for i in range(steps) for h in range(heads)]
+    coming = scores_of(*pairs[0])
     charge = None
-    for h in range(heads):
-        top = functools.reduce(jnp.maximum, [jnp.max(s, axis=0, keepdims=True) for s in scores[h]])
+    for at, (i, h) in enumerate(pairs):
+        listed, scores = coming
+        if at + 1 < len(pairs):
+            coming = scores_of(*pairs[at + 1])
+        g = block_of(i)
+        top = functools.reduce(jnp.maximum, [jnp.max(s, axis=0, keepdims=True) for s in scores])
         mixed = 0.0
         for e, b in enumerate(listed):
-            w16 = jnp.exp2(scores[h][e] - top).astype(BF)
+            w16 = jnp.exp2(scores[e] - top).astype(BF)
             p_ref[i, h, e * BS : (e + 1) * BS, :] = w16
-            v = jnp.concatenate([v0[b, h * head_chan : (h + 1) * head_chan, :], top_row], axis=0)
-            mixed = mixed + dot(v, w16, ((1,), (0,)))
-        denominator = mixed[head_chan : head_chan + 1]
-        scale = jnp.where(live_q, 1.0 / denominator, 0.0)
+            mixed = mixed + dot(v0[b, h], w16, ((1,), (0,)))
+        live_q = lane[0:1] < counts[first + g]
+        scale = jnp.where(live_q, 1.0 / mixed[head_chan : head_chan + 1], 0.0)
         scale_ref[i, h : h + 1, :] = scale
         att0 = (mixed[:head_chan] * scale).astype(BF)
         term = dot(cw_ref[:, h * head_chan : (h + 1) * head_chan], att0, ((1,), (0,)))
-        charge = term if charge is None else charge + term
-    charge_ref[...] = charge
+        charge = term if h == 0 else charge + term
+        if h == heads - 1:
+            charge_ref[:, columns(g)] = charge
 
 
 def scores_call(part, lists, counts, place, q, k, v0, cw, sides, heads, head_dim):
@@ -175,41 +188,22 @@
     head_chan = chans // heads
     band = blocks + 2 * REACH
     steps = blocks - 2 * REACH if part == "interior" else 2 * REACH
-
-    def at(i, lists, counts, place):
-        return i + REACH if part == "interior" else edge_block(i, place, blocks)
-
     whole = lambda shape: pl.BlockSpec(shape, lambda g, *_: (0,) * len(shape), pipeline_mode=pl.Buffered(1))
-    any_space = pl.BlockSpec(memory_space=pl.ANY)
+    shapes = [((steps, heads, NNB * BS, BS), BF), ((steps, heads, BS), F32), ((nq, atoms), F32)]
     return pl.pallas_call(
         functools.partial(score_kernel, heads, head_dim, head_chan, blocks, part),
         grid_spec=pltpu.PrefetchScalarGridSpec(
             num_scalar_prefetch=3,
-            grid=(steps,),
-            in_specs=[
-                pl.BlockSpec((heads * head_dim, BS), lambda i, *s: (0, at(i, *s))),
-                whole(k.shape),
-                whole(v0.shape),
-                whole(cw.shape),
-            ]
-            + [whole(s.shape) for s in sides[:2]] + [any_space] * len(sides[2:]),
-            out_specs=[
-                whole((steps, heads, NNB * BS, BS)),
-                whole((steps, heads, BS)),
-                pl.BlockSpec((nq, BS), lambda i, *s: (0, at(i, *s))),
-            ],
+            grid=(1,),
+            in_specs=[whole(x.shape) for x in (q, k, v0, cw, *sides)],
+            out_specs=[whole(shape) for shape, _ in shapes],
             scratch_shapes=[
                 pltpu.VMEM((band, heads, 3 * head_dim + 16, BS), BF),
-                pltpu.VMEM((band, chans, BS), BF),
+                pltpu.VMEM((band, heads, head_chan + 16, BS), BF),
             ],
         ),
-        out_shape=[
-            jax.ShapeDtypeStruct((steps, heads, NNB * BS, BS), BF),
-            jax.ShapeDtypeStruct((steps, heads, BS), F32),
-            jax.ShapeDtypeStruct((nq, atoms), F32),
-        ],
-        input_output_aliases={9: 2} if sides else {},
-        compiler_params=params(10),
+        out_shape=[jax.ShapeDtypeStruct(*x) for x in shapes],
+        compiler_params=params(16),
         cost_estimate=pl.CostEstimate(
             flops=steps * heads * NNB * BS * BS * 200, transcendentals=steps * heads * NNB * BS * BS,
             bytes_accessed=steps * heads * NNB * BS * BS * 2,

time: 85.2 us -> 83.4 us (0.979)
  Pallas kernels: 28.6 us -> 26.8 us
    pallas_call x2, Pallas kernels: 8.94 us -> 7.11 us  [scores_call(): pl.pallas_call(functools.partial(score_kernel, heads, head_dim, head_chan...]
  transfers between devices with their start and end apart: 11 -> 11, of which waited for: 5 -> 5; matrix products, arithmetic and copies ran while one was open for 0% -> 0% of each run, Pallas kernels for 25% -> 24%
where the time goes in v4:
time: 83.4 us; the launch traced here: 83.2 us
  waiting for transfers between devices  34 us (41%)
  Pallas kernels  26.8 us (32%)
  starting transfers between devices  21.5 us (26%)
    ppermute x6, waiting for transfers between devices, exchanged(): return x + lax.ppermute(x, axis, [(i, i ^ step) for i in range(size)])  34 us
    ppermute x4, starting transfers between devices, swap(): return lax.ppermute(x, 'seq', pairs)  10.8 us
    pallas_call x4, Pallas kernels, mix_call(): pl.pallas_call(functools.partial(mix_kernel, heads, head_dim, chans // he...  10 us
    ppermute x6, starting transfers between devices, exchanged(): return x + lax.ppermute(x, axis, [(i, i ^ step) for i in range(size)])  9.18 us
    pallas_call x2, Pallas kernels, scores_call(): pl.pallas_call(functools.partial(score_kernel, heads, head_dim, head_chan...  7.11 us
    pallas_call x1, Pallas kernels, table_call(): pl.pallas_call(functools.partial(table_kernel, planes), grid_spec=pltpu.P...  2.8 us
    pallas_call x1, Pallas kernels, field_call(): pl.pallas_call(functools.partial(field_kernel, planes), grid_spec=pltpu.P...  2.45 us
    pallas_call x1, Pallas kernels, load_call(): pl.pallas_call(functools.partial(load_kernel, chans, rows, width), grid_s...  2.34 us
  transfers between devices with their start and end apart: 11, of which 5 were waited for; matrix products, arithmetic and copies ran while one was open for 0% of the time, Pallas kernels for 24%

profile of v4, /device:TPU:0, one launch (start us, length us, event | category | flops | bytes accessed | tf_op | source)
XLA Modules:
  0.0 83.2 jit_solution(8559065264755637425)
XLA Ops:
  0.6 0.1 pad_add_fusion.place
  0.7 2.3 %load.1 = (bf16[64,512]{1,0:T(8,128)(2,1)S(1)}, bf16[64,512]{1,0:T(8,128)(2,1)S(1)}, bf16[24,32,512]{2,1,0:T(8,128)(2,1)S(1)}, bf16[24,32,512]{2,1,0:T(8,128)(2,...) custom-call(s32[2]{0:T(128)S(1)} %pad_add_fusion.place, ...), custom_call_target="tpu_custom_call" | custom-call | bytes 1638400 | tf_op jit(solution)/shard_map/load/pallas_call | solution.py:85
  3.1 0.0 copy-start.1
  3.1 0.7 collective-permute-start
  3.7 5.8 %collective-permute-start.1 = (bf16[64,512]{1,0:T(8,128)(2,1)S(1)}, bf16[64,512]{1,0:T(8,128)(2,1)S(1)}, u32[]{:S(2)}, u32[]{:S(2)}) collective-permute-start(bf16[64,512]{1,0:T(8,128)(2,1)S(1)} %get-tuple-element.31), channel_id=1, source_target_pairs={{0,4},{4,0},{8,12},{12,8},{16,20},{20,16},{24,28},{28,24},{1,5},{5... | collective-permute-start | bytes 196616 | tf_op jit(solution)/shard_map/ppermute | solution.py:515
  9.6 3.5 %shard_map.103 = (bf16[4,2,768,256]{3,2,1,0:T(8,128)(2,1)S(1)}, f32[4,2,256]{2,1,0:T(2,128)S(1)}, f32[16,2048]{1,0:T(8,128)S(1)}) custom-call(s32[3,8]{1,0:T(4,128)S(1)} %get-tuple-element.24.lists, s32[64]{0:T(128)S(1)} %get-tuple-element.25.counts, s32[2]{0:T(128)S(1)} %pad_add_fusion.place, bf16[32,2048]{1,0:T(8,128)(2,1)S(1)} %get-tuple-element.26.refs_0_, ...), custom_call_target="tpu_custom_call" | custom-call | flops 314572800 | bytes 3145728 | tf_op jit(solution)/shard_map/pallas_call | solution.py:193
  13.1 3.6 %shard_map.104 = (bf16[4,2,768,256]{3,2,1,0:T(8,128)(2,1)S(1)}, f32[4,2,256]{2,1,0:T(2,128)S(1)}, f32[16,2048]{1,0:T(8,128)S(1)}) custom-call(s32[3,8]{1,0:T(4,128)S(1)} %get-tuple-element.24.lists, s32[64]{0:T(128)S(1)} %get-tuple-element.25.counts, s32[2]{0:T(128)S(1)} %pad_add_fusion.place, bf16[32,2048]{1,0:T(8,128)(2,1)S(1)} %get-tuple-element.26.refs_0_, ...), custom_call_target="tpu_custom_call" | custom-call | flops 314572800 | bytes 3145728 | tf_op jit(solution)/shard_map/pallas_call | solution.py:193
  16.7 0.0 collective-permute-start.4
  16.7 0.7 collective-permute-start.3
  17.4 0.6 collective-permute-done.4
  18.1 1.6 %collective-permute-start.5 = (f32[16,2048]{1,0:T(8,128)S(1)}, f32[16,2048]{1,0:T(8,128)S(1)}, u32[]{:S(2)}, u32[]{:S(2)}) collective-permute-start(f32[16,2048]{1,0:T(8,128)S(1)} %add.18), channel_id=1, source_target_pairs={{0,2},{1,3},{2,0},{3,1},{4,6},{5,7},{6,4},{7,5},{8,10},{9,11},{10,... | collective-permute-start | bytes 393224 | tf_op jit(solution)/shard_map/ppermute | solution.py:481
  19.6 3.6 %collective-permute-start.2 = (bf16[24,32,512]{2,1,0:T(8,128)(2,1)S(1)}, bf16[24,32,512]{2,1,0:T(8,128)(2,1)S(1)}, u32[]{:S(2)}, u32[]{:S(2)}) collective-permute-start(bf16[24,32,512]{2,1,0:T(8,128)(2,1)S(1)} %get-tuple-element.35), channel_id=1, source_target_pairs={{0,4},{4,0},{8,12},{12,8},{16,20},{20,16},{24,28},{28,24},{1,5},{5... | collective-permute-start | bytes 2359304 | tf_op jit(solution)/shard_map/ppermute | solution.py:515
  23.2 2.8 %table.1 = (bf16[2,480,2048]{2,1,0:T(8,128)(2,1)S(1)}, f32[1,480]{1,0:T(1,128)S(1)}) custom-call(s32[2]{0:T(128)S(1)} %pad_add_fusion.place, s32[3,2048]{1,0:T(4,128)S(1)} %get-tuple-element.40.n_ref, f32[3,2048]{1,0:T(4,128)S(1)} %copy-done.1), custom_call_target="tpu_custom_call" | custom-call | flops 39321600 | bytes 3932160 | tf_op jit(solution)/shard_map/table/pallas_call | solution.py:364
  26.0 0.0 collective-permute-done.5
  26.1 1.4 %structure.1 = f32[16,960]{1,0:T(8,128)S(1)} custom-call(f32[16,2048]{1,0:T(8,128)S(1)} %add.19.c_ref, bf16[960,2048]{1,0:T(8,128)(2,1)S(1)} %bitcast.14), custom_call_target="tpu_custom_call" | custom-call | flops 1006632960 | bytes 3932160 | tf_op jit(solution)/shard_map/structure/pallas_call | solution.py:398
  27.5 1.4 %collective-permute-start.6 = (f32[16,960]{1,0:T(8,128)S(1)}, f32[16,960]{1,0:T(8,128)S(1)}, u32[]{:S(2)}, u32[]{:S(2)}) collective-permute-start(f32[16,960]{1,0:T(8,128)S(1)} %structure.1), channel_id=1, source_target_pairs={{0,4},{4,0},{8,12},{12,8},{16,20},{20,16},{24,28},{28,24},{1,5},{5... | collective-permute-start | bytes 184328 | tf_op jit(solution)/shard_map/ppermute | solution.py:481
  28.8 27.3 %collective-permute-done.6 = f32[16,960]{1,0:T(8,128)S(1)} collective-permute-done((f32[16,960]{1,0:T(8,128)S(1)}, f32[16,960]{1,0:T(8,128)S(1)}, u32[]{:S(2)}, u32[]{:S(2)}) %collective-permute-start.6) | collective-permute-done | bytes 61472 | tf_op jit(solution)/shard_map/ppermute | solution.py:481
  56.2 3.2 %collective-permute-start.7 = (f32[16,960]{1,0:T(8,128)S(1)}, f32[16,960]{1,0:T(8,128)S(1)}, u32[]{:S(2)}, u32[]{:S(2)}) collective-permute-start(f32[16,960]{1,0:T(8,128)S(1)} %add.20), channel_id=1, source_target_pairs={{0,8},{4,12},{8,0},{12,4},{16,24},{20,28},{24,16},{28,20},{1,9},{5... | collective-permute-start | bytes 184328 | tf_op jit(solution)/shard_map/ppermute | solution.py:481
  59.4 2.3 %collective-permute-done.7 = f32[16,960]{1,0:T(8,128)S(1)} collective-permute-done((f32[16,960]{1,0:T(8,128)S(1)}, f32[16,960]{1,0:T(8,128)S(1)}, u32[]{:S(2)}, u32[]{:S(2)}) %collective-permute-start.7) | collective-permute-done | bytes 61472 | tf_op jit(solution)/shard_map/ppermute | solution.py:481
  61.7 3.0 %collective-permute-start.8 = (f32[16,960]{1,0:T(8,128)S(1)}, f32[16,960]{1,0:T(8,128)S(1)}, u32[]{:S(2)}, u32[]{:S(2)}) collective-permute-start(f32[16,960]{1,0:T(8,128)S(1)} %add.21), channel_id=1, source_target_pairs={{0,16},{4,20},{8,24},{12,28},{16,0},{20,4},{24,8},{28,12},{1,17},{... | collective-permute-start | bytes 184328 | tf_op jit(solution)/shard_map/ppermute | solution.py:481
  64.7 2.2 %collective-permute-done.8 = f32[16,960]{1,0:T(8,128)S(1)} collective-permute-done((f32[16,960]{1,0:T(8,128)S(1)}, f32[16,960]{1,0:T(8,128)S(1)}, u32[]{:S(2)}, u32[]{:S(2)}) %collective-permute-start.8) | collective-permute-done | bytes 61472 | tf_op jit(solution)/shard_map/ppermute | solution.py:481
  67.0 2.4 %fields.1 = f32[24,2048]{1,0:T(8,128)S(1)} custom-call(s32[2]{0:T(128)S(1)} %pad_add_fusion.place, f32[16,960]{1,0:T(8,128)S(1)} %add.22.s_ref, f32[1,480]{1,0:T(1,128)S(1)} %get-tuple-element.42.weight_ref, f32[16,2048]{1,0:T(8,128)S(1)} %add.19.c_ref, bf16[2,480,2048]{2,1,0:T(8,128)(2,1)S(1)} %get-tuple-element.41.t_ref), custom_call_target="tpu_custom_call" | custom-call | flops 503316480 | bytes 1966080 | tf_op jit(solution)/shard_map/fields/pallas_call | solution.py:440
  69.4 0.1 collective-permute-start.9
  69.5 1.4 %collective-permute-done.9 = f32[24,2048]{1,0:T(8,128)S(1)} collective-permute-done((f32[24,2048]{1,0:T(8,128)S(1)}, f32[24,2048]{1,0:T(8,128)S(1)}, u32[]{:S(2)}, u32[]{:S(2)}) %collective-permute-start.9) | collective-permute-done | bytes 196640 | tf_op jit(solution)/shard_map/ppermute | solution.py:481
  71.0 1.5 %collective-permute-start.10 = (f32[24,2048]{1,0:T(8,128)S(1)}, f32[24,2048]{1,0:T(8,128)S(1)}, u32[]{:S(2)}, u32[]{:S(2)}) collective-permute-start(f32[24,2048]{1,0:T(8,128)S(1)} %add.23.mine_ref), channel_id=1, source_target_pairs={{0,2},{1,3},{2,0},{3,1},{4,6},{5,7},{6,4},{7,5},{8,10},{9,11},{10,... | collective-permute-start | bytes 589832 | tf_op jit(solution)/shard_map/ppermute | solution.py:541
  72.5 2.3 %shard_map.105.refs_0_ = bf16[25,32,2048]{2,1,0:T(8,128)(2,1)} custom-call(s32[3,8]{1,0:T(4,128)S(1)} %get-tuple-element.24.lists, s32[2]{0:T(128)S(1)} %pad_add_fusion.place, bf16[25,32,2048]{2,1,0:T(8,128)(2,1)S(1)} %bitcast.10, bf16[4,2,768,256]{3,2,1,0:T(8,128)(2,1)S(1)} %get-tuple-element.37.p_ref, f32[4,2,256]{2,1,0:T(2,128)S(1)} %get-tuple-element.38.scale_ref), custom_call_target="tpu_custom_call" | custom-call | flops 629145600 | bytes 3276800 | tf_op jit(solution)/shard_map/pallas_call | solution.py:269
  74.8 2.3 %shard_map.106.refs_2_ = bf16[25,32,2048]{2,1,0:T(8,128)(2,1)} custom-call(s32[3,8]{1,0:T(4,128)S(1)} %get-tuple-element.24.lists, s32[2]{0:T(128)S(1)} %pad_add_fusion.place, bf16[25,32,2048]{2,1,0:T(8,128)(2,1)S(1)} %bitcast.11, bf16[4,2,768,256]{3,2,1,0:T(8,128)(2,1)S(1)} %get-tuple-element.37.p_ref, ...), custom_call_target="tpu_custom_call", output_to_operand_aliasing={{}: (5, {})} | custom-call | flops 629145600 | bytes 3276800 | tf_op jit(solution)/shard_map/pallas_call | solution.py:269
  77.2 2.7 %shard_map.107.refs_2_ = bf16[25,32,2048]{2,1,0:T(8,128)(2,1)} custom-call(s32[3,8]{1,0:T(4,128)S(1)} %get-tuple-element.24.lists, s32[2]{0:T(128)S(1)} %pad_add_fusion.place, bf16[25,32,2048]{2,1,0:T(8,128)(2,1)S(1)} %bitcast.12, bf16[4,2,768,256]{3,2,1,0:T(8,128)(2,1)S(1)} %get-tuple-element.33.p_ref, ...), custom_call_target="tpu_custom_call", output_to_operand_aliasing={{}: (7, {})} | custom-call | flops 629145600 | bytes 3276800 | tf_op jit(solution)/shard_map/pallas_call | solution.py:269
  79.8 0.0 collective-permute-done.2.refs_1_
  79.8 2.7 %shard_map.108 = bf16[25,32,2048]{2,1,0:T(8,128)(2,1)} custom-call(s32[3,8]{1,0:T(4,128)S(1)} %get-tuple-element.24.lists, s32[2]{0:T(128)S(1)} %pad_add_fusion.place, bf16[25,32,2048]{2,1,0:T(8,128)(2,1)S(1)} %bitcast.13, bf16[4,2,768,256]{3,2,1,0:T(8,128)(2,1)S(1)} %get-tuple-element.33.p_ref, ...), custom_call_target="tpu_custom_call", output_to_operand_aliasing={{}: (7, {})} | custom-call | flops 629145600 | bytes 3276800 | tf_op jit(solution)/shard_map/pallas_call | solution.py:269
  82.5 0.0 collective-permute-done.10.theirs_ref
  82.5 0.7 finish.1
  (12 shorter events, 0.1 us)
Async XLA Ops:
  3.1 20.2 %copy-start.1 = (f32[3,2048]{1,0:T(4,128)S(1)}, f32[3,2048]{1,0:T(4,128)}, u32[]{:S(2)}) copy-start(f32[3,2048]{1,0:T(4,128)} %f_ref.1) | copy-start | bytes 73732
  3.1 10.0 %collective-permute-start = (bf16[64,512]{1,0:T(8,128)(2,1)S(1)}, bf16[64,512]{1,0:T(8,128)(2,1)S(1)}, u32[]{:S(2)}, u32[]{:S(2)}) collective-permute-start(bf16[64,512]{1,0:T(8,128)(2,1)S(1)} %get-tuple-element.30), channel_id=1, source_target_pairs={{4,8},{8,4},{12,16},{16,12},{20,24},{24,20},{5,9},{9,5},{13,17},{1... | collective-permute-start | bytes 196616 | tf_op jit(solution)/shard_map/ppermute | solution.py:515
  3.7 9.4 %collective-permute-start.1 = (bf16[64,512]{1,0:T(8,128)(2,1)S(1)}, bf16[64,512]{1,0:T(8,128)(2,1)S(1)}, u32[]{:S(2)}, u32[]{:S(2)}) collective-permute-start(bf16[64,512]{1,0:T(8,128)(2,1)S(1)} %get-tuple-element.31), channel_id=1, source_target_pairs={{0,4},{4,0},{8,12},{12,8},{16,20},{20,16},{24,28},{28,24},{1,5},{5... | collective-permute-start | bytes 196616 | tf_op jit(solution)/shard_map/ppermute | solution.py:515
  16.7 1.4 %collective-permute-start.4 = (f32[16,2048]{1,0:T(8,128)S(1)}, f32[16,2048]{1,0:T(8,128)S(1)}, u32[]{:S(2)}, u32[]{:S(2)}) collective-permute-start(f32[16,2048]{1,0:T(8,128)S(1)} %get-tuple-element.39), channel_id=1, source_target_pairs={{0,1},{1,0},{2,3},{3,2},{4,5},{5,4},{6,7},{7,6},{8,9},{9,8},{10,11... | collective-permute-start | bytes 393224 | tf_op jit(solution)/shard_map/ppermute | solution.py:481
  16.7 60.5 %collective-permute-start.3 = (bf16[24,32,512]{2,1,0:T(8,128)(2,1)S(1)}, bf16[24,32,512]{2,1,0:T(8,128)(2,1)S(1)}, u32[]{:S(2)}, u32[]{:S(2)}) collective-permute-start(bf16[24,32,512]{2,1,0:T(8,128)(2,1)S(1)} %get-tuple-element.36), channel_id=1, source_target_pairs={{4,8},{8,4},{12,16},{16,12},{20,24},{24,20},{5,9},{9,5},{13,17},{1... | collective-permute-start | bytes 2359304 | tf_op jit(solution)/shard_map/ppermute | solution.py:515
  18.1 8.0 %collective-permute-start.5 = (f32[16,2048]{1,0:T(8,128)S(1)}, f32[16,2048]{1,0:T(8,128)S(1)}, u32[]{:S(2)}, u32[]{:S(2)}) collective-permute-start(f32[16,2048]{1,0:T(8,128)S(1)} %add.18), channel_id=1, source_target_pairs={{0,2},{1,3},{2,0},{3,1},{4,6},{5,7},{6,4},{7,5},{8,10},{9,11},{10,... | collective-permute-start | bytes 393224 | tf_op jit(solution)/shard_map/ppermute | solution.py:481
  19.6 60.2 %collective-permute-start.2 = (bf16[24,32,512]{2,1,0:T(8,128)(2,1)S(1)}, bf16[24,32,512]{2,1,0:T(8,128)(2,1)S(1)}, u32[]{:S(2)}, u32[]{:S(2)}) collective-permute-start(bf16[24,32,512]{2,1,0:T(8,128)(2,1)S(1)} %get-tuple-element.35), channel_id=1, source_target_pairs={{0,4},{4,0},{8,12},{12,8},{16,20},{20,16},{24,28},{28,24},{1,5},{5... | collective-permute-start | bytes 2359304 | tf_op jit(solution)/shard_map/ppermute | solution.py:515
  27.5 45.0 %copy-start = (bf16[32,25,2048]{2,0,1:T(8,128)(2,1)S(1)}, bf16[32,25,2048]{2,0,1:T(8,128)(2,1)}, u32[]{:S(2)}) copy-start(bf16[32,25,2048]{2,0,1:T(8,128)(2,1)} %param.10) | copy-start | bytes 9830404
  27.5 28.7 %collective-permute-start.6 = (f32[16,960]{1,0:T(8,128)S(1)}, f32[16,960]{1,0:T(8,128)S(1)}, u32[]{:S(2)}, u32[]{:S(2)}) collective-permute-start(f32[16,960]{1,0:T(8,128)S(1)} %structure.1), channel_id=1, source_target_pairs={{0,4},{4,0},{8,12},{12,8},{16,20},{20,16},{24,28},{28,24},{1,5},{5... | collective-permute-start | bytes 184328 | tf_op jit(solution)/shard_map/ppermute | solution.py:481
  56.2 5.5 %collective-permute-start.7 = (f32[16,960]{1,0:T(8,128)S(1)}, f32[16,960]{1,0:T(8,128)S(1)}, u32[]{:S(2)}, u32[]{:S(2)}) collective-permute-start(f32[16,960]{1,0:T(8,128)S(1)} %add.20), channel_id=1, source_target_pairs={{0,8},{4,12},{8,0},{12,4},{16,24},{20,28},{24,16},{28,20},{1,9},{5... | collective-permute-start | bytes 184328 | tf_op jit(solution)/shard_map/ppermute | solution.py:481
  61.7 5.3 %collective-permute-start.8 = (f32[16,960]{1,0:T(8,128)S(1)}, f32[16,960]{1,0:T(8,128)S(1)}, u32[]{:S(2)}, u32[]{:S(2)}) collective-permute-start(f32[16,960]{1,0:T(8,128)S(1)} %add.21), channel_id=1, source_target_pairs={{0,16},{4,20},{8,24},{12,28},{16,0},{20,4},{24,8},{28,12},{1,17},{... | collective-permute-start | bytes 184328 | tf_op jit(solution)/shard_map/ppermute | solution.py:481
  69.4 1.5 %collective-permute-start.9 = (f32[24,2048]{1,0:T(8,128)S(1)}, f32[24,2048]{1,0:T(8,128)S(1)}, u32[]{:S(2)}, u32[]{:S(2)}) collective-permute-start(f32[24,2048]{1,0:T(8,128)S(1)} %fields.1), channel_id=1, source_target_pairs={{0,1},{1,0},{2,3},{3,2},{4,5},{5,4},{6,7},{7,6},{8,9},{9,8},{10,11... | collective-permute-start | bytes 589832 | tf_op jit(solution)/shard_map/ppermute | solution.py:481
  71.0 11.6 %collective-permute-start.10 = (f32[24,2048]{1,0:T(8,128)S(1)}, f32[24,2048]{1,0:T(8,128)S(1)}, u32[]{:S(2)}, u32[]{:S(2)}) collective-permute-start(f32[24,2048]{1,0:T(8,128)S(1)} %add.23.mine_ref), channel_id=1, source_target_pairs={{0,2},{1,3},{2,0},{3,1},{4,6},{5,7},{6,4},{7,5},{8,10},{9,11},{10,... | collective-permute-start | bytes 589832 | tf_op jit(solution)/shard_map/ppermute | solution.py:541

commit v5 on v4

--- a/solution.py
+++ b/solution.py
@@ -334,46 +334,37 @@
     return jnp.where(norm > 0, times * (ewald_scale * jnp.exp(-ewald_damp * safe) / safe), 0.0)
 
 
-def table_kernel(planes, place, n_ref, f_ref, out_ref, weight_ref, pairs):
+def table_kernel(planes, step, place, n_ref, f_ref, out_ref, weight_ref, pairs):
     base = place[1] * planes
-
-    @pl.when(pl.program_id(0) == 0)
-    def _():
-        weight_ref[...] = grid_weights(n_ref[...], base, planes)
-
-    atoms = f_ref.shape[1]
-    wide = lax.broadcasted_iota(jnp.int32, (WIDE, atoms), 0)
-    steps = (wide - KMAX).astype(F32)
-    second = wave(steps * f_ref[1:2, :])
-    third = wave(steps * f_ref[2:3, :])
-    for plane in range(planes):
-        first = wave((base + plane).astype(F32) * f_ref[0:1, :])
-        pairs[0, plane] = first[0] * second[0] - first[1] * second[1]
-        pairs[1, plane] = first[1] * second[0] + first[0] * second[1]
-        for m in range(SPREAD):
-            real, imag = pairs[0, plane, m : m + 1, :], pairs[1, plane, m : m + 1, :]
-            at = slice((plane * SPREAD + m) * WIDE, (plane * SPREAD + m + 1) * WIDE)
-            out_ref[0, at, :] = (real * third[0] - imag * third[1]).astype(BF)
-            out_ref[1, at, :] = (imag * third[0] + real * third[1]).astype(BF)
+    weight_ref[...] = grid_weights(n_ref[...], base, planes)
+    steps = (lax.broadcasted_iota(jnp.int32, (WIDE, step), 0) - KMAX).astype(F32)
+    for start in range(0, f_ref.shape[1], step):
+        cols = slice(start, start + step)
+        second = wave(steps * f_ref[1:2, cols])
+        third = wave(steps * f_ref[2:3, cols])
+        for plane in range(planes):
+            first = wave((base + plane).astype(F32) * f_ref[0:1, cols])
+            pairs[0, plane] = first[0] * second[0] - first[1] * second[1]
+            pairs[1, plane] = first[1] * second[0] + first[0] * second[1]
+            for m in range(SPREAD):
+                real, imag = pairs[0, plane, m : m + 1, :], pairs[1, plane, m : m + 1, :]
+                at = slice((plane * SPREAD + m) * WIDE, (plane * SPREAD + m + 1) * WIDE)
+                out_ref[0, at, cols] = (real * third[0] - imag * third[1]).astype(BF)
+                out_ref[1, at, cols] = (imag * third[0] + real * third[1]).astype(BF)
 
 
 def table_call(place, n, f, planes):
     rows = planes * SPREAD * WIDE
     atoms = f.shape[1]
     step = 256
-    return pl.pallas_call(
-        functools.partial(table_kernel, planes),
+    whole = lambda shape: pl.BlockSpec(shape, lambda g, *_: (0,) * len(shape), pipeline_mode=pl.Buffered(1))
+    return pl.pallas_call(
+        functools.partial(table_kernel, planes, step),
         grid_spec=pltpu.PrefetchScalarGridSpec(
             num_scalar_prefetch=1,
-            grid=(atoms // step,),
-            in_specs=[
-                pl.BlockSpec(n.shape, lambda i, place: (0, 0), pipeline_mode=pl.Buffered(1)),
-                pl.BlockSpec((3, step), lambda i, place: (0, i)),
-            ],
-            out_specs=[
-                pl.BlockSpec((2, rows, step), lambda i, place: (0, 0, i)),
-                pl.BlockSpec((1, rows), lambda i, place: (0, 0)),
-            ],
+            grid=(1,),
+            in_specs=[whole(n.shape), whole(f.shape)],
+            out_specs=[whole((2, rows, atoms)), whole((1, rows))],
             scratch_shapes=[pltpu.VMEM((2, planes, WIDE, step), F32)],
         ),
         out_shape=[jax.ShapeDtypeStruct((2, rows, atoms), BF), jax.ShapeDtypeStruct((1, rows), F32)],
@@ -407,49 +398,38 @@
     )(c, table)
 
 
-def field_kernel(planes, place, s_ref, weight_ref, c_ref, t_ref, out_ref, coeff):
+def field_kernel(planes, step, place, s_ref, weight_ref, c_ref, t_ref, out_ref):
     nq = c_ref.shape[0]
     waves = weight_ref.shape[1]
-
-    @pl.when(pl.program_id(0) == 0)
-    def _():
-        n = grid_points(place[1] * planes, planes)
-        real = s_ref[:, :waves] * weight_ref[...]
-        imag = s_ref[:, waves:] * weight_ref[...]
-        with_cos = jnp.concatenate([real] + [-imag * n[d] for d in range(3)], axis=0)
-        with_sin = jnp.concatenate([imag] + [real * n[d] for d in range(3)], axis=0)
-        for part, x in enumerate((with_cos, with_sin)):
-            high, low = halves(x)
-            coeff[part, 0 : 4 * nq] = high
-            coeff[part, 4 * nq :] = low
-
-    both = dot(coeff[0], t_ref[0], ((1,), (0,))) + dot(coeff[1], t_ref[1], ((1,), (0,)))
-    sums = both[: 4 * nq] + both[4 * nq :]
-    c = c_ref[...]
-    out_ref[0:nq, :] = sums[:nq]
-    forces = [
-        jnp.sum(c * sums[(d + 1) * nq : (d + 2) * nq], axis=0, keepdims=True) for d in range(3)
-    ]
-    out_ref[nq : nq + 8, :] = jnp.concatenate(forces + [jnp.zeros((5, c.shape[1]), F32)], axis=0)
+    n = grid_points(place[1] * planes, planes)
+    real = s_ref[:, :waves] * weight_ref[...]
+    imag = s_ref[:, waves:] * weight_ref[...]
+    with_cos = jnp.concatenate([real] + [-imag * n[d] for d in range(3)], axis=0)
+    with_sin = jnp.concatenate([imag] + [real * n[d] for d in range(3)], axis=0)
+    with_cos, with_sin = [jnp.concatenate(halves(x), axis=0) for x in (with_cos, with_sin)]
+    for start in range(0, c_ref.shape[1], step):
+        cols = slice(start, start + step)
+        both = dot(with_cos, t_ref[0, :, cols], ((1,), (0,))) + dot(with_sin, t_ref[1, :, cols], ((1,), (0,)))
+        sums = both[: 4 * nq] + both[4 * nq :]
+        c = c_ref[:, cols]
+        out_ref[0:nq, cols] = sums[:nq]
+        forces = [
+            jnp.sum(c * sums[(d + 1) * nq : (d + 2) * nq], axis=0, keepdims=True) for d in range(3)
+        ]
+        out_ref[nq : nq + 8, cols] = jnp.concatenate(forces + [jnp.zeros((5, step), F32)], axis=0)
 
 
 def field_call(place, s, weight, c, table, planes):
     _, rows, atoms = table.shape
-    step = 512
     nq = c.shape[0]
-    return pl.pallas_call(
-        functools.partial(field_kernel, planes),
+    whole = lambda shape: pl.BlockSpec(shape, lambda g, *_: (0,) * len(shape), pipeline_mode=pl.Buffered(1))
+    return pl.pallas_call(
+        functools.partial(field_kernel, planes, 512),
         grid_spec=pltpu.PrefetchScalarGridSpec(
             num_scalar_prefetch=1,
-            grid=(atoms // step,),
-            in_specs=[
-                pl.BlockSpec(s.shape, lambda i, place: (0, 0)),
-                pl.BlockSpec(weight.shape, lambda i, place: (0, 0)),
-                pl.BlockSpec((nq, step), lambda i, place: (0, i)),
-                pl.BlockSpec((2, rows, step), lambda i, place: (0, 0, i)),
-            ],
-            out_specs=pl.BlockSpec((nq + 8, step), lambda i, place: (0, i)),
-            scratch_shapes=[pltpu.VMEM((2, 8 * nq, rows), BF)],
+            grid=(1,),
+            in_specs=[whole(x.shape) for x in (s, weight, c, table)],
+            out_specs=whole((nq + 8, atoms)),
         ),
         out_shape=jax.ShapeDtypeStruct((nq + 8, atoms), F32),
         compiler_params=params(12),
@@ -460,8 +440,9 @@
 
 def finish_kernel(mine_ref, theirs_ref, potential_ref, force_ref):
     nq = potential_ref.shape[0]
-    potential_ref[...] = mine_ref[0:nq] + theirs_ref[0:nq]
-    force_ref[...] = (mine_ref[nq : nq + 8] + theirs_ref[nq : nq + 8])[:3]
+    total = mine_ref[...].astype(F32) + theirs_ref[...].astype(F32)
+    potential_ref[...] = total[:nq]
+    force_ref[...] = total[nq : nq + 3]
 
 
 def finish_call(mine, theirs, nq):
@@ -537,14 +518,14 @@
     structure = summed(structure, "seq")
     fields = field_call(place, structure, wave_weight, charges, table, planes)
     last = lax.axis_size("inner") // 2
-    fields = summed(fields, "inner", stop=last)
+    fields = summed(fields, "inner", stop=last).astype(BF)
     others = lax.ppermute(fields, "inner", [(i, i ^ last) for i in range(2 * last)])
     potential, forces = finish_call(fields, others, nq)
 
     mix = functools.partial(mix_call, heads=heads, head_dim=head_dim)
-    attention = mix("low", lists, place, values, p_in, scale_in, (), None)
+    attention = mix("far", lists, place, values, p_out, scale_out, (far, far_big), None)
+    attention = mix("low", lists, place, values, p_in, scale_in, (), attention)
     attention = mix("high", lists, place, values, p_in, scale_in, (), attention)
-    attention = mix("far", lists, place, values, p_out, scale_out, (far, far_big), attention)
     attention = mix("near", lists, place, values, p_out, scale_out, (near, near_big), attention)
     return (attention.transpose(1, 0, 2), potential, forces)
 

time: 83.4 us -> 77.8 us (0.933)
  starting transfers between devices: 21.5 us -> 16.3 us
  Pallas kernels: 26.8 us -> 25.1 us
  waiting for transfers between devices: 34 us -> 35.2 us
    ppermute x4, waiting for transfers between devices: 0.01 us -> 9.59 us  [swap(): return lax.ppermute(x, 'seq', pairs)]
    ppermute x6, waiting for transfers between devices: 34 us -> 25.6 us  [exchanged(): return x + lax.ppermute(x, axis, [(i, i ^ step) for i in range(size)])]
    ppermute x4, starting transfers between devices: 10.8 us -> 7.26 us  [swap(): return lax.ppermute(x, 'seq', pairs)]
    ppermute x6, starting transfers between devices: 9.18 us -> 7.46 us  [exchanged(): return x + lax.ppermute(x, axis, [(i, i ^ step) for i in range(size)])]
    pallas_call x2, Pallas kernels: 5.25 us -> 3.62 us  [the longest x1 2.13 us: table_call(): pl.pallas_call(functools.partial(table_kernel, planes, step), grid_spec=p...]
  transfers between devices with their start and end apart: 11 -> 11, of which waited for: 5 -> 7; matrix products, arithmetic and copies ran while one was open for 0% -> 0% of each run, Pallas kernels for 24% -> 22%
where the time goes in v5:
time: 77.8 us; the launch traced here: 77.5 us
  waiting for transfers between devices  35.2 us (45%)
  Pallas kernels  25.1 us (32%)
  starting transfers between devices  16.3 us (21%)
    ppermute x6, waiting for transfers between devices, exchanged(): return x + lax.ppermute(x, axis, [(i, i ^ step) for i in range(size)])  25.6 us
    pallas_call x4, Pallas kernels, mix_call(): pl.pallas_call(functools.partial(mix_kernel, heads, head_dim, chans // he...  10 us
    ppermute x4, waiting for transfers between devices, swap(): return lax.ppermute(x, 'seq', pairs)  9.59 us
    ppermute x6, starting transfers between devices, exchanged(): return x + lax.ppermute(x, axis, [(i, i ^ step) for i in range(size)])  7.46 us
    ppermute x4, starting transfers between devices, swap(): return lax.ppermute(x, 'seq', pairs)  7.26 us
    pallas_call x2, Pallas kernels, scores_call(): pl.pallas_call(functools.partial(score_kernel, heads, head_dim, head_chan...  7.1 us
    pallas_call x1, Pallas kernels, load_call(): pl.pallas_call(functools.partial(load_kernel, chans, rows, width), grid_s...  2.34 us
    pallas_call x1, Pallas kernels, table_call(): pl.pallas_call(functools.partial(table_kernel, planes, step), grid_spec=p...  2.13 us
  transfers between devices with their start and end apart: 11, of which 7 were waited for; matrix products, arithmetic and copies ran while one was open for 0% of the time, Pallas kernels for 22%

profile of v5, /device:TPU:0, one launch (start us, length us, event | category | flops | bytes accessed | tf_op | source)
XLA Modules:
  0.0 77.5 jit_solution(15753233620442244803)
XLA Ops:
  0.6 0.1 pad_add_fusion.place
  0.7 2.3 %load.1 = (bf16[64,512]{1,0:T(8,128)(2,1)S(1)}, bf16[64,512]{1,0:T(8,128)(2,1)S(1)}, bf16[24,32,512]{2,1,0:T(8,128)(2,1)S(1)}, bf16[24,32,512]{2,1,0:T(8,128)(2,...) custom-call(s32[2]{0:T(128)S(1)} %pad_add_fusion.place, ...), custom_call_target="tpu_custom_call" | custom-call | bytes 1638400 | tf_op jit(solution)/shard_map/load/pallas_call | solution.py:85
  3.1 0.0 copy-start.1
  3.1 0.7 collective-permute-start
  3.7 5.8 %collective-permute-start.1 = (bf16[64,512]{1,0:T(8,128)(2,1)S(1)}, bf16[64,512]{1,0:T(8,128)(2,1)S(1)}, u32[]{:S(2)}, u32[]{:S(2)}) collective-permute-start(bf16[64,512]{1,0:T(8,128)(2,1)S(1)} %get-tuple-element.31), channel_id=1, source_target_pairs={{0,4},{4,0},{8,12},{12,8},{16,20},{20,16},{24,28},{28,24},{1,5},{5... | collective-permute-start | bytes 196616 | tf_op jit(solution)/shard_map/ppermute | solution.py:496
  9.6 3.5 %shard_map.103 = (bf16[4,2,768,256]{3,2,1,0:T(8,128)(2,1)S(1)}, f32[4,2,256]{2,1,0:T(2,128)S(1)}, f32[16,2048]{1,0:T(8,128)S(1)}) custom-call(s32[3,8]{1,0:T(4,128)S(1)} %get-tuple-element.24.lists, s32[64]{0:T(128)S(1)} %get-tuple-element.25.counts, s32[2]{0:T(128)S(1)} %pad_add_fusion.place, bf16[32,2048]{1,0:T(8,128)(2,1)S(1)} %get-tuple-element.26.refs_0_, ...), custom_call_target="tpu_custom_call" | custom-call | flops 314572800 | bytes 3145728 | tf_op jit(solution)/shard_map/pallas_call | solution.py:193
  13.1 0.0 collective-permute-done.refs_4_.refs_0_
  13.1 0.0 collective-permute-done.1.refs_5_.refs_0_
  13.1 3.6 %shard_map.104 = (bf16[4,2,768,256]{3,2,1,0:T(8,128)(2,1)S(1)}, f32[4,2,256]{2,1,0:T(2,128)S(1)}, f32[16,2048]{1,0:T(8,128)S(1)}) custom-call(s32[3,8]{1,0:T(4,128)S(1)} %get-tuple-element.24.lists, s32[64]{0:T(128)S(1)} %get-tuple-element.25.counts, s32[2]{0:T(128)S(1)} %pad_add_fusion.place, bf16[32,2048]{1,0:T(8,128)(2,1)S(1)} %get-tuple-element.26.refs_0_, ...), custom_call_target="tpu_custom_call" | custom-call | flops 314572800 | bytes 3145728 | tf_op jit(solution)/shard_map/pallas_call | solution.py:193
  16.7 1.4 %collective-permute-done.4 = f32[16,2048]{1,0:T(8,128)S(1)} collective-permute-done((f32[16,2048]{1,0:T(8,128)S(1)}, f32[16,2048]{1,0:T(8,128)S(1)}, u32[]{:S(2)}, u32[]{:S(2)}) %collective-permute-start.4) | collective-permute-done | bytes 131104 | tf_op jit(solution)/shard_map/ppermute | solution.py:462
  18.1 1.6 %collective-permute-start.5 = (f32[16,2048]{1,0:T(8,128)S(1)}, f32[16,2048]{1,0:T(8,128)S(1)}, u32[]{:S(2)}, u32[]{:S(2)}) collective-permute-start(f32[16,2048]{1,0:T(8,128)S(1)} %add.18), channel_id=1, source_target_pairs={{0,2},{1,3},{2,0},{3,1},{4,6},{5,7},{6,4},{7,5},{8,10},{9,11},{10,... | collective-permute-start | bytes 393224 | tf_op jit(solution)/shard_map/ppermute | solution.py:462
  19.6 2.1 %table.1 = (bf16[2,480,2048]{2,1,0:T(8,128)(2,1)S(1)}, f32[1,480]{1,0:T(1,128)S(1)}) custom-call(s32[2]{0:T(128)S(1)} %pad_add_fusion.place, s32[3,2048]{1,0:T(4,128)S(1)} %get-tuple-element.40.n_ref, f32[3,2048]{1,0:T(4,128)S(1)} %copy-done.1), custom_call_target="tpu_custom_call" | custom-call | flops 39321600 | bytes 3932160 | tf_op jit(solution)/shard_map/table/pallas_call | solution.py:361
  21.8 1.9 %collective-permute-done.5 = f32[16,2048]{1,0:T(8,128)S(1)} collective-permute-done((f32[16,2048]{1,0:T(8,128)S(1)}, f32[16,2048]{1,0:T(8,128)S(1)}, u32[]{:S(2)}, u32[]{:S(2)}) %collective-permute-start.5) | collective-permute-done | bytes 131104 | tf_op jit(solution)/shard_map/ppermute | solution.py:462
  23.7 1.4 %structure.1 = f32[16,960]{1,0:T(8,128)S(1)} custom-call(f32[16,2048]{1,0:T(8,128)S(1)} %add.19.c_ref, bf16[960,2048]{1,0:T(8,128)(2,1)S(1)} %bitcast.14), custom_call_target="tpu_custom_call" | custom-call | flops 1006632960 | bytes 3932160 | tf_op jit(solution)/shard_map/structure/pallas_call | solution.py:389
  25.1 1.0 %collective-permute-start.6 = (f32[16,960]{1,0:T(8,128)S(1)}, f32[16,960]{1,0:T(8,128)S(1)}, u32[]{:S(2)}, u32[]{:S(2)}) collective-permute-start(f32[16,960]{1,0:T(8,128)S(1)} %structure.1), channel_id=1, source_target_pairs={{0,4},{4,0},{8,12},{12,8},{16,20},{20,16},{24,28},{28,24},{1,5},{5... | collective-permute-start | bytes 184328 | tf_op jit(solution)/shard_map/ppermute | solution.py:462
  26.1 3.3 %collective-permute-done.6 = f32[16,960]{1,0:T(8,128)S(1)} collective-permute-done((f32[16,960]{1,0:T(8,128)S(1)}, f32[16,960]{1,0:T(8,128)S(1)}, u32[]{:S(2)}, u32[]{:S(2)}) %collective-permute-start.6) | collective-permute-done | bytes 61472 | tf_op jit(solution)/shard_map/ppermute | solution.py:462
  29.4 1.6 %collective-permute-start.7 = (f32[16,960]{1,0:T(8,128)S(1)}, f32[16,960]{1,0:T(8,128)S(1)}, u32[]{:S(2)}, u32[]{:S(2)}) collective-permute-start(f32[16,960]{1,0:T(8,128)S(1)} %add.20), channel_id=1, source_target_pairs={{0,8},{4,12},{8,0},{12,4},{16,24},{20,28},{24,16},{28,20},{1,9},{5... | collective-permute-start | bytes 184328 | tf_op jit(solution)/shard_map/ppermute | solution.py:462
  31.1 0.7 collective-permute-start.3
  31.8 2.0 %collective-permute-done.7 = f32[16,960]{1,0:T(8,128)S(1)} collective-permute-done((f32[16,960]{1,0:T(8,128)S(1)}, f32[16,960]{1,0:T(8,128)S(1)}, u32[]{:S(2)}, u32[]{:S(2)}) %collective-permute-start.7) | collective-permute-done | bytes 61472 | tf_op jit(solution)/shard_map/ppermute | solution.py:462
  33.8 3.2 %collective-permute-start.8 = (f32[16,960]{1,0:T(8,128)S(1)}, f32[16,960]{1,0:T(8,128)S(1)}, u32[]{:S(2)}, u32[]{:S(2)}) collective-permute-start(f32[16,960]{1,0:T(8,128)S(1)} %add.21), channel_id=1, source_target_pairs={{0,16},{4,20},{8,24},{12,28},{16,0},{20,4},{24,8},{28,12},{1,17},{... | collective-permute-start | bytes 184328 | tf_op jit(solution)/shard_map/ppermute | solution.py:462
  36.9 15.7 %collective-permute-done.8 = f32[16,960]{1,0:T(8,128)S(1)} collective-permute-done((f32[16,960]{1,0:T(8,128)S(1)}, f32[16,960]{1,0:T(8,128)S(1)}, u32[]{:S(2)}, u32[]{:S(2)}) %collective-permute-start.8) | collective-permute-done | bytes 61472 | tf_op jit(solution)/shard_map/ppermute | solution.py:462
  52.7 1.5 %fields.1 = f32[24,2048]{1,0:T(8,128)S(1)} custom-call(s32[2]{0:T(128)S(1)} %pad_add_fusion.place, f32[16,960]{1,0:T(8,128)S(1)} %add.22.s_ref, f32[1,480]{1,0:T(1,128)S(1)} %get-tuple-element.42.weight_ref, f32[16,2048]{1,0:T(8,128)S(1)} %add.19.c_ref, bf16[2,480,2048]{2,1,0:T(8,128)(2,1)S(1)} %get-tuple-element.41.t_ref), custom_call_target="tpu_custom_call" | custom-call | flops 503316480 | bytes 1966080 | tf_op jit(solution)/shard_map/fields/pallas_call | solution.py:426
  54.2 0.1 collective-permute-start.9
  54.2 0.1 collective-permute-start.2
  54.3 1.3 %collective-permute-done.9 = f32[24,2048]{1,0:T(8,128)S(1)} collective-permute-done((f32[24,2048]{1,0:T(8,128)S(1)}, f32[24,2048]{1,0:T(8,128)S(1)}, u32[]{:S(2)}, u32[]{:S(2)}) %collective-permute-start.9) | collective-permute-done | bytes 196640 | tf_op jit(solution)/shard_map/ppermute | solution.py:462
  55.7 1.6 %collective-permute-start.10 = (bf16[24,2048]{1,0:T(8,128)(2,1)S(1)}, bf16[24,2048]{1,0:T(8,128)(2,1)S(1)}, u32[]{:S(2)}, u32[]{:S(2)}) collective-permute-start(bf16[24,2048]{1,0:T(8,128)(2,1)S(1)} %add_convert_fusion.mine_ref), channel_id=1, source_target_pairs={{0,2},{1,3},{2,0},{3,1},{4,6},{5,7},{6,4},{7,5},{8,10},{9,11},{10,... | collective-permute-start | bytes 294920 | tf_op jit(solution)/shard_map/ppermute | solution.py:522
  57.3 2.7 %shard_map.105.refs_0_ = bf16[25,32,2048]{2,1,0:T(8,128)(2,1)} custom-call(s32[3,8]{1,0:T(4,128)S(1)} %get-tuple-element.24.lists, s32[2]{0:T(128)S(1)} %pad_add_fusion.place, bf16[25,32,2048]{2,1,0:T(8,128)(2,1)S(1)} %bitcast.10, bf16[4,2,768,256]{3,2,1,0:T(8,128)(2,1)S(1)} %get-tuple-element.33.p_ref, f32[4,2,256]{2,1,0:T(2,128)S(1)} %get-tuple-element.34.scale_ref, ...), custom_call_target="tpu_custom_call" | custom-call | flops 629145600 | bytes 3276800 | tf_op jit(solution)/shard_map/pallas_call | solution.py:269
  60.0 2.3 %shard_map.106.refs_0_ = bf16[25,32,2048]{2,1,0:T(8,128)(2,1)} custom-call(s32[3,8]{1,0:T(4,128)S(1)} %get-tuple-element.24.lists, s32[2]{0:T(128)S(1)} %pad_add_fusion.place, bf16[25,32,2048]{2,1,0:T(8,128)(2,1)S(1)} %bitcast.11, bf16[4,2,768,256]{3,2,1,0:T(8,128)(2,1)S(1)} %get-tuple-element.36.p_ref, ...), custom_call_target="tpu_custom_call", output_to_operand_aliasing={{}: (5, {})} | custom-call | flops 629145600 | bytes 3276800 | tf_op jit(solution)/shard_map/pallas_call | solution.py:269
  62.3 2.3 %shard_map.107.refs_2_ = bf16[25,32,2048]{2,1,0:T(8,128)(2,1)} custom-call(s32[3,8]{1,0:T(4,128)S(1)} %get-tuple-element.24.lists, s32[2]{0:T(128)S(1)} %pad_add_fusion.place, bf16[25,32,2048]{2,1,0:T(8,128)(2,1)S(1)} %bitcast.12, bf16[4,2,768,256]{3,2,1,0:T(8,128)(2,1)S(1)} %get-tuple-element.36.p_ref, ...), custom_call_target="tpu_custom_call", output_to_operand_aliasing={{}: (5, {})} | custom-call | flops 629145600 | bytes 3276800 | tf_op jit(solution)/shard_map/pallas_call | solution.py:269
  64.6 9.6 %collective-permute-done.2.refs_1_ = bf16[24,32,512]{2,1,0:T(8,128)(2,1)S(1)} collective-permute-done((bf16[24,32,512]{2,1,0:T(8,128)(2,1)S(1)}, bf16[24,32,512]{2,1,0:T(8,128)(2,1)S(1)}, u32[]{:S(2)}, u32[]{:S(2)}) %collective-permute-start.2) | collective-permute-done | bytes 786464 | tf_op jit(solution)/shard_map/ppermute | solution.py:496
  74.2 2.7 %shard_map.108 = bf16[25,32,2048]{2,1,0:T(8,128)(2,1)} custom-call(s32[3,8]{1,0:T(4,128)S(1)} %get-tuple-element.24.lists, s32[2]{0:T(128)S(1)} %pad_add_fusion.place, bf16[25,32,2048]{2,1,0:T(8,128)(2,1)S(1)} %bitcast.13, bf16[4,2,768,256]{3,2,1,0:T(8,128)(2,1)S(1)} %get-tuple-element.33.p_ref, ...), custom_call_target="tpu_custom_call", output_to_operand_aliasing={{}: (7, {})} | custom-call | flops 629145600 | bytes 3276800 | tf_op jit(solution)/shard_map/pallas_call | solution.py:269
  76.9 0.7 finish.1
  (12 shorter events, 0.1 us)
Async XLA Ops:
  3.1 16.6 %copy-start.1 = (f32[3,2048]{1,0:T(4,128)S(1)}, f32[3,2048]{1,0:T(4,128)}, u32[]{:S(2)}) copy-start(f32[3,2048]{1,0:T(4,128)} %f_ref.1) | copy-start | bytes 73732
  3.1 10.0 %collective-permute-start = (bf16[64,512]{1,0:T(8,128)(2,1)S(1)}, bf16[64,512]{1,0:T(8,128)(2,1)S(1)}, u32[]{:S(2)}, u32[]{:S(2)}) collective-permute-start(bf16[64,512]{1,0:T(8,128)(2,1)S(1)} %get-tuple-element.30), channel_id=1, source_target_pairs={{4,8},{8,4},{12,16},{16,12},{20,24},{24,20},{5,9},{9,5},{13,17},{1... | collective-permute-start | bytes 196616 | tf_op jit(solution)/shard_map/ppermute | solution.py:496
  3.7 9.4 %collective-permute-start.1 = (bf16[64,512]{1,0:T(8,128)(2,1)S(1)}, bf16[64,512]{1,0:T(8,128)(2,1)S(1)}, u32[]{:S(2)}, u32[]{:S(2)}) collective-permute-start(bf16[64,512]{1,0:T(8,128)(2,1)S(1)} %get-tuple-element.31), channel_id=1, source_target_pairs={{0,4},{4,0},{8,12},{12,8},{16,20},{20,16},{24,28},{28,24},{1,5},{5... | collective-permute-start | bytes 196616 | tf_op jit(solution)/shard_map/ppermute | solution.py:496
  16.7 1.4 %collective-permute-start.4 = (f32[16,2048]{1,0:T(8,128)S(1)}, f32[16,2048]{1,0:T(8,128)S(1)}, u32[]{:S(2)}, u32[]{:S(2)}) collective-permute-start(f32[16,2048]{1,0:T(8,128)S(1)} %get-tuple-element.39), channel_id=1, source_target_pairs={{0,1},{1,0},{2,3},{3,2},{4,5},{5,4},{6,7},{7,6},{8,9},{9,8},{10,11... | collective-permute-start | bytes 393224 | tf_op jit(solution)/shard_map/ppermute | solution.py:462
  18.1 5.6 %collective-permute-start.5 = (f32[16,2048]{1,0:T(8,128)S(1)}, f32[16,2048]{1,0:T(8,128)S(1)}, u32[]{:S(2)}, u32[]{:S(2)}) collective-permute-start(f32[16,2048]{1,0:T(8,128)S(1)} %add.18), channel_id=1, source_target_pairs={{0,2},{1,3},{2,0},{3,1},{4,6},{5,7},{6,4},{7,5},{8,10},{9,11},{10,... | collective-permute-start | bytes 393224 | tf_op jit(solution)/shard_map/ppermute | solution.py:462
  25.1 32.2 %copy-start = (bf16[32,25,2048]{2,0,1:T(8,128)(2,1)S(1)}, bf16[32,25,2048]{2,0,1:T(8,128)(2,1)}, u32[]{:S(2)}) copy-start(bf16[32,25,2048]{2,0,1:T(8,128)(2,1)} %param.10) | copy-start | bytes 9830404
  25.1 4.3 %collective-permute-start.6 = (f32[16,960]{1,0:T(8,128)S(1)}, f32[16,960]{1,0:T(8,128)S(1)}, u32[]{:S(2)}, u32[]{:S(2)}) collective-permute-start(f32[16,960]{1,0:T(8,128)S(1)} %structure.1), channel_id=1, source_target_pairs={{0,4},{4,0},{8,12},{12,8},{16,20},{20,16},{24,28},{28,24},{1,5},{5... | collective-permute-start | bytes 184328 | tf_op jit(solution)/shard_map/ppermute | solution.py:462
  29.4 4.3 %collective-permute-start.7 = (f32[16,960]{1,0:T(8,128)S(1)}, f32[16,960]{1,0:T(8,128)S(1)}, u32[]{:S(2)}, u32[]{:S(2)}) collective-permute-start(f32[16,960]{1,0:T(8,128)S(1)} %add.20), channel_id=1, source_target_pairs={{0,8},{4,12},{8,0},{12,4},{16,24},{20,28},{24,16},{28,20},{1,9},{5... | collective-permute-start | bytes 184328 | tf_op jit(solution)/shard_map/ppermute | solution.py:462
  31.1 26.2 %collective-permute-start.3 = (bf16[24,32,512]{2,1,0:T(8,128)(2,1)S(1)}, bf16[24,32,512]{2,1,0:T(8,128)(2,1)S(1)}, u32[]{:S(2)}, u32[]{:S(2)}) collective-permute-start(bf16[24,32,512]{2,1,0:T(8,128)(2,1)S(1)} %get-tuple-element.38), channel_id=1, source_target_pairs={{4,8},{8,4},{12,16},{16,12},{20,24},{24,20},{5,9},{9,5},{13,17},{1... | collective-permute-start | bytes 2359304 | tf_op jit(solution)/shard_map/ppermute | solution.py:496
  33.8 18.9 %collective-permute-start.8 = (f32[16,960]{1,0:T(8,128)S(1)}, f32[16,960]{1,0:T(8,128)S(1)}, u32[]{:S(2)}, u32[]{:S(2)}) collective-permute-start(f32[16,960]{1,0:T(8,128)S(1)} %add.21), channel_id=1, source_target_pairs={{0,16},{4,20},{8,24},{12,28},{16,0},{20,4},{24,8},{28,12},{1,17},{... | collective-permute-start | bytes 184328 | tf_op jit(solution)/shard_map/ppermute | solution.py:462
  54.2 1.5 %collective-permute-start.9 = (f32[24,2048]{1,0:T(8,128)S(1)}, f32[24,2048]{1,0:T(8,128)S(1)}, u32[]{:S(2)}, u32[]{:S(2)}) collective-permute-start(f32[24,2048]{1,0:T(8,128)S(1)} %fields.1), channel_id=1, source_target_pairs={{0,1},{1,0},{2,3},{3,2},{4,5},{5,4},{6,7},{7,6},{8,9},{9,8},{10,11... | collective-permute-start | bytes 589832 | tf_op jit(solution)/shard_map/ppermute | solution.py:462
  54.2 19.9 %collective-permute-start.2 = (bf16[24,32,512]{2,1,0:T(8,128)(2,1)S(1)}, bf16[24,32,512]{2,1,0:T(8,128)(2,1)S(1)}, u32[]{:S(2)}, u32[]{:S(2)}) collective-permute-start(bf16[24,32,512]{2,1,0:T(8,128)(2,1)S(1)} %get-tuple-element.35), channel_id=1, source_target_pairs={{0,4},{4,0},{8,12},{12,8},{16,20},{20,16},{24,28},{28,24},{1,5},{5... | collective-permute-start | bytes 2359304 | tf_op jit(solution)/shard_map/ppermute | solution.py:496
  55.7 21.2 %collective-permute-start.10 = (bf16[24,2048]{1,0:T(8,128)(2,1)S(1)}, bf16[24,2048]{1,0:T(8,128)(2,1)S(1)}, u32[]{:S(2)}, u32[]{:S(2)}) collective-permute-start(bf16[24,2048]{1,0:T(8,128)(2,1)S(1)} %add_convert_fusion.mine_ref), channel_id=1, source_target_pairs={{0,2},{1,3},{2,0},{3,1},{4,6},{5,7},{6,4},{7,5},{8,10},{9,11},{10,... | collective-permute-start | bytes 294920 | tf_op jit(solution)/shard_map/ppermute | solution.py:522

commit v6 on v5

--- a/solution.py
+++ b/solution.py
@@ -513,19 +513,27 @@
         "edges", lists, counts, place, asked, keys, v0, weight, (far, near, part), heads, head_dim
     )
     table, wave_weight = table_call(place, vectors, fractional, planes)
-    charges = summed(part, "inner")
+    last = lax.axis_size("inner") // 2
+
+    def halfway(x, name):
+        x = summed(x, "inner", stop=last)
+        x = x.astype(BF) if name == "charge" else x
+        return x, lax.ppermute(x, "inner", [(i, i ^ last) for i in range(2 * last)])
+
+    mine, theirs = halfway(part, "charge")
+    charges = mine.astype(F32) + theirs.astype(F32)
     structure = structure_call(charges, table.reshape(-1, atoms), inv_root)
-    structure = summed(structure, "seq")
+    for step in (2, 1):
+        structure = exchanged(structure, "seq", step)
+    structure = summed(structure, "seq", 4)
     fields = field_call(place, structure, wave_weight, charges, table, planes)
-    last = lax.axis_size("inner") // 2
-    fields = summed(fields, "inner", stop=last).astype(BF)
-    others = lax.ppermute(fields, "inner", [(i, i ^ last) for i in range(2 * last)])
+    fields, others = halfway(fields, "field")
     potential, forces = finish_call(fields, others, nq)
 
     mix = functools.partial(mix_call, heads=heads, head_dim=head_dim)
-    attention = mix("far", lists, place, values, p_out, scale_out, (far, far_big), None)
-    attention = mix("low", lists, place, values, p_in, scale_in, (), attention)
+    attention = mix("low", lists, place, values, p_in, scale_in, (), None)
     attention = mix("high", lists, place, values, p_in, scale_in, (), attention)
+    attention = mix("far", lists, place, values, p_out, scale_out, (far, far_big), attention)
     attention = mix("near", lists, place, values, p_out, scale_out, (near, near_big), attention)
     return (attention.transpose(1, 0, 2), potential, forces)
 

time: 77.8 us -> 76.7 us (0.986)
  waiting for transfers between devices: 35.2 us -> 32 us
  starting transfers between devices: 16.3 us -> 18.4 us
    ppermute x4, waiting for transfers between devices: 9.59 us -> 0.01 us  [swap(): return lax.ppermute(x, 'seq', pairs)]
    ppermute x6 -> x5, waiting for transfers between devices: 25.6 us -> 32 us  [exchanged(): return x + lax.ppermute(x, axis, [(i, i ^ step) for i in range(size)])]
    ppermute x4, starting transfers between devices: 7.26 us -> 8.16 us  [swap(): return lax.ppermute(x, 'seq', pairs)]
    ppermute x6 -> x5, starting transfers between devices: 7.46 us -> 8.13 us  [exchanged(): return x + lax.ppermute(x, axis, [(i, i ^ step) for i in range(size)])]
    ppermute x1 -> x2, starting transfers between devices: 1.57 us -> 2.15 us  [halfway(): lax.ppermute(x, 'inner', [(i, i ^ last) for i in range(2 * last)])]
  transfers between devices with their start and end apart: 11 -> 11, of which waited for: 7 -> 5; matrix products, arithmetic and copies ran while one was open for 0% -> 0% of each run, Pallas kernels for 22% -> 24%
where the time goes in v6:
time: 76.7 us; the launch traced here: 76.5 us
  waiting for transfers between devices  32 us (42%)
  Pallas kernels  25.1 us (33%)
  starting transfers between devices  18.4 us (24%)
    ppermute x5, waiting for transfers between devices, exchanged(): return x + lax.ppermute(x, axis, [(i, i ^ step) for i in range(size)])  32 us
    pallas_call x4, Pallas kernels, mix_call(): pl.pallas_call(functools.partial(mix_kernel, heads, head_dim, chans // he...  10 us
    ppermute x4, starting transfers between devices, swap(): return lax.ppermute(x, 'seq', pairs)  8.16 us
    ppermute x5, starting transfers between devices, exchanged(): return x + lax.ppermute(x, axis, [(i, i ^ step) for i in range(size)])  8.13 us
    pallas_call x2, Pallas kernels, scores_call(): pl.pallas_call(functools.partial(score_kernel, heads, head_dim, head_chan...  7.1 us
    pallas_call x1, Pallas kernels, load_call(): pl.pallas_call(functools.partial(load_kernel, chans, rows, width), grid_s...  2.34 us
    ppermute x2, starting transfers between devices, halfway(): lax.ppermute(x, 'inner', [(i, i ^ last) for i in range(2 * last)])  2.15 us
    pallas_call x1, Pallas kernels, table_call(): pl.pallas_call(functools.partial(table_kernel, planes, step), grid_spec=p...  2.13 us
  transfers between devices with their start and end apart: 11, of which 5 were waited for; matrix products, arithmetic and copies ran while one was open for 0% of the time, Pallas kernels for 24%

profile of v6, /device:TPU:0, one launch (start us, length us, event | category | flops | bytes accessed | tf_op | source)
XLA Modules:
  0.0 76.5 jit_solution(16299982739328734597)
XLA Ops:
  0.6 0.1 pad_add_fusion.place
  0.7 2.3 %load.1 = (bf16[64,512]{1,0:T(8,128)(2,1)S(1)}, bf16[64,512]{1,0:T(8,128)(2,1)S(1)}, bf16[24,32,512]{2,1,0:T(8,128)(2,1)S(1)}, bf16[24,32,512]{2,1,0:T(8,128)(2,...) custom-call(s32[2]{0:T(128)S(1)} %pad_add_fusion.place, ...), custom_call_target="tpu_custom_call" | custom-call | bytes 1638400 | tf_op jit(solution)/shard_map/load/pallas_call | solution.py:85
  3.1 0.0 copy-start.1
  3.1 0.7 collective-permute-start
  3.7 5.8 %collective-permute-start.1 = (bf16[64,512]{1,0:T(8,128)(2,1)S(1)}, bf16[64,512]{1,0:T(8,128)(2,1)S(1)}, u32[]{:S(2)}, u32[]{:S(2)}) collective-permute-start(bf16[64,512]{1,0:T(8,128)(2,1)S(1)} %get-tuple-element.31), channel_id=1, source_target_pairs={{0,4},{4,0},{8,12},{12,8},{16,20},{20,16},{24,28},{28,24},{1,5},{5... | collective-permute-start | bytes 196616 | tf_op jit(solution)/shard_map/ppermute | solution.py:496
  9.6 3.5 %shard_map.103 = (bf16[4,2,768,256]{3,2,1,0:T(8,128)(2,1)S(1)}, f32[4,2,256]{2,1,0:T(2,128)S(1)}, f32[16,2048]{1,0:T(8,128)S(1)}) custom-call(s32[3,8]{1,0:T(4,128)S(1)} %get-tuple-element.24.lists, s32[64]{0:T(128)S(1)} %get-tuple-element.25.counts, s32[2]{0:T(128)S(1)} %pad_add_fusion.place, bf16[32,2048]{1,0:T(8,128)(2,1)S(1)} %get-tuple-element.26.refs_0_, ...), custom_call_target="tpu_custom_call" | custom-call | flops 314572800 | bytes 3145728 | tf_op jit(solution)/shard_map/pallas_call | solution.py:193
  13.1 0.0 collective-permute-done.refs_4_.refs_0_
  13.1 0.0 collective-permute-done.1.refs_5_.refs_0_
  13.1 3.6 %shard_map.104 = (bf16[4,2,768,256]{3,2,1,0:T(8,128)(2,1)S(1)}, f32[4,2,256]{2,1,0:T(2,128)S(1)}, f32[16,2048]{1,0:T(8,128)S(1)}) custom-call(s32[3,8]{1,0:T(4,128)S(1)} %get-tuple-element.24.lists, s32[64]{0:T(128)S(1)} %get-tuple-element.25.counts, s32[2]{0:T(128)S(1)} %pad_add_fusion.place, bf16[32,2048]{1,0:T(8,128)(2,1)S(1)} %get-tuple-element.26.refs_0_, ...), custom_call_target="tpu_custom_call" | custom-call | flops 314572800 | bytes 3145728 | tf_op jit(solution)/shard_map/pallas_call | solution.py:193
  16.7 0.0 collective-permute-start.4
  16.7 1.4 %collective-permute-done.4 = f32[16,2048]{1,0:T(8,128)S(1)} collective-permute-done((f32[16,2048]{1,0:T(8,128)S(1)}, f32[16,2048]{1,0:T(8,128)S(1)}, u32[]{:S(2)}, u32[]{:S(2)}) %collective-permute-start.4) | collective-permute-done | bytes 131104 | tf_op jit(solution)/shard_map/ppermute | solution.py:462
  18.1 1.6 %collective-permute-start.5 = (bf16[16,2048]{1,0:T(8,128)(2,1)S(1)}, bf16[16,2048]{1,0:T(8,128)(2,1)S(1)}, u32[]{:S(2)}, u32[]{:S(2)}) collective-permute-start(bf16[16,2048]{1,0:T(8,128)(2,1)S(1)} %add_convert_fusion), channel_id=1, source_target_pairs={{0,2},{1,3},{2,0},{3,1},{4,6},{5,7},{6,4},{7,5},{8,10},{9,11},{10,... | collective-permute-start | bytes 196616 | tf_op jit(solution)/shard_map/ppermute | solution.py:521
  19.6 1.0 %collective-permute-start.2 = (bf16[24,32,512]{2,1,0:T(8,128)(2,1)S(1)}, bf16[24,32,512]{2,1,0:T(8,128)(2,1)S(1)}, u32[]{:S(2)}, u32[]{:S(2)}) collective-permute-start(bf16[24,32,512]{2,1,0:T(8,128)(2,1)S(1)} %get-tuple-element.35), channel_id=1, source_target_pairs={{0,4},{4,0},{8,12},{12,8},{16,20},{20,16},{24,28},{28,24},{1,5},{5... | collective-permute-start | bytes 2359304 | tf_op jit(solution)/shard_map/ppermute | solution.py:496
  20.6 0.7 collective-permute-start.3
  21.3 2.1 %table.1 = (bf16[2,480,2048]{2,1,0:T(8,128)(2,1)S(1)}, f32[1,480]{1,0:T(1,128)S(1)}) custom-call(s32[2]{0:T(128)S(1)} %pad_add_fusion.place, s32[3,2048]{1,0:T(4,128)S(1)} %get-tuple-element.40.n_ref, f32[3,2048]{1,0:T(4,128)S(1)} %copy-done.1), custom_call_target="tpu_custom_call" | custom-call | flops 39321600 | bytes 3932160 | tf_op jit(solution)/shard_map/table/pallas_call | solution.py:361
  23.5 1.4 %structure.1 = f32[16,960]{1,0:T(8,128)S(1)} custom-call(f32[16,2048]{1,0:T(8,128)S(1)} %convert_add_fusion.c_ref, bf16[960,2048]{1,0:T(8,128)(2,1)S(1)} %bitcast.14), custom_call_target="tpu_custom_call" | custom-call | flops 1006632960 | bytes 3932160 | tf_op jit(solution)/shard_map/structure/pallas_call | solution.py:389
  24.9 3.8 %collective-permute-start.6 = (f32[16,960]{1,0:T(8,128)S(1)}, f32[16,960]{1,0:T(8,128)S(1)}, u32[]{:S(2)}, u32[]{:S(2)}) collective-permute-start(f32[16,960]{1,0:T(8,128)S(1)} %structure.1), channel_id=1, source_target_pairs={{0,8},{4,12},{8,0},{12,4},{16,24},{20,28},{24,16},{28,20},{1,9},{5... | collective-permute-start | bytes 184328 | tf_op jit(solution)/shard_map/ppermute | solution.py:462
  28.6 14.8 %collective-permute-done.6 = f32[16,960]{1,0:T(8,128)S(1)} collective-permute-done((f32[16,960]{1,0:T(8,128)S(1)}, f32[16,960]{1,0:T(8,128)S(1)}, u32[]{:S(2)}, u32[]{:S(2)}) %collective-permute-start.6) | collective-permute-done | bytes 61472 | tf_op jit(solution)/shard_map/ppermute | solution.py:462
  43.5 0.1 collective-permute-start.7
  43.6 12.1 %collective-permute-done.7 = f32[16,960]{1,0:T(8,128)S(1)} collective-permute-done((f32[16,960]{1,0:T(8,128)S(1)}, f32[16,960]{1,0:T(8,128)S(1)}, u32[]{:S(2)}, u32[]{:S(2)}) %collective-permute-start.7) | collective-permute-done | bytes 61472 | tf_op jit(solution)/shard_map/ppermute | solution.py:462
  55.7 4.2 %collective-permute-start.8 = (f32[16,960]{1,0:T(8,128)S(1)}, f32[16,960]{1,0:T(8,128)S(1)}, u32[]{:S(2)}, u32[]{:S(2)}) collective-permute-start(f32[16,960]{1,0:T(8,128)S(1)} %add.21), channel_id=1, source_target_pairs={{0,16},{4,20},{8,24},{12,28},{16,0},{20,4},{24,8},{28,12},{1,17},{... | collective-permute-start | bytes 184328 | tf_op jit(solution)/shard_map/ppermute | solution.py:462
  59.9 2.3 %collective-permute-done.8 = f32[16,960]{1,0:T(8,128)S(1)} collective-permute-done((f32[16,960]{1,0:T(8,128)S(1)}, f32[16,960]{1,0:T(8,128)S(1)}, u32[]{:S(2)}, u32[]{:S(2)}) %collective-permute-start.8) | collective-permute-done | bytes 61472 | tf_op jit(solution)/shard_map/ppermute | solution.py:462
  62.2 1.5 %fields.1 = f32[24,2048]{1,0:T(8,128)S(1)} custom-call(s32[2]{0:T(128)S(1)} %pad_add_fusion.place, f32[16,960]{1,0:T(8,128)S(1)} %add.22.s_ref, f32[1,480]{1,0:T(1,128)S(1)} %get-tuple-element.42.weight_ref, f32[16,2048]{1,0:T(8,128)S(1)} %convert_add_fusion.c_ref, bf16[2,480,2048]{2,1,0:T(8,128)(2,1)S(1)} %get-tuple-element.41.t_ref), custom_call_target="tpu_custom_call" | custom-call | flops 503316480 | bytes 1966080 | tf_op jit(solution)/shard_map/fields/pallas_call | solution.py:426
  63.7 0.1 collective-permute-start.9
  63.8 1.4 %collective-permute-done.9 = f32[24,2048]{1,0:T(8,128)S(1)} collective-permute-done((f32[24,2048]{1,0:T(8,128)S(1)}, f32[24,2048]{1,0:T(8,128)S(1)}, u32[]{:S(2)}, u32[]{:S(2)}) %collective-permute-start.9) | collective-permute-done | bytes 196640 | tf_op jit(solution)/shard_map/ppermute | solution.py:462
  65.2 0.6 collective-permute-start.10
  65.8 2.3 %shard_map.105.refs_0_ = bf16[25,32,2048]{2,1,0:T(8,128)(2,1)} custom-call(s32[3,8]{1,0:T(4,128)S(1)} %get-tuple-element.24.lists, s32[2]{0:T(128)S(1)} %pad_add_fusion.place, bf16[25,32,2048]{2,1,0:T(8,128)(2,1)S(1)} %bitcast.10, bf16[4,2,768,256]{3,2,1,0:T(8,128)(2,1)S(1)} %get-tuple-element.37.p_ref, f32[4,2,256]{2,1,0:T(2,128)S(1)} %get-tuple-element.38.scale_ref), custom_call_target="tpu_custom_call" | custom-call | flops 629145600 | bytes 3276800 | tf_op jit(solution)/shard_map/pallas_call | solution.py:269
  68.2 2.3 %shard_map.106.refs_2_ = bf16[25,32,2048]{2,1,0:T(8,128)(2,1)} custom-call(s32[3,8]{1,0:T(4,128)S(1)} %get-tuple-element.24.lists, s32[2]{0:T(128)S(1)} %pad_add_fusion.place, bf16[25,32,2048]{2,1,0:T(8,128)(2,1)S(1)} %bitcast.11, bf16[4,2,768,256]{3,2,1,0:T(8,128)(2,1)S(1)} %get-tuple-element.37.p_ref, ...), custom_call_target="tpu_custom_call", output_to_operand_aliasing={{}: (5, {})} | custom-call | flops 629145600 | bytes 3276800 | tf_op jit(solution)/shard_map/pallas_call | solution.py:269
  70.5 0.0 collective-permute-done.3.refs_1_
  70.5 2.7 %shard_map.107.refs_2_ = bf16[25,32,2048]{2,1,0:T(8,128)(2,1)} custom-call(s32[3,8]{1,0:T(4,128)S(1)} %get-tuple-element.24.lists, s32[2]{0:T(128)S(1)} %pad_add_fusion.place, bf16[25,32,2048]{2,1,0:T(8,128)(2,1)S(1)} %bitcast.12, bf16[4,2,768,256]{3,2,1,0:T(8,128)(2,1)S(1)} %get-tuple-element.33.p_ref, ...), custom_call_target="tpu_custom_call", output_to_operand_aliasing={{}: (7, {})} | custom-call | flops 629145600 | bytes 3276800 | tf_op jit(solution)/shard_map/pallas_call | solution.py:269
  73.2 2.7 %shard_map.108 = bf16[25,32,2048]{2,1,0:T(8,128)(2,1)} custom-call(s32[3,8]{1,0:T(4,128)S(1)} %get-tuple-element.24.lists, s32[2]{0:T(128)S(1)} %pad_add_fusion.place, bf16[25,32,2048]{2,1,0:T(8,128)(2,1)S(1)} %bitcast.13, bf16[4,2,768,256]{3,2,1,0:T(8,128)(2,1)S(1)} %get-tuple-element.33.p_ref, ...), custom_call_target="tpu_custom_call", output_to_operand_aliasing={{}: (7, {})} | custom-call | flops 629145600 | bytes 3276800 | tf_op jit(solution)/shard_map/pallas_call | solution.py:269
  75.8 0.7 finish.1
  (12 shorter events, 0.1 us)
Async XLA Ops:
  3.1 18.2 %copy-start.1 = (f32[3,2048]{1,0:T(4,128)S(1)}, f32[3,2048]{1,0:T(4,128)}, u32[]{:S(2)}) copy-start(f32[3,2048]{1,0:T(4,128)} %f_ref.1) | copy-start | bytes 73732
  3.1 10.0 %collective-permute-start = (bf16[64,512]{1,0:T(8,128)(2,1)S(1)}, bf16[64,512]{1,0:T(8,128)(2,1)S(1)}, u32[]{:S(2)}, u32[]{:S(2)}) collective-permute-start(bf16[64,512]{1,0:T(8,128)(2,1)S(1)} %get-tuple-element.30), channel_id=1, source_target_pairs={{4,8},{8,4},{12,16},{16,12},{20,24},{24,20},{5,9},{9,5},{13,17},{1... | collective-permute-start | bytes 196616 | tf_op jit(solution)/shard_map/ppermute | solution.py:496
  3.7 9.4 %collective-permute-start.1 = (bf16[64,512]{1,0:T(8,128)(2,1)S(1)}, bf16[64,512]{1,0:T(8,128)(2,1)S(1)}, u32[]{:S(2)}, u32[]{:S(2)}) collective-permute-start(bf16[64,512]{1,0:T(8,128)(2,1)S(1)} %get-tuple-element.31), channel_id=1, source_target_pairs={{0,4},{4,0},{8,12},{12,8},{16,20},{20,16},{24,28},{28,24},{1,5},{5... | collective-permute-start | bytes 196616 | tf_op jit(solution)/shard_map/ppermute | solution.py:496
  16.7 1.4 %collective-permute-start.4 = (f32[16,2048]{1,0:T(8,128)S(1)}, f32[16,2048]{1,0:T(8,128)S(1)}, u32[]{:S(2)}, u32[]{:S(2)}) collective-permute-start(f32[16,2048]{1,0:T(8,128)S(1)} %get-tuple-element.39), channel_id=1, source_target_pairs={{0,1},{1,0},{2,3},{3,2},{4,5},{5,4},{6,7},{7,6},{8,9},{9,8},{10,11... | collective-permute-start | bytes 393224 | tf_op jit(solution)/shard_map/ppermute | solution.py:462
  18.1 5.4 %collective-permute-start.5 = (bf16[16,2048]{1,0:T(8,128)(2,1)S(1)}, bf16[16,2048]{1,0:T(8,128)(2,1)S(1)}, u32[]{:S(2)}, u32[]{:S(2)}) collective-permute-start(bf16[16,2048]{1,0:T(8,128)(2,1)S(1)} %add_convert_fusion), channel_id=1, source_target_pairs={{0,2},{1,3},{2,0},{3,1},{4,6},{5,7},{6,4},{7,5},{8,10},{9,11},{10,... | collective-permute-start | bytes 196616 | tf_op jit(solution)/shard_map/ppermute | solution.py:521
  19.6 53.6 %collective-permute-start.2 = (bf16[24,32,512]{2,1,0:T(8,128)(2,1)S(1)}, bf16[24,32,512]{2,1,0:T(8,128)(2,1)S(1)}, u32[]{:S(2)}, u32[]{:S(2)}) collective-permute-start(bf16[24,32,512]{2,1,0:T(8,128)(2,1)S(1)} %get-tuple-element.35), channel_id=1, source_target_pairs={{0,4},{4,0},{8,12},{12,8},{16,20},{20,16},{24,28},{28,24},{1,5},{5... | collective-permute-start | bytes 2359304 | tf_op jit(solution)/shard_map/ppermute | solution.py:496
  20.6 49.9 %collective-permute-start.3 = (bf16[24,32,512]{2,1,0:T(8,128)(2,1)S(1)}, bf16[24,32,512]{2,1,0:T(8,128)(2,1)S(1)}, u32[]{:S(2)}, u32[]{:S(2)}) collective-permute-start(bf16[24,32,512]{2,1,0:T(8,128)(2,1)S(1)} %get-tuple-element.36), channel_id=1, source_target_pairs={{4,8},{8,4},{12,16},{16,12},{20,24},{24,20},{5,9},{9,5},{13,17},{1... | collective-permute-start | bytes 2359304 | tf_op jit(solution)/shard_map/ppermute | solution.py:496
  24.9 41.0 %copy-start = (bf16[32,25,2048]{2,0,1:T(8,128)(2,1)S(1)}, bf16[32,25,2048]{2,0,1:T(8,128)(2,1)}, u32[]{:S(2)}) copy-start(bf16[32,25,2048]{2,0,1:T(8,128)(2,1)} %param.10) | copy-start | bytes 9830404
  24.9 18.6 %collective-permute-start.6 = (f32[16,960]{1,0:T(8,128)S(1)}, f32[16,960]{1,0:T(8,128)S(1)}, u32[]{:S(2)}, u32[]{:S(2)}) collective-permute-start(f32[16,960]{1,0:T(8,128)S(1)} %structure.1), channel_id=1, source_target_pairs={{0,8},{4,12},{8,0},{12,4},{16,24},{20,28},{24,16},{28,20},{1,9},{5... | collective-permute-start | bytes 184328 | tf_op jit(solution)/shard_map/ppermute | solution.py:462
  43.5 12.2 %collective-permute-start.7 = (f32[16,960]{1,0:T(8,128)S(1)}, f32[16,960]{1,0:T(8,128)S(1)}, u32[]{:S(2)}, u32[]{:S(2)}) collective-permute-start(f32[16,960]{1,0:T(8,128)S(1)} %add.20), channel_id=1, source_target_pairs={{0,4},{4,0},{8,12},{12,8},{16,20},{20,16},{24,28},{28,24},{1,5},{5... | collective-permute-start | bytes 184328 | tf_op jit(solution)/shard_map/ppermute | solution.py:462
  55.7 6.5 %collective-permute-start.8 = (f32[16,960]{1,0:T(8,128)S(1)}, f32[16,960]{1,0:T(8,128)S(1)}, u32[]{:S(2)}, u32[]{:S(2)}) collective-permute-start(f32[16,960]{1,0:T(8,128)S(1)} %add.21), channel_id=1, source_target_pairs={{0,16},{4,20},{8,24},{12,28},{16,0},{20,4},{24,8},{28,12},{1,17},{... | collective-permute-start | bytes 184328 | tf_op jit(solution)/shard_map/ppermute | solution.py:462
  63.7 1.5 %collective-permute-start.9 = (f32[24,2048]{1,0:T(8,128)S(1)}, f32[24,2048]{1,0:T(8,128)S(1)}, u32[]{:S(2)}, u32[]{:S(2)}) collective-permute-start(f32[24,2048]{1,0:T(8,128)S(1)} %fields.1), channel_id=1, source_target_pairs={{0,1},{1,0},{2,3},{3,2},{4,5},{5,4},{6,7},{7,6},{8,9},{9,8},{10,11... | collective-permute-start | bytes 589832 | tf_op jit(solution)/shard_map/ppermute | solution.py:462
  65.2 10.6 %collective-permute-start.10 = (f32[24,2048]{1,0:T(8,128)S(1)}, f32[24,2048]{1,0:T(8,128)S(1)}, u32[]{:S(2)}, u32[]{:S(2)}) collective-permute-start(f32[24,2048]{1,0:T(8,128)S(1)} %add.23.mine_ref), channel_id=1, source_target_pairs={{0,2},{1,3},{2,0},{3,1},{4,6},{5,7},{6,4},{7,5},{8,10},{9,11},{10,... | collective-permute-start | bytes 589832 | tf_op jit(solution)/shard_map/ppermute | solution.py:521

commit v7 on v6

--- a/solution.py
+++ b/solution.py
@@ -52,23 +52,12 @@
     return high, low, ((x - high.astype(F32)) - low.astype(F32)).astype(BF)
 
 
-def load_kernel(chans, rows, width, place, *refs):
-    (k, v, others), (near, far, near_big, far_big, v0, *copies) = (refs[0], refs[1], refs[2:7]), refs[7:-1]
-    sems = refs[-1]
-    atoms = v.shape[2]
-    even = place[0] % 2 == 0
-    last = atoms - width
-    near_cols = pl.ds(pl.multiple_of(jnp.where(even, last, 0), 128), width)
-    far_cols = pl.ds(pl.multiple_of(jnp.where(even, 0, last), 128), width)
-    moves = []
-    for piece, cols in ((far, far_cols), (near, near_cols)):
-        moves.append((k.at[:, cols], piece.at[pl.ds(0, rows)]))
-        moves.append((v.at[0, :, cols], piece.at[pl.ds(rows, chans)]))
-    moves.append((k, copies[0]))
-    moves.append((v.at[0], v0))
-    moves += list(zip(others, copies[1:]))
-    for piece, cols in ((far_big, far_cols), (near_big, near_cols)):
-        moves.append((v.at[pl.ds(1, piece.shape[0]), :, cols], piece))
+def columns_of(place, width, atoms, far):
+    first = on_left(place, far)
+    return pl.ds(pl.multiple_of(jnp.where(first, 0, atoms - width), 128), width)
+
+
+def run(moves, sems):
     started = [pltpu.make_async_copy(src, dst, sems.at[i]) for i, (src, dst) in enumerate(moves)]
     for copy in started:
         copy.start()
@@ -76,26 +65,56 @@
         copy.wait()
 
 
-def load_call(place, k, v, others, width):
-    comps, chans, atoms = v.shape
-    rows = k.shape[0]
-    shape = jax.ShapeDtypeStruct
-    outs = [shape((rows + chans, width), BF)] * 2 + [shape((comps - 1, chans, width), BF)] * 2
-    outs += [shape((chans, atoms), BF)] + [shape(x.shape, x.dtype) for x in (k, *others)]
-    return pl.pallas_call(
-        functools.partial(load_kernel, chans, rows, width),
+def piece_kernel(place, k, v, near, far, far_big, sems):
+    rows, atoms = k.shape
+    chans, width = v.shape[1], near.shape[1]
+    moves = []
+    for piece, is_far in ((far, True), (near, False)):
+        cols = columns_of(place, width, atoms, is_far)
+        moves.append((k.at[:, cols], piece.at[pl.ds(0, rows)]))
+        moves.append((v.at[0, :, cols], piece.at[pl.ds(rows, chans)]))
+    moves.append((v.at[pl.ds(1, far_big.shape[0]), :, columns_of(place, width, atoms, True)], far_big))
+    run(moves, sems)
+
+
+def load_kernel(place, v, *refs):
+    others, (near_big, v0, *copies), sems = refs[: (len(refs) - 3) // 2], refs[(len(refs) - 3) // 2 : -1], refs[-1]
+    cols = columns_of(place, near_big.shape[2], v.shape[2], False)
+    run(
+        list(zip(others, copies)) + [(v.at[0], v0), (v.at[pl.ds(1, near_big.shape[0]), :, cols], near_big)],
+        sems,
+    )
+
+
+def copying_call(kernel, place, operands, outs):
+    return pl.pallas_call(
+        kernel,
         grid_spec=pltpu.PrefetchScalarGridSpec(
             num_scalar_prefetch=1,
             grid=(1,),
-            in_specs=[pl.BlockSpec(memory_space=pltpu.HBM)] * (2 + len(others)),
+            in_specs=[pl.BlockSpec(memory_space=pltpu.HBM)] * len(operands),
             out_specs=[pl.BlockSpec(memory_space=pl.ANY)] * len(outs),
-            scratch_shapes=[pltpu.SemaphoreType.DMA((8 + len(others),))],
+            scratch_shapes=[pltpu.SemaphoreType.DMA((8,))],
         ),
         out_shape=outs,
         compiler_params=params(2),
-        cost_estimate=pl.CostEstimate(flops=0, transcendentals=0, bytes_accessed=4 * comps * chans * width),
-        name="load",
-    )(place, *[pltpu.with_memory_space_constraint(x, pltpu.HBM) for x in (k, v, *others)])
+        cost_estimate=pl.CostEstimate(flops=0, transcendentals=0, bytes_accessed=1 << 20),
+    )(place, *[pltpu.with_memory_space_constraint(x, pltpu.HBM) for x in operands])
+
+
+def piece_call(place, k, v, width):
+    comps, chans, _ = v.shape
+    small = jax.ShapeDtypeStruct((k.shape[0] + chans, width), BF)
+    return copying_call(
+        piece_kernel, place, (k, v), [small, small, jax.ShapeDtypeStruct((comps - 1, chans, width), BF)]
+    )
+
+
+def load_call(place, v, others, width):
+    comps, chans, atoms = v.shape
+    shape = jax.ShapeDtypeStruct
+    outs = [shape((comps - 1, chans, width), BF), shape((chans, atoms), BF)] + [shape(x.shape, x.dtype) for x in others]
+    return copying_call(load_kernel, place, (v, *others), outs)
 
 
 def on_left(place, far):
@@ -496,11 +515,12 @@
         return lax.ppermute(x, "seq", pairs)
 
     values = value_states.transpose(1, 0, 2)
-    near, far, near_big, far_big, v0, keys, asked, weight, counts, lists, vectors = load_call(
-        place, key_states.reshape(heads * head_dim, atoms), values,
-        (queries.reshape(heads * head_dim, atoms), charge_weight.T, block_counts, neighbors.T, integer_wave_vectors),
-        width,
-    )
+    keys = key_states.reshape(heads * head_dim, atoms)
+    near, far, far_big = piece_call(place, keys, values, width)
+    near_big, v0, keys, asked, weight, counts, lists = load_call(
+        place, values, (keys, queries.reshape(heads * head_dim, atoms), charge_weight.T, block_counts, neighbors.T), width
+    )
+    vectors = integer_wave_vectors
     far = swap(far, far_pairs)
     near = swap(near, near_pairs)
     far_big = swap(far_big, far_pairs)
@@ -515,25 +535,22 @@
     table, wave_weight = table_call(place, vectors, fractional, planes)
     last = lax.axis_size("inner") // 2
 
-    def halfway(x, name):
-        x = summed(x, "inner", stop=last)
-        x = x.astype(BF) if name == "charge" else x
+    def halfway(x):
+        x = summed(x, "inner", stop=last).astype(BF)
         return x, lax.ppermute(x, "inner", [(i, i ^ last) for i in range(2 * last)])
 
-    mine, theirs = halfway(part, "charge")
+    mine, theirs = halfway(part)
     charges = mine.astype(F32) + theirs.astype(F32)
     structure = structure_call(charges, table.reshape(-1, atoms), inv_root)
-    for step in (2, 1):
-        structure = exchanged(structure, "seq", step)
-    structure = summed(structure, "seq", 4)
+    structure = summed(structure, "seq")
     fields = field_call(place, structure, wave_weight, charges, table, planes)
-    fields, others = halfway(fields, "field")
+    fields, others = halfway(fields)
     potential, forces = finish_call(fields, others, nq)
 
     mix = functools.partial(mix_call, heads=heads, head_dim=head_dim)
     attention = mix("low", lists, place, values, p_in, scale_in, (), None)
+    attention = mix("far", lists, place, values, p_out, scale_out, (far, far_big), attention)
     attention = mix("high", lists, place, values, p_in, scale_in, (), attention)
-    attention = mix("far", lists, place, values, p_out, scale_out, (far, far_big), attention)
     attention = mix("near", lists, place, values, p_out, scale_out, (near, near_big), attention)
     return (attention.transpose(1, 0, 2), potential, forces)
 

time: 76.7 us -> 74.3 us (0.969)
  starting transfers between devices: 18.4 us -> 15.6 us
  Pallas kernels: 25.1 us -> 26.6 us
  waiting for transfers between devices: 32 us -> 30.6 us
    ppermute x5, waiting for transfers between devices: 32 us -> 12.4 us  [exchanged(): return x + lax.ppermute(x, axis, [(i, i ^ step) for i in range(size)])]
    ppermute x4, waiting for transfers between devices: 0.01 us -> 16.7 us  [swap(): return lax.ppermute(x, 'seq', pairs)]
    ppermute x5, starting transfers between devices: 8.13 us -> 4.91 us  [exchanged(): return x + lax.ppermute(x, axis, [(i, i ^ step) for i in range(size)])]
    pallas_call x1 -> x2, Pallas kernels: 2.34 us -> 3.83 us  [copying_call(): pl.pallas_call(kernel, grid_spec=pltpu.PrefetchScalarGridSpec(num_scalar_...]
    ppermute x2, waiting for transfers between devices: 0.01 us -> 1.4 us  [halfway(): lax.ppermute(x, 'inner', [(i, i ^ last) for i in range(2 * last)])]
    ppermute x2, starting transfers between devices: 2.15 us -> 3.44 us  [halfway(): lax.ppermute(x, 'inner', [(i, i ^ last) for i in range(2 * last)])]
    ppermute x4, starting transfers between devices: 8.16 us -> 7.26 us  [swap(): return lax.ppermute(x, 'seq', pairs)]
  transfers between devices with their start and end apart: 11 -> 11, of which waited for: 5 -> 8; matrix products, arithmetic and copies ran while one was open for 0% -> 0% of each run, Pallas kernels for 24% -> 23%
where the time goes in v7:
time: 74.3 us; the launch traced here: 73.7 us
  waiting for transfers between devices  30.6 us (41%)
  Pallas kernels  26.6 us (36%)
  starting transfers between devices  15.6 us (21%)
  between operations  0.75 us (1%)
    ppermute x4, waiting for transfers between devices, swap(): return lax.ppermute(x, 'seq', pairs)  16.7 us
    ppermute x5, waiting for transfers between devices, exchanged(): return x + lax.ppermute(x, axis, [(i, i ^ step) for i in range(size)])  12.4 us
    pallas_call x4, Pallas kernels, mix_call(): pl.pallas_call(functools.partial(mix_kernel, heads, head_dim, chans // he...  10 us
    ppermute x4, starting transfers between devices, swap(): return lax.ppermute(x, 'seq', pairs)  7.26 us
    pallas_call x2, Pallas kernels, scores_call(): pl.pallas_call(functools.partial(score_kernel, heads, head_dim, head_chan...  7.1 us
    ppermute x5, starting transfers between devices, exchanged(): return x + lax.ppermute(x, axis, [(i, i ^ step) for i in range(size)])  4.91 us
    pallas_call x2, Pallas kernels, copying_call(): pl.pallas_call(kernel, grid_spec=pltpu.PrefetchScalarGridSpec(num_scalar_...  3.83 us
    ppermute x2, starting transfers between devices, halfway(): lax.ppermute(x, 'inner', [(i, i ^ last) for i in range(2 * last)])  3.44 us
  transfers between devices with their start and end apart: 11, of which 8 were waited for; matrix products, arithmetic and copies ran while one was open for 0% of the time, Pallas kernels for 23%

profile of v7, /device:TPU:0, one launch (start us, length us, event | category | flops | bytes accessed | tf_op | source)
XLA Modules:
  0.0 73.7 jit_solution(10176672379988023581)
XLA Ops:
  0.6 0.1 pad_add_fusion.place
  0.7 1.8 %shard_map.104 = (bf16[64,512]{1,0:T(8,128)(2,1)S(1)}, bf16[64,512]{1,0:T(8,128)(2,1)S(1)}, bf16[24,32,512]{2,1,0:T(8,128)(2,1)S(1)}) custom-call(s32[2]{0:T(128)S(1)} %pad_add_fusion.place, bf16[32,2048]{1,0:T(8,128)(2,1)} %bitcast.17, bf16[25,32,2048]{2,1,0:T(8,128)(2,1)} %bitcast.9), custom_call_target="tpu_custom_call" | custom-call | bytes 1048576 | tf_op jit(solution)/shard_map/pallas_call | solution.py:90
  2.5 0.7 collective-permute-start
  3.2 5.8 %collective-permute-start.1 = (bf16[64,512]{1,0:T(8,128)(2,1)S(1)}, bf16[64,512]{1,0:T(8,128)(2,1)S(1)}, u32[]{:S(2)}, u32[]{:S(2)}) collective-permute-start(bf16[64,512]{1,0:T(8,128)(2,1)S(1)} %get-tuple-element.30), channel_id=1, source_target_pairs={{0,4},{4,0},{8,12},{12,8},{16,20},{20,16},{24,28},{28,24},{1,5},{5... | collective-permute-start | bytes 196616 | tf_op jit(solution)/shard_map/ppermute | solution.py:515
  9.0 2.0 %shard_map.103 = (bf16[24,32,512]{2,1,0:T(8,128)(2,1)S(1)}, bf16[32,2048]{1,0:T(8,128)(2,1)S(1)}, bf16[32,2048]{1,0:T(8,128)(2,1)S(1)}, bf16[32,2048]{1,0:T(8,12...) custom-call(s32[2]{0:T(128)S(1)} %pad_add_fusion.place, ...), custom_call_target="tpu_custom_call" | custom-call | bytes 1048576 | tf_op jit(solution)/shard_map/pallas_call | solution.py:90
  11.0 0.0 copy-start.1
  11.1 3.5 %shard_map.105 = (bf16[4,2,768,256]{3,2,1,0:T(8,128)(2,1)S(1)}, f32[4,2,256]{2,1,0:T(2,128)S(1)}, f32[16,2048]{1,0:T(8,128)S(1)}) custom-call(s32[3,8]{1,0:T(4,128)S(1)} %get-tuple-element.23.lists, s32[64]{0:T(128)S(1)} %get-tuple-element.24.counts, s32[2]{0:T(128)S(1)} %pad_add_fusion.place, bf16[32,2048]{1,0:T(8,128)(2,1)S(1)} %get-tuple-element.25.refs_0_, ...), custom_call_target="tpu_custom_call" | custom-call | flops 314572800 | bytes 3145728 | tf_op jit(solution)/shard_map/pallas_call | solution.py:212
  14.6 3.6 %shard_map.106 = (bf16[4,2,768,256]{3,2,1,0:T(8,128)(2,1)S(1)}, f32[4,2,256]{2,1,0:T(2,128)S(1)}, f32[16,2048]{1,0:T(8,128)S(1)}) custom-call(s32[3,8]{1,0:T(4,128)S(1)} %get-tuple-element.23.lists, s32[64]{0:T(128)S(1)} %get-tuple-element.24.counts, s32[2]{0:T(128)S(1)} %pad_add_fusion.place, bf16[32,2048]{1,0:T(8,128)(2,1)S(1)} %get-tuple-element.25.refs_0_, ...), custom_call_target="tpu_custom_call" | custom-call | flops 314572800 | bytes 3145728 | tf_op jit(solution)/shard_map/pallas_call | solution.py:212
  18.2 1.4 %collective-permute-done.4 = f32[16,2048]{1,0:T(8,128)S(1)} collective-permute-done((f32[16,2048]{1,0:T(8,128)S(1)}, f32[16,2048]{1,0:T(8,128)S(1)}, u32[]{:S(2)}, u32[]{:S(2)}) %collective-permute-start.4) | collective-permute-done | bytes 131104 | tf_op jit(solution)/shard_map/ppermute | solution.py:481
  19.6 1.6 %collective-permute-start.5 = (bf16[16,2048]{1,0:T(8,128)(2,1)S(1)}, bf16[16,2048]{1,0:T(8,128)(2,1)S(1)}, u32[]{:S(2)}, u32[]{:S(2)}) collective-permute-start(bf16[16,2048]{1,0:T(8,128)(2,1)S(1)} %add_convert_fusion.1), channel_id=1, source_target_pairs={{0,2},{1,3},{2,0},{3,1},{4,6},{5,7},{6,4},{7,5},{8,10},{9,11},{10,... | collective-permute-start | bytes 196616 | tf_op jit(solution)/shard_map/ppermute | solution.py:540
  21.1 2.1 %table.1 = (bf16[2,480,2048]{2,1,0:T(8,128)(2,1)S(1)}, f32[1,480]{1,0:T(1,128)S(1)}) custom-call(s32[2]{0:T(128)S(1)} %pad_add_fusion.place, s32[3,2048]{1,0:T(4,128)S(1)} %copy-done.1, f32[3,2048]{1,0:T(4,128)S(1)} %copy-done.2), custom_call_target="tpu_custom_call" | custom-call | flops 39321600 | bytes 3932160 | tf_op jit(solution)/shard_map/table/pallas_call | solution.py:380
  23.3 0.6 collective-permute-done.5
  23.9 1.4 %structure.1 = f32[16,960]{1,0:T(8,128)S(1)} custom-call(f32[16,2048]{1,0:T(8,128)S(1)} %convert_add_fusion.c_ref, bf16[960,2048]{1,0:T(8,128)(2,1)S(1)} %bitcast.15), custom_call_target="tpu_custom_call" | custom-call | flops 1006632960 | bytes 3932160 | tf_op jit(solution)/shard_map/structure/pallas_call | solution.py:408
  25.3 0.1 collective-permute-start.6
  25.4 4.2 %collective-permute-done.6 = f32[16,960]{1,0:T(8,128)S(1)} collective-permute-done((f32[16,960]{1,0:T(8,128)S(1)}, f32[16,960]{1,0:T(8,128)S(1)}, u32[]{:S(2)}, u32[]{:S(2)}) %collective-permute-start.6) | collective-permute-done | bytes 61472 | tf_op jit(solution)/shard_map/ppermute | solution.py:481
  29.6 1.6 %collective-permute-start.7 = (f32[16,960]{1,0:T(8,128)S(1)}, f32[16,960]{1,0:T(8,128)S(1)}, u32[]{:S(2)}, u32[]{:S(2)}) collective-permute-start(f32[16,960]{1,0:T(8,128)S(1)} %add.20), channel_id=1, source_target_pairs={{0,8},{4,12},{8,0},{12,4},{16,24},{20,28},{24,16},{28,20},{1,9},{5... | collective-permute-start | bytes 184328 | tf_op jit(solution)/shard_map/ppermute | solution.py:481
  31.3 2.7 %collective-permute-done.7 = f32[16,960]{1,0:T(8,128)S(1)} collective-permute-done((f32[16,960]{1,0:T(8,128)S(1)}, f32[16,960]{1,0:T(8,128)S(1)}, u32[]{:S(2)}, u32[]{:S(2)}) %collective-permute-start.7) | collective-permute-done | bytes 61472 | tf_op jit(solution)/shard_map/ppermute | solution.py:481
  34.0 3.1 %collective-permute-start.8 = (f32[16,960]{1,0:T(8,128)S(1)}, f32[16,960]{1,0:T(8,128)S(1)}, u32[]{:S(2)}, u32[]{:S(2)}) collective-permute-start(f32[16,960]{1,0:T(8,128)S(1)} %add.21), channel_id=1, source_target_pairs={{0,16},{4,20},{8,24},{12,28},{16,0},{20,4},{24,8},{28,12},{1,17},{... | collective-permute-start | bytes 184328 | tf_op jit(solution)/shard_map/ppermute | solution.py:481
  37.1 0.7 collective-permute-start.3
  37.8 2.8 %collective-permute-done.8 = f32[16,960]{1,0:T(8,128)S(1)} collective-permute-done((f32[16,960]{1,0:T(8,128)S(1)}, f32[16,960]{1,0:T(8,128)S(1)}, u32[]{:S(2)}, u32[]{:S(2)}) %collective-permute-start.8) | collective-permute-done | bytes 61472 | tf_op jit(solution)/shard_map/ppermute | solution.py:481
  40.6 1.5 %fields.1 = f32[24,2048]{1,0:T(8,128)S(1)} custom-call(s32[2]{0:T(128)S(1)} %pad_add_fusion.place, f32[16,960]{1,0:T(8,128)S(1)} %add.22.s_ref, f32[1,480]{1,0:T(1,128)S(1)} %get-tuple-element.40.weight_ref, f32[16,2048]{1,0:T(8,128)S(1)} %convert_add_fusion.c_ref, bf16[2,480,2048]{2,1,0:T(8,128)(2,1)S(1)} %get-tuple-element.39.t_ref), custom_call_target="tpu_custom_call" | custom-call | flops 503316480 | bytes 1966080 | tf_op jit(solution)/shard_map/fields/pallas_call | solution.py:445
  42.1 0.1 collective-permute-start.9
  42.2 0.1 collective-permute-start.2
  42.3 1.3 %collective-permute-done.9 = f32[24,2048]{1,0:T(8,128)S(1)} collective-permute-done((f32[24,2048]{1,0:T(8,128)S(1)}, f32[24,2048]{1,0:T(8,128)S(1)}, u32[]{:S(2)}, u32[]{:S(2)}) %collective-permute-start.9) | collective-permute-done | bytes 196640 | tf_op jit(solution)/shard_map/ppermute | solution.py:481
  43.7 1.9 %collective-permute-start.10 = (bf16[24,2048]{1,0:T(8,128)(2,1)S(1)}, bf16[24,2048]{1,0:T(8,128)(2,1)S(1)}, u32[]{:S(2)}, u32[]{:S(2)}) collective-permute-start(bf16[24,2048]{1,0:T(8,128)(2,1)S(1)} %add_convert_fusion.mine_ref), channel_id=1, source_target_pairs={{0,2},{1,3},{2,0},{3,1},{4,6},{5,7},{6,4},{7,5},{8,10},{9,11},{10,... | collective-permute-start | bytes 294920 | tf_op jit(solution)/shard_map/ppermute | solution.py:540
  45.5 2.3 %shard_map.107.refs_2_ = bf16[25,32,2048]{2,1,0:T(8,128)(2,1)} custom-call(s32[3,8]{1,0:T(4,128)S(1)} %get-tuple-element.23.lists, s32[2]{0:T(128)S(1)} %pad_add_fusion.place, bf16[25,32,2048]{2,1,0:T(8,128)(2,1)S(1)} %bitcast.11, bf16[4,2,768,256]{3,2,1,0:T(8,128)(2,1)S(1)} %get-tuple-element.35.p_ref, f32[4,2,256]{2,1,0:T(2,128)S(1)} %get-tuple-element.36.scale_ref), custom_call_target="tpu_custom_call" | custom-call | flops 629145600 | bytes 3276800 | tf_op jit(solution)/shard_map/pallas_call | solution.py:288
  47.9 0.8 %collective-permute-done.10.theirs_ref = bf16[24,2048]{1,0:T(8,128)(2,1)S(1)} collective-permute-done((bf16[24,2048]{1,0:T(8,128)(2,1)S(1)}, bf16[24,2048]{1,0:T(8,128)(2,1)S(1)}, u32[]{:S(2)}, u32[]{:S(2)}) %collective-permute-start.10) | collective-permute-done | bytes 98336 | tf_op jit(solution)/shard_map/ppermute | solution.py:540
  48.6 0.7 finish.1
  49.3 2.7 %shard_map.108.refs_0_ = bf16[25,32,2048]{2,1,0:T(8,128)(2,1)} custom-call(s32[3,8]{1,0:T(4,128)S(1)} %get-tuple-element.23.lists, s32[2]{0:T(128)S(1)} %pad_add_fusion.place, bf16[25,32,2048]{2,1,0:T(8,128)(2,1)S(1)} %bitcast.12, bf16[4,2,768,256]{3,2,1,0:T(8,128)(2,1)S(1)} %get-tuple-element.32.p_ref, ...), custom_call_target="tpu_custom_call", output_to_operand_aliasing={{}: (7, {})} | custom-call | flops 629145600 | bytes 3276800 | tf_op jit(solution)/shard_map/pallas_call | solution.py:288
  52.0 2.3 %shard_map.109.refs_2_ = bf16[25,32,2048]{2,1,0:T(8,128)(2,1)} custom-call(s32[3,8]{1,0:T(4,128)S(1)} %get-tuple-element.23.lists, s32[2]{0:T(128)S(1)} %pad_add_fusion.place, bf16[25,32,2048]{2,1,0:T(8,128)(2,1)S(1)} %bitcast.13, bf16[4,2,768,256]{3,2,1,0:T(8,128)(2,1)S(1)} %get-tuple-element.35.p_ref, ...), custom_call_target="tpu_custom_call", output_to_operand_aliasing={{}: (5, {})} | custom-call | flops 629145600 | bytes 3276800 | tf_op jit(solution)/shard_map/pallas_call | solution.py:288
  54.3 16.7 %collective-permute-done.2.refs_1_ = bf16[24,32,512]{2,1,0:T(8,128)(2,1)S(1)} collective-permute-done((bf16[24,32,512]{2,1,0:T(8,128)(2,1)S(1)}, bf16[24,32,512]{2,1,0:T(8,128)(2,1)S(1)}, u32[]{:S(2)}, u32[]{:S(2)}) %collective-permute-start.2) | collective-permute-done | bytes 786464 | tf_op jit(solution)/shard_map/ppermute | solution.py:515
  71.0 2.7 %shard_map.110 = bf16[25,32,2048]{2,1,0:T(8,128)(2,1)} custom-call(s32[3,8]{1,0:T(4,128)S(1)} %get-tuple-element.23.lists, s32[2]{0:T(128)S(1)} %pad_add_fusion.place, bf16[25,32,2048]{2,1,0:T(8,128)(2,1)S(1)} %bitcast.14, bf16[4,2,768,256]{3,2,1,0:T(8,128)(2,1)S(1)} %get-tuple-element.32.p_ref, ...), custom_call_target="tpu_custom_call", output_to_operand_aliasing={{}: (7, {})} | custom-call | flops 629145600 | bytes 3276800 | tf_op jit(solution)/shard_map/pallas_call | solution.py:288
  (15 shorter events, 0.1 us)
Async XLA Ops:
  2.5 12.1 %collective-permute-start = (bf16[64,512]{1,0:T(8,128)(2,1)S(1)}, bf16[64,512]{1,0:T(8,128)(2,1)S(1)}, u32[]{:S(2)}, u32[]{:S(2)}) collective-permute-start(bf16[64,512]{1,0:T(8,128)(2,1)S(1)} %get-tuple-element.29), channel_id=1, source_target_pairs={{4,8},{8,4},{12,16},{16,12},{20,24},{24,20},{5,9},{9,5},{13,17},{1... | collective-permute-start | bytes 196616 | tf_op jit(solution)/shard_map/ppermute | solution.py:515
  3.2 11.4 %collective-permute-start.1 = (bf16[64,512]{1,0:T(8,128)(2,1)S(1)}, bf16[64,512]{1,0:T(8,128)(2,1)S(1)}, u32[]{:S(2)}, u32[]{:S(2)}) collective-permute-start(bf16[64,512]{1,0:T(8,128)(2,1)S(1)} %get-tuple-element.30), channel_id=1, source_target_pairs={{0,4},{4,0},{8,12},{12,8},{16,20},{20,16},{24,28},{28,24},{1,5},{5... | collective-permute-start | bytes 196616 | tf_op jit(solution)/shard_map/ppermute | solution.py:515
  11.0 10.1 %copy-start.1 = (s32[3,2048]{1,0:T(4,128)S(1)}, s32[3,2048]{1,0:T(4,128)}, u32[]{:S(2)}) copy-start(s32[3,2048]{1,0:T(4,128)} %n_ref.1) | copy-start | bytes 73732
  11.1 10.1 %copy-start.2 = (f32[3,2048]{1,0:T(4,128)S(1)}, f32[3,2048]{1,0:T(4,128)}, u32[]{:S(2)}) copy-start(f32[3,2048]{1,0:T(4,128)} %f_ref.1) | copy-start | bytes 73732
  18.2 1.4 %collective-permute-start.4 = (f32[16,2048]{1,0:T(8,128)S(1)}, f32[16,2048]{1,0:T(8,128)S(1)}, u32[]{:S(2)}, u32[]{:S(2)}) collective-permute-start(f32[16,2048]{1,0:T(8,128)S(1)} %get-tuple-element.38), channel_id=1, source_target_pairs={{0,1},{1,0},{2,3},{3,2},{4,5},{5,4},{6,7},{7,6},{8,9},{9,8},{10,11... | collective-permute-start | bytes 393224 | tf_op jit(solution)/shard_map/ppermute | solution.py:481
  19.6 4.3 %collective-permute-start.5 = (bf16[16,2048]{1,0:T(8,128)(2,1)S(1)}, bf16[16,2048]{1,0:T(8,128)(2,1)S(1)}, u32[]{:S(2)}, u32[]{:S(2)}) collective-permute-start(bf16[16,2048]{1,0:T(8,128)(2,1)S(1)} %add_convert_fusion.1), channel_id=1, source_target_pairs={{0,2},{1,3},{2,0},{3,1},{4,6},{5,7},{6,4},{7,5},{8,10},{9,11},{10,... | collective-permute-start | bytes 196616 | tf_op jit(solution)/shard_map/ppermute | solution.py:540
  25.3 20.2 %copy-start = (bf16[32,25,2048]{2,0,1:T(8,128)(2,1)S(1)}, bf16[32,25,2048]{2,0,1:T(8,128)(2,1)}, u32[]{:S(2)}) copy-start(bf16[32,25,2048]{2,0,1:T(8,128)(2,1)} %param.10) | copy-start | bytes 9830404
  25.3 4.3 %collective-permute-start.6 = (f32[16,960]{1,0:T(8,128)S(1)}, f32[16,960]{1,0:T(8,128)S(1)}, u32[]{:S(2)}, u32[]{:S(2)}) collective-permute-start(f32[16,960]{1,0:T(8,128)S(1)} %structure.1), channel_id=1, source_target_pairs={{0,4},{4,0},{8,12},{12,8},{16,20},{20,16},{24,28},{28,24},{1,5},{5... | collective-permute-start | bytes 184328 | tf_op jit(solution)/shard_map/ppermute | solution.py:481
  29.6 4.3 %collective-permute-start.7 = (f32[16,960]{1,0:T(8,128)S(1)}, f32[16,960]{1,0:T(8,128)S(1)}, u32[]{:S(2)}, u32[]{:S(2)}) collective-permute-start(f32[16,960]{1,0:T(8,128)S(1)} %add.20), channel_id=1, source_target_pairs={{0,8},{4,12},{8,0},{12,4},{16,24},{20,28},{24,16},{28,20},{1,9},{5... | collective-permute-start | bytes 184328 | tf_op jit(solution)/shard_map/ppermute | solution.py:481
  34.0 6.6 %collective-permute-start.8 = (f32[16,960]{1,0:T(8,128)S(1)}, f32[16,960]{1,0:T(8,128)S(1)}, u32[]{:S(2)}, u32[]{:S(2)}) collective-permute-start(f32[16,960]{1,0:T(8,128)S(1)} %add.21), channel_id=1, source_target_pairs={{0,16},{4,20},{8,24},{12,28},{16,0},{20,4},{24,8},{28,12},{1,17},{... | collective-permute-start | bytes 184328 | tf_op jit(solution)/shard_map/ppermute | solution.py:481
  37.1 12.2 %collective-permute-start.3 = (bf16[24,32,512]{2,1,0:T(8,128)(2,1)S(1)}, bf16[24,32,512]{2,1,0:T(8,128)(2,1)S(1)}, u32[]{:S(2)}, u32[]{:S(2)}) collective-permute-start(bf16[24,32,512]{2,1,0:T(8,128)(2,1)S(1)} %get-tuple-element.37), channel_id=1, source_target_pairs={{4,8},{8,4},{12,16},{16,12},{20,24},{24,20},{5,9},{9,5},{13,17},{1... | collective-permute-start | bytes 2359304 | tf_op jit(solution)/shard_map/ppermute | solution.py:515
  42.1 1.5 %collective-permute-start.9 = (f32[24,2048]{1,0:T(8,128)S(1)}, f32[24,2048]{1,0:T(8,128)S(1)}, u32[]{:S(2)}, u32[]{:S(2)}) collective-permute-start(f32[24,2048]{1,0:T(8,128)S(1)} %fields.1), channel_id=1, source_target_pairs={{0,1},{1,0},{2,3},{3,2},{4,5},{5,4},{6,7},{7,6},{8,9},{9,8},{10,11... | collective-permute-start | bytes 589832 | tf_op jit(solution)/shard_map/ppermute | solution.py:481
  42.2 28.8 %collective-permute-start.2 = (bf16[24,32,512]{2,1,0:T(8,128)(2,1)S(1)}, bf16[24,32,512]{2,1,0:T(8,128)(2,1)S(1)}, u32[]{:S(2)}, u32[]{:S(2)}) collective-permute-start(bf16[24,32,512]{2,1,0:T(8,128)(2,1)S(1)} %get-tuple-element.34), channel_id=1, source_target_pairs={{0,4},{4,0},{8,12},{12,8},{16,20},{20,16},{24,28},{28,24},{1,5},{5... | collective-permute-start | bytes 2359304 | tf_op jit(solution)/shard_map/ppermute | solution.py:515
  43.7 5.0 %collective-permute-start.10 = (bf16[24,2048]{1,0:T(8,128)(2,1)S(1)}, bf16[24,2048]{1,0:T(8,128)(2,1)S(1)}, u32[]{:S(2)}, u32[]{:S(2)}) collective-permute-start(bf16[24,2048]{1,0:T(8,128)(2,1)S(1)} %add_convert_fusion.mine_ref), channel_id=1, source_target_pairs={{0,2},{1,3},{2,0},{3,1},{4,6},{5,7},{6,4},{7,5},{8,10},{9,11},{10,... | collective-permute-start | bytes 294920 | tf_op jit(solution)/shard_map/ppermute | solution.py:540

commit v8 on v7

--- a/solution.py
+++ b/solution.py
@@ -65,7 +65,8 @@
         copy.wait()
 
 
-def piece_kernel(place, k, v, near, far, far_big, sems):
+def load_kernel(place, k, v, *refs):
+    others, (near, far, far_big, v0, *copies), sems = refs[: (len(refs) - 6) // 2], refs[(len(refs) - 6) // 2 : -1], refs[-1]
     rows, atoms = k.shape
     chans, width = v.shape[1], near.shape[1]
     moves = []
@@ -73,48 +74,31 @@
         cols = columns_of(place, width, atoms, is_far)
         moves.append((k.at[:, cols], piece.at[pl.ds(0, rows)]))
         moves.append((v.at[0, :, cols], piece.at[pl.ds(rows, chans)]))
+    moves += list(zip((k, *others), copies)) + [(v.at[0], v0)]
     moves.append((v.at[pl.ds(1, far_big.shape[0]), :, columns_of(place, width, atoms, True)], far_big))
     run(moves, sems)
 
 
-def load_kernel(place, v, *refs):
-    others, (near_big, v0, *copies), sems = refs[: (len(refs) - 3) // 2], refs[(len(refs) - 3) // 2 : -1], refs[-1]
-    cols = columns_of(place, near_big.shape[2], v.shape[2], False)
-    run(
-        list(zip(others, copies)) + [(v.at[0], v0), (v.at[pl.ds(1, near_big.shape[0]), :, cols], near_big)],
-        sems,
-    )
-
-
-def copying_call(kernel, place, operands, outs):
-    return pl.pallas_call(
-        kernel,
+def load_call(place, k, v, others, width):
+    comps, chans, atoms = v.shape
+    shape = jax.ShapeDtypeStruct
+    outs = [shape((k.shape[0] + chans, width), BF)] * 2 + [shape((comps - 1, chans, width), BF)]
+    outs += [shape((chans, atoms), BF)] + [shape(x.shape, x.dtype) for x in (k, *others)]
+    operands = (k, v, *others)
+    return pl.pallas_call(
+        load_kernel,
         grid_spec=pltpu.PrefetchScalarGridSpec(
             num_scalar_prefetch=1,
             grid=(1,),
             in_specs=[pl.BlockSpec(memory_space=pltpu.HBM)] * len(operands),
             out_specs=[pl.BlockSpec(memory_space=pl.ANY)] * len(outs),
-            scratch_shapes=[pltpu.SemaphoreType.DMA((8,))],
+            scratch_shapes=[pltpu.SemaphoreType.DMA((7 + len(others),))],
         ),
         out_shape=outs,
         compiler_params=params(2),
         cost_estimate=pl.CostEstimate(flops=0, transcendentals=0, bytes_accessed=1 << 20),
+        name="load",
     )(place, *[pltpu.with_memory_space_constraint(x, pltpu.HBM) for x in operands])
-
-
-def piece_call(place, k, v, width):
-    comps, chans, _ = v.shape
-    small = jax.ShapeDtypeStruct((k.shape[0] + chans, width), BF)
-    return copying_call(
-        piece_kernel, place, (k, v), [small, small, jax.ShapeDtypeStruct((comps - 1, chans, width), BF)]
-    )
-
-
-def load_call(place, v, others, width):
-    comps, chans, atoms = v.shape
-    shape = jax.ShapeDtypeStruct
-    outs = [shape((comps - 1, chans, width), BF), shape((chans, atoms), BF)] + [shape(x.shape, x.dtype) for x in others]
-    return copying_call(load_kernel, place, (v, *others), outs)
 
 
 def on_left(place, far):
@@ -129,7 +113,15 @@
 
 def score_kernel(heads, head_dim, head_chan, blocks, part, lists, counts, place, *refs):
     q_ref, k_ref, v_ref, cw_ref = refs[:4]
-    sides, (p_ref, scale_ref, charge_ref, kaug, v0) = refs[4:-5], refs[-5:]
+    if part == "interior":
+        sides = ()
+        values, p_ref, scale_ref, charge_ref, near_big, kaug, v0, sems = refs[4:]
+        atoms, width = values.shape[2], near_big.shape[2]
+        cut = values.at[pl.ds(1, near_big.shape[0]), :, columns_of(place, width, atoms, False)]
+        cutting = pltpu.make_async_copy(cut, near_big, sems.at[0])
+        cutting.start()
+    else:
+        sides, (p_ref, scale_ref, charge_ref, kaug, v0) = refs[4:7], refs[7:]
     first = place[0] * blocks
     total = counts.shape[0]
     lane = lax.broadcasted_iota(jnp.int32, (16, BS), 1)
@@ -198,6 +190,8 @@
         charge = term if h == 0 else charge + term
         if h == heads - 1:
             charge_ref[:, columns(g)] = charge
+    if part == "interior":
+        cutting.wait()
 
 
 def scores_call(part, lists, counts, place, q, k, v0, cw, sides, heads, head_dim):
@@ -209,19 +203,25 @@
     steps = blocks - 2 * REACH if part == "interior" else 2 * REACH
     whole = lambda shape: pl.BlockSpec(shape, lambda g, *_: (0,) * len(shape), pipeline_mode=pl.Buffered(1))
     shapes = [((steps, heads, NNB * BS, BS), BF), ((steps, heads, BS), F32), ((nq, atoms), F32)]
+    interior = part == "interior"
+    cuts = [((sides[0].shape[0] - 1, chans, REACH * BS), BF)] if interior else []
+    if interior:
+        sides = [pltpu.with_memory_space_constraint(x, pltpu.HBM) for x in sides]
     return pl.pallas_call(
         functools.partial(score_kernel, heads, head_dim, head_chan, blocks, part),
         grid_spec=pltpu.PrefetchScalarGridSpec(
             num_scalar_prefetch=3,
             grid=(1,),
-            in_specs=[whole(x.shape) for x in (q, k, v0, cw, *sides)],
-            out_specs=[whole(shape) for shape, _ in shapes],
+            in_specs=[whole(x.shape) for x in (q, k, v0, cw)]
+            + [pl.BlockSpec(memory_space=pltpu.HBM) if interior else whole(x.shape) for x in sides],
+            out_specs=[whole(shape) for shape, _ in shapes] + [pl.BlockSpec(memory_space=pl.ANY)] * len(cuts),
             scratch_shapes=[
                 pltpu.VMEM((band, heads, 3 * head_dim + 16, BS), BF),
                 pltpu.VMEM((band, heads, head_chan + 16, BS), BF),
-            ],
-        ),
-        out_shape=[jax.ShapeDtypeStruct(*x) for x in shapes],
+            ]
+            + [pltpu.SemaphoreType.DMA((1,))] * len(cuts),
+        ),
+        out_shape=[jax.ShapeDtypeStruct(*x) for x in shapes + cuts],
         compiler_params=params(16),
         cost_estimate=pl.CostEstimate(
             flops=steps * heads * NNB * BS * BS * 200, transcendentals=steps * heads * NNB * BS * BS,
@@ -516,19 +516,19 @@
 
     values = value_states.transpose(1, 0, 2)
     keys = key_states.reshape(heads * head_dim, atoms)
-    near, far, far_big = piece_call(place, keys, values, width)
-    near_big, v0, keys, asked, weight, counts, lists = load_call(
-        place, values, (keys, queries.reshape(heads * head_dim, atoms), charge_weight.T, block_counts, neighbors.T), width
+    asked = queries.reshape(heads * head_dim, atoms)
+    near, far, far_big, v0, keys, asked, weight, counts, lists = load_call(
+        place, keys, values, (asked, charge_weight.T, block_counts, neighbors.T), width
     )
     vectors = integer_wave_vectors
     far = swap(far, far_pairs)
     near = swap(near, near_pairs)
     far_big = swap(far_big, far_pairs)
+
+    p_in, scale_in, part, near_big = scores_call(
+        "interior", lists, counts, place, asked, keys, v0, weight, (values,), heads, head_dim
+    )
     near_big = swap(near_big, near_pairs)
-
-    p_in, scale_in, part = scores_call(
-        "interior", lists, counts, place, asked, keys, v0, weight, (), heads, head_dim
-    )
     p_out, scale_out, part = scores_call(
         "edges", lists, counts, place, asked, keys, v0, weight, (far, near, part), heads, head_dim
     )

time: 74.3 us -> 73.6 us (level)
    pallas_call x2 -> x1, Pallas kernels: 3.83 us -> 2.08 us  [load_call(): pl.pallas_call(load_kernel, grid_spec=pltpu.PrefetchScalarGridSpec(num_sc...]
    pallas_call x2, Pallas kernels: 7.1 us -> 8.12 us  [scores_call(): pl.pallas_call(functools.partial(score_kernel, heads, head_dim, head_chan...]
  transfers between devices with their start and end apart: 11 -> 11, of which waited for: 8 -> 8; matrix products, arithmetic and copies ran while one was open for 0% -> 0% of each run, Pallas kernels for 23% -> 22%
where the time goes in v8:
time: 73.6 us; the launch traced here: 73 us
  waiting for transfers between devices  30.5 us (41%)
  Pallas kernels  25.9 us (35%)
  starting transfers between devices  15.7 us (21%)
  between operations  0.75 us (1%)
    ppermute x4, waiting for transfers between devices, swap(): return lax.ppermute(x, 'seq', pairs)  16.7 us
    ppermute x5, waiting for transfers between devices, exchanged(): return x + lax.ppermute(x, axis, [(i, i ^ step) for i in range(size)])  12.4 us
    pallas_call x4, Pallas kernels, mix_call(): pl.pallas_call(functools.partial(mix_kernel, heads, head_dim, chans // he...  10 us
    pallas_call x2, Pallas kernels, scores_call(): pl.pallas_call(functools.partial(score_kernel, heads, head_dim, head_chan...  8.12 us
    ppermute x4, starting transfers between devices, swap(): return lax.ppermute(x, 'seq', pairs)  7.26 us
    ppermute x5, starting transfers between devices, exchanged(): return x + lax.ppermute(x, axis, [(i, i ^ step) for i in range(size)])  4.97 us
    ppermute x2, starting transfers between devices, halfway(): lax.ppermute(x, 'inner', [(i, i ^ last) for i in range(2 * last)])  3.43 us
    pallas_call x1, Pallas kernels, table_call(): pl.pallas_call(functools.partial(table_kernel, planes, step), grid_spec=p...  2.13 us
  transfers between devices with their start and end apart: 11, of which 8 were waited for; matrix products, arithmetic and copies ran while one was open for 0% of the time, Pallas kernels for 22%

profile of v8, /device:TPU:0, one launch (start us, length us, event | category | flops | bytes accessed | tf_op | source)
XLA Modules:
  0.0 73.0 jit_solution(2796835305573535017)
XLA Ops:
  0.6 0.1 pad_add_fusion.place
  0.7 2.1 %load.1 = (bf16[64,512]{1,0:T(8,128)(2,1)S(1)}, bf16[64,512]{1,0:T(8,128)(2,1)S(1)}, bf16[24,32,512]{2,1,0:T(8,128)(2,1)S(1)}, bf16[32,2048]{1,0:T(8,128)(2,1)S(...) custom-call(s32[2]{0:T(128)S(1)} %pad_add_fusion.place, ...), custom_call_target="tpu_custom_call" | custom-call | bytes 1048576 | tf_op jit(solution)/shard_map/load/pallas_call | solution.py:88
  2.8 0.7 collective-permute-start
  3.5 5.8 %collective-permute-start.1 = (bf16[64,512]{1,0:T(8,128)(2,1)S(1)}, bf16[64,512]{1,0:T(8,128)(2,1)S(1)}, u32[]{:S(2)}, u32[]{:S(2)}) collective-permute-start(bf16[64,512]{1,0:T(8,128)(2,1)S(1)} %get-tuple-element.30), channel_id=1, source_target_pairs={{0,4},{4,0},{8,12},{12,8},{16,20},{20,16},{24,28},{28,24},{1,5},{5... | collective-permute-start | bytes 196616 | tf_op jit(solution)/shard_map/ppermute | solution.py:515
  9.3 4.6 %shard_map.103 = (bf16[4,2,768,256]{3,2,1,0:T(8,128)(2,1)S(1)}, f32[4,2,256]{2,1,0:T(2,128)S(1)}, f32[16,2048]{1,0:T(8,128)S(1)}, bf16[24,32,512]{2,1,0:T(8,128)(2,1)S(1)}) custom-call(s32[3,8]{1,0:T(4,128)S(1)} %get-tuple-element.23.lists, s32[64]{0:T(128)S(1)} %get-tuple-element.24.counts, s32[2]{0:T(128)S(1)} %pad_add_fusion.place, ...), custom_call_target="tpu_custom_call" | custom-call | flops 314572800 | bytes 3145728 | tf_op jit(solution)/shard_map/pallas_call | solution.py:210
  13.9 0.0 collective-permute-done.1.refs_5_.refs_0_
  13.9 3.6 %shard_map.104 = (bf16[4,2,768,256]{3,2,1,0:T(8,128)(2,1)S(1)}, f32[4,2,256]{2,1,0:T(2,128)S(1)}, f32[16,2048]{1,0:T(8,128)S(1)}) custom-call(s32[3,8]{1,0:T(4,128)S(1)} %get-tuple-element.23.lists, s32[64]{0:T(128)S(1)} %get-tuple-element.24.counts, s32[2]{0:T(128)S(1)} %pad_add_fusion.place, bf16[32,2048]{1,0:T(8,128)(2,1)S(1)} %get-tuple-element.25.refs_0_, ...), custom_call_target="tpu_custom_call" | custom-call | flops 314572800 | bytes 3145728 | tf_op jit(solution)/shard_map/pallas_call | solution.py:210
  17.5 0.0 collective-permute-start.4
  17.5 1.4 %collective-permute-done.4 = f32[16,2048]{1,0:T(8,128)S(1)} collective-permute-done((f32[16,2048]{1,0:T(8,128)S(1)}, f32[16,2048]{1,0:T(8,128)S(1)}, u32[]{:S(2)}, u32[]{:S(2)}) %collective-permute-start.4) | collective-permute-done | bytes 131104 | tf_op jit(solution)/shard_map/ppermute | solution.py:481
  18.8 1.6 %collective-permute-start.5 = (bf16[16,2048]{1,0:T(8,128)(2,1)S(1)}, bf16[16,2048]{1,0:T(8,128)(2,1)S(1)}, u32[]{:S(2)}, u32[]{:S(2)}) collective-permute-start(bf16[16,2048]{1,0:T(8,128)(2,1)S(1)} %add_convert_fusion.1), channel_id=1, source_target_pairs={{0,2},{1,3},{2,0},{3,1},{4,6},{5,7},{6,4},{7,5},{8,10},{9,11},{10,... | collective-permute-start | bytes 196616 | tf_op jit(solution)/shard_map/ppermute | solution.py:540
  20.4 2.1 %table.1 = (bf16[2,480,2048]{2,1,0:T(8,128)(2,1)S(1)}, f32[1,480]{1,0:T(1,128)S(1)}) custom-call(s32[2]{0:T(128)S(1)} %pad_add_fusion.place, s32[3,2048]{1,0:T(4,128)S(1)} %copy-done.1, f32[3,2048]{1,0:T(4,128)S(1)} %copy-done.2), custom_call_target="tpu_custom_call" | custom-call | flops 39321600 | bytes 3932160 | tf_op jit(solution)/shard_map/table/pallas_call | solution.py:380
  22.5 0.6 collective-permute-done.5
  23.2 1.4 %structure.1 = f32[16,960]{1,0:T(8,128)S(1)} custom-call(f32[16,2048]{1,0:T(8,128)S(1)} %convert_add_fusion.c_ref, bf16[960,2048]{1,0:T(8,128)(2,1)S(1)} %bitcast.15), custom_call_target="tpu_custom_call" | custom-call | flops 1006632960 | bytes 3932160 | tf_op jit(solution)/shard_map/structure/pallas_call | solution.py:408
  24.6 0.1 collective-permute-start.6
  24.7 4.2 %collective-permute-done.6 = f32[16,960]{1,0:T(8,128)S(1)} collective-permute-done((f32[16,960]{1,0:T(8,128)S(1)}, f32[16,960]{1,0:T(8,128)S(1)}, u32[]{:S(2)}, u32[]{:S(2)}) %collective-permute-start.6) | collective-permute-done | bytes 61472 | tf_op jit(solution)/shard_map/ppermute | solution.py:481
  28.9 1.6 %collective-permute-start.7 = (f32[16,960]{1,0:T(8,128)S(1)}, f32[16,960]{1,0:T(8,128)S(1)}, u32[]{:S(2)}, u32[]{:S(2)}) collective-permute-start(f32[16,960]{1,0:T(8,128)S(1)} %add.20), channel_id=1, source_target_pairs={{0,8},{4,12},{8,0},{12,4},{16,24},{20,28},{24,16},{28,20},{1,9},{5... | collective-permute-start | bytes 184328 | tf_op jit(solution)/shard_map/ppermute | solution.py:481
  30.6 2.7 %collective-permute-done.7 = f32[16,960]{1,0:T(8,128)S(1)} collective-permute-done((f32[16,960]{1,0:T(8,128)S(1)}, f32[16,960]{1,0:T(8,128)S(1)}, u32[]{:S(2)}, u32[]{:S(2)}) %collective-permute-start.7) | collective-permute-done | bytes 61472 | tf_op jit(solution)/shard_map/ppermute | solution.py:481
  33.3 3.2 %collective-permute-start.8 = (f32[16,960]{1,0:T(8,128)S(1)}, f32[16,960]{1,0:T(8,128)S(1)}, u32[]{:S(2)}, u32[]{:S(2)}) collective-permute-start(f32[16,960]{1,0:T(8,128)S(1)} %add.21), channel_id=1, source_target_pairs={{0,16},{4,20},{8,24},{12,28},{16,0},{20,4},{24,8},{28,12},{1,17},{... | collective-permute-start | bytes 184328 | tf_op jit(solution)/shard_map/ppermute | solution.py:481
  36.4 0.7 collective-permute-start.3
  37.1 2.8 %collective-permute-done.8 = f32[16,960]{1,0:T(8,128)S(1)} collective-permute-done((f32[16,960]{1,0:T(8,128)S(1)}, f32[16,960]{1,0:T(8,128)S(1)}, u32[]{:S(2)}, u32[]{:S(2)}) %collective-permute-start.8) | collective-permute-done | bytes 61472 | tf_op jit(solution)/shard_map/ppermute | solution.py:481
  39.9 1.5 %fields.1 = f32[24,2048]{1,0:T(8,128)S(1)} custom-call(s32[2]{0:T(128)S(1)} %pad_add_fusion.place, f32[16,960]{1,0:T(8,128)S(1)} %add.22.s_ref, f32[1,480]{1,0:T(1,128)S(1)} %get-tuple-element.40.weight_ref, f32[16,2048]{1,0:T(8,128)S(1)} %convert_add_fusion.c_ref, bf16[2,480,2048]{2,1,0:T(8,128)(2,1)S(1)} %get-tuple-element.39.t_ref), custom_call_target="tpu_custom_call" | custom-call | flops 503316480 | bytes 1966080 | tf_op jit(solution)/shard_map/fields/pallas_call | solution.py:445
  41.4 0.1 collective-permute-start.9
  41.5 0.1 collective-permute-start.2
  41.6 1.3 %collective-permute-done.9 = f32[24,2048]{1,0:T(8,128)S(1)} collective-permute-done((f32[24,2048]{1,0:T(8,128)S(1)}, f32[24,2048]{1,0:T(8,128)S(1)}, u32[]{:S(2)}, u32[]{:S(2)}) %collective-permute-start.9) | collective-permute-done | bytes 196640 | tf_op jit(solution)/shard_map/ppermute | solution.py:481
  42.9 1.9 %collective-permute-start.10 = (bf16[24,2048]{1,0:T(8,128)(2,1)S(1)}, bf16[24,2048]{1,0:T(8,128)(2,1)S(1)}, u32[]{:S(2)}, u32[]{:S(2)}) collective-permute-start(bf16[24,2048]{1,0:T(8,128)(2,1)S(1)} %add_convert_fusion.mine_ref), channel_id=1, source_target_pairs={{0,2},{1,3},{2,0},{3,1},{4,6},{5,7},{6,4},{7,5},{8,10},{9,11},{10,... | collective-permute-start | bytes 294920 | tf_op jit(solution)/shard_map/ppermute | solution.py:540
  44.8 2.3 %shard_map.105.refs_2_ = bf16[25,32,2048]{2,1,0:T(8,128)(2,1)} custom-call(s32[3,8]{1,0:T(4,128)S(1)} %get-tuple-element.23.lists, s32[2]{0:T(128)S(1)} %pad_add_fusion.place, bf16[25,32,2048]{2,1,0:T(8,128)(2,1)S(1)} %bitcast.11, bf16[4,2,768,256]{3,2,1,0:T(8,128)(2,1)S(1)} %get-tuple-element.35.p_ref, f32[4,2,256]{2,1,0:T(2,128)S(1)} %get-tuple-element.36.scale_ref), custom_call_target="tpu_custom_call" | custom-call | flops 629145600 | bytes 3276800 | tf_op jit(solution)/shard_map/pallas_call | solution.py:288
  47.1 0.8 %collective-permute-done.10.theirs_ref = bf16[24,2048]{1,0:T(8,128)(2,1)S(1)} collective-permute-done((bf16[24,2048]{1,0:T(8,128)(2,1)S(1)}, bf16[24,2048]{1,0:T(8,128)(2,1)S(1)}, u32[]{:S(2)}, u32[]{:S(2)}) %collective-permute-start.10) | collective-permute-done | bytes 98336 | tf_op jit(solution)/shard_map/ppermute | solution.py:540
  47.9 0.7 finish.1
  48.6 2.7 %shard_map.106.refs_0_ = bf16[25,32,2048]{2,1,0:T(8,128)(2,1)} custom-call(s32[3,8]{1,0:T(4,128)S(1)} %get-tuple-element.23.lists, s32[2]{0:T(128)S(1)} %pad_add_fusion.place, bf16[25,32,2048]{2,1,0:T(8,128)(2,1)S(1)} %bitcast.12, bf16[4,2,768,256]{3,2,1,0:T(8,128)(2,1)S(1)} %get-tuple-element.32.p_ref, ...), custom_call_target="tpu_custom_call", output_to_operand_aliasing={{}: (7, {})} | custom-call | flops 629145600 | bytes 3276800 | tf_op jit(solution)/shard_map/pallas_call | solution.py:288
  51.3 2.3 %shard_map.107.refs_2_ = bf16[25,32,2048]{2,1,0:T(8,128)(2,1)} custom-call(s32[3,8]{1,0:T(4,128)S(1)} %get-tuple-element.23.lists, s32[2]{0:T(128)S(1)} %pad_add_fusion.place, bf16[25,32,2048]{2,1,0:T(8,128)(2,1)S(1)} %bitcast.13, bf16[4,2,768,256]{3,2,1,0:T(8,128)(2,1)S(1)} %get-tuple-element.35.p_ref, ...), custom_call_target="tpu_custom_call", output_to_operand_aliasing={{}: (5, {})} | custom-call | flops 629145600 | bytes 3276800 | tf_op jit(solution)/shard_map/pallas_call | solution.py:288
  53.6 16.7 %collective-permute-done.2.refs_1_ = bf16[24,32,512]{2,1,0:T(8,128)(2,1)S(1)} collective-permute-done((bf16[24,32,512]{2,1,0:T(8,128)(2,1)S(1)}, bf16[24,32,512]{2,1,0:T(8,128)(2,1)S(1)}, u32[]{:S(2)}, u32[]{:S(2)}) %collective-permute-start.2) | collective-permute-done | bytes 786464 | tf_op jit(solution)/shard_map/ppermute | solution.py:515
  70.3 2.7 %shard_map.108 = bf16[25,32,2048]{2,1,0:T(8,128)(2,1)} custom-call(s32[3,8]{1,0:T(4,128)S(1)} %get-tuple-element.23.lists, s32[2]{0:T(128)S(1)} %pad_add_fusion.place, bf16[25,32,2048]{2,1,0:T(8,128)(2,1)S(1)} %bitcast.14, bf16[4,2,768,256]{3,2,1,0:T(8,128)(2,1)S(1)} %get-tuple-element.32.p_ref, ...), custom_call_target="tpu_custom_call", output_to_operand_aliasing={{}: (7, {})} | custom-call | flops 629145600 | bytes 3276800 | tf_op jit(solution)/shard_map/pallas_call | solution.py:288
  (14 shorter events, 0.1 us)
Async XLA Ops:
  2.8 11.1 %collective-permute-start = (bf16[64,512]{1,0:T(8,128)(2,1)S(1)}, bf16[64,512]{1,0:T(8,128)(2,1)S(1)}, u32[]{:S(2)}, u32[]{:S(2)}) collective-permute-start(bf16[64,512]{1,0:T(8,128)(2,1)S(1)} %get-tuple-element.29), channel_id=1, source_target_pairs={{4,8},{8,4},{12,16},{16,12},{20,24},{24,20},{5,9},{9,5},{13,17},{1... | collective-permute-start | bytes 196616 | tf_op jit(solution)/shard_map/ppermute | solution.py:515
  3.5 10.4 %collective-permute-start.1 = (bf16[64,512]{1,0:T(8,128)(2,1)S(1)}, bf16[64,512]{1,0:T(8,128)(2,1)S(1)}, u32[]{:S(2)}, u32[]{:S(2)}) collective-permute-start(bf16[64,512]{1,0:T(8,128)(2,1)S(1)} %get-tuple-element.30), channel_id=1, source_target_pairs={{0,4},{4,0},{8,12},{12,8},{16,20},{20,16},{24,28},{28,24},{1,5},{5... | collective-permute-start | bytes 196616 | tf_op jit(solution)/shard_map/ppermute | solution.py:515
  9.3 11.1 %copy-start.1 = (s32[3,2048]{1,0:T(4,128)S(1)}, s32[3,2048]{1,0:T(4,128)}, u32[]{:S(2)}) copy-start(s32[3,2048]{1,0:T(4,128)} %n_ref.1) | copy-start | bytes 73732
  9.3 11.1 %copy-start.2 = (f32[3,2048]{1,0:T(4,128)S(1)}, f32[3,2048]{1,0:T(4,128)}, u32[]{:S(2)}) copy-start(f32[3,2048]{1,0:T(4,128)} %f_ref.1) | copy-start | bytes 73732
  17.5 1.4 %collective-permute-start.4 = (f32[16,2048]{1,0:T(8,128)S(1)}, f32[16,2048]{1,0:T(8,128)S(1)}, u32[]{:S(2)}, u32[]{:S(2)}) collective-permute-start(f32[16,2048]{1,0:T(8,128)S(1)} %get-tuple-element.38), channel_id=1, source_target_pairs={{0,1},{1,0},{2,3},{3,2},{4,5},{5,4},{6,7},{7,6},{8,9},{9,8},{10,11... | collective-permute-start | bytes 393224 | tf_op jit(solution)/shard_map/ppermute | solution.py:481
  18.8 4.3 %collective-permute-start.5 = (bf16[16,2048]{1,0:T(8,128)(2,1)S(1)}, bf16[16,2048]{1,0:T(8,128)(2,1)S(1)}, u32[]{:S(2)}, u32[]{:S(2)}) collective-permute-start(bf16[16,2048]{1,0:T(8,128)(2,1)S(1)} %add_convert_fusion.1), channel_id=1, source_target_pairs={{0,2},{1,3},{2,0},{3,1},{4,6},{5,7},{6,4},{7,5},{8,10},{9,11},{10,... | collective-permute-start | bytes 196616 | tf_op jit(solution)/shard_map/ppermute | solution.py:540
  24.6 20.2 %copy-start = (bf16[32,25,2048]{2,0,1:T(8,128)(2,1)S(1)}, bf16[32,25,2048]{2,0,1:T(8,128)(2,1)}, u32[]{:S(2)}) copy-start(bf16[32,25,2048]{2,0,1:T(8,128)(2,1)} %param.10) | copy-start | bytes 9830404
  24.6 4.3 %collective-permute-start.6 = (f32[16,960]{1,0:T(8,128)S(1)}, f32[16,960]{1,0:T(8,128)S(1)}, u32[]{:S(2)}, u32[]{:S(2)}) collective-permute-start(f32[16,960]{1,0:T(8,128)S(1)} %structure.1), channel_id=1, source_target_pairs={{0,4},{4,0},{8,12},{12,8},{16,20},{20,16},{24,28},{28,24},{1,5},{5... | collective-permute-start | bytes 184328 | tf_op jit(solution)/shard_map/ppermute | solution.py:481
  28.9 4.3 %collective-permute-start.7 = (f32[16,960]{1,0:T(8,128)S(1)}, f32[16,960]{1,0:T(8,128)S(1)}, u32[]{:S(2)}, u32[]{:S(2)}) collective-permute-start(f32[16,960]{1,0:T(8,128)S(1)} %add.20), channel_id=1, source_target_pairs={{0,8},{4,12},{8,0},{12,4},{16,24},{20,28},{24,16},{28,20},{1,9},{5... | collective-permute-start | bytes 184328 | tf_op jit(solution)/shard_map/ppermute | solution.py:481
  33.3 6.7 %collective-permute-start.8 = (f32[16,960]{1,0:T(8,128)S(1)}, f32[16,960]{1,0:T(8,128)S(1)}, u32[]{:S(2)}, u32[]{:S(2)}) collective-permute-start(f32[16,960]{1,0:T(8,128)S(1)} %add.21), channel_id=1, source_target_pairs={{0,16},{4,20},{8,24},{12,28},{16,0},{20,4},{24,8},{28,12},{1,17},{... | collective-permute-start | bytes 184328 | tf_op jit(solution)/shard_map/ppermute | solution.py:481
  36.4 12.2 %collective-permute-start.3 = (bf16[24,32,512]{2,1,0:T(8,128)(2,1)S(1)}, bf16[24,32,512]{2,1,0:T(8,128)(2,1)S(1)}, u32[]{:S(2)}, u32[]{:S(2)}) collective-permute-start(bf16[24,32,512]{2,1,0:T(8,128)(2,1)S(1)} %get-tuple-element.37), channel_id=1, source_target_pairs={{4,8},{8,4},{12,16},{16,12},{20,24},{24,20},{5,9},{9,5},{13,17},{1... | collective-permute-start | bytes 2359304 | tf_op jit(solution)/shard_map/ppermute | solution.py:515
  41.4 1.5 %collective-permute-start.9 = (f32[24,2048]{1,0:T(8,128)S(1)}, f32[24,2048]{1,0:T(8,128)S(1)}, u32[]{:S(2)}, u32[]{:S(2)}) collective-permute-start(f32[24,2048]{1,0:T(8,128)S(1)} %fields.1), channel_id=1, source_target_pairs={{0,1},{1,0},{2,3},{3,2},{4,5},{5,4},{6,7},{7,6},{8,9},{9,8},{10,11... | collective-permute-start | bytes 589832 | tf_op jit(solution)/shard_map/ppermute | solution.py:481
  41.5 28.8 %collective-permute-start.2 = (bf16[24,32,512]{2,1,0:T(8,128)(2,1)S(1)}, bf16[24,32,512]{2,1,0:T(8,128)(2,1)S(1)}, u32[]{:S(2)}, u32[]{:S(2)}) collective-permute-start(bf16[24,32,512]{2,1,0:T(8,128)(2,1)S(1)} %get-tuple-element.34), channel_id=1, source_target_pairs={{0,4},{4,0},{8,12},{12,8},{16,20},{20,16},{24,28},{28,24},{1,5},{5... | collective-permute-start | bytes 2359304 | tf_op jit(solution)/shard_map/ppermute | solution.py:515
  42.9 5.0 %collective-permute-start.10 = (bf16[24,2048]{1,0:T(8,128)(2,1)S(1)}, bf16[24,2048]{1,0:T(8,128)(2,1)S(1)}, u32[]{:S(2)}, u32[]{:S(2)}) collective-permute-start(bf16[24,2048]{1,0:T(8,128)(2,1)S(1)} %add_convert_fusion.mine_ref), channel_id=1, source_target_pairs={{0,2},{1,3},{2,0},{3,1},{4,6},{5,7},{6,4},{7,5},{8,10},{9,11},{10,... | collective-permute-start | bytes 294920 | tf_op jit(solution)/shard_map/ppermute | solution.py:540

commit v9 on v8

--- a/solution.py
+++ b/solution.py
@@ -310,6 +310,96 @@
     )(lists, place, v, p, scale, *extra)
 
 
+def own_kernel(heads, head_chan, blocks, lists, place, v_ref, p_ref, sum_ref):
+    comps = v_ref.shape[0]
+    for i in range(REACH):
+        g = edge_block(i + REACH, place, blocks)
+        for h in range(heads):
+            rows = slice(h * head_chan, (h + 1) * head_chan)
+            acc = 0.0
+            for e in range(NNB):
+                b = lists[e, g] - place[0] * blocks
+                own = jnp.where((b >= 0) & (b < blocks), 1.0, 0.0)
+                cols = pl.ds(pl.multiple_of(jnp.clip(b, 0, blocks - 1) * BS, BS), BS)
+                v = v_ref[:, rows, cols].reshape(comps * head_chan, BS)
+                acc = acc + own * dot(v, p_ref[i + REACH, h, e * BS : (e + 1) * BS, :], ((1,), (0,)))
+            sum_ref[i, h] = acc
+
+
+def own_call(lists, place, v, p, heads):
+    comps, chans, atoms = v.shape
+    blocks = atoms // BS
+    whole = lambda shape: pl.BlockSpec(shape, lambda g, *_: (0,) * len(shape), pipeline_mode=pl.Buffered(1))
+    shape = (REACH, heads, comps * chans // heads, BS)
+    return pl.pallas_call(
+        functools.partial(own_kernel, heads, chans // heads, blocks),
+        grid_spec=pltpu.PrefetchScalarGridSpec(
+            num_scalar_prefetch=2,
+            grid=(1,),
+            in_specs=[whole(v.shape), whole(p.shape)],
+            out_specs=whole(shape),
+        ),
+        out_shape=jax.ShapeDtypeStruct(shape, F32),
+        compiler_params=params(16),
+        cost_estimate=pl.CostEstimate(
+            flops=REACH * chans * comps * NNB * BS * BS * 2, transcendentals=0,
+            bytes_accessed=REACH * chans * comps * BS * 8,
+        ),
+        name="near_own",
+    )(lists, place, v, p)
+
+
+def near_kernel(heads, head_dim, head_chan, blocks, lists, place, sum_ref, p_ref, scale_ref, small, big, prev, out_ref, acc):
+    i = pl.program_id(0)
+    g = edge_block(i + REACH, place, blocks)
+    comps = big.shape[0] + 1
+    for h in range(heads):
+        rows = slice(h * head_chan, (h + 1) * head_chan)
+        first = heads * head_dim + h * head_chan
+        acc[h] = sum_ref[i, h]
+        for e in range(NNB):
+            b = lists[e, g] - place[0] * blocks
+
+            @pl.when((b < 0) | (b >= blocks))
+            def _():
+                at = jnp.clip(jnp.where(b < 0, b + REACH, b - blocks), 0, REACH - 1)
+                cols = pl.ds(pl.multiple_of(at * BS, BS), BS)
+                v = jnp.concatenate([small[first : first + head_chan, cols][None], big[:, rows, cols]], axis=0)
+                v = v.reshape(comps * head_chan, BS)
+                acc[h] += dot(v, p_ref[i + REACH, h, e * BS : (e + 1) * BS, :], ((1,), (0,)))
+
+    for h in range(heads):
+        rows = slice(h * head_chan, (h + 1) * head_chan)
+        total = acc[h] * scale_ref[i + REACH, h : h + 1, :]
+        out_ref[:, rows, :] = total.astype(BF).reshape(comps, head_chan, BS)
+
+
+def near_call(lists, place, v_shape, sums, p, scale, halo, prev, heads, head_dim):
+    comps, chans, atoms = v_shape
+    blocks = atoms // BS
+    whole = lambda shape: pl.BlockSpec(shape, lambda g, *_: (0,) * len(shape), pipeline_mode=pl.Buffered(1))
+    return pl.pallas_call(
+        functools.partial(near_kernel, heads, head_dim, chans // heads, blocks),
+        grid_spec=pltpu.PrefetchScalarGridSpec(
+            num_scalar_prefetch=2,
+            grid=(REACH,),
+            in_specs=[whole(x.shape) for x in (sums, p, scale, *halo)] + [pl.BlockSpec(memory_space=pl.ANY)],
+            out_specs=pl.BlockSpec(
+                (comps, chans, BS), lambda i, lists, place: (0, 0, edge_block(i + REACH, place, blocks))
+            ),
+            scratch_shapes=[pltpu.VMEM(sums.shape[1:], F32)],
+        ),
+        out_shape=jax.ShapeDtypeStruct(v_shape, BF),
+        input_output_aliases={7: 0},
+        compiler_params=params(16),
+        cost_estimate=pl.CostEstimate(
+            flops=REACH * chans * comps * NNB * BS * BS, transcendentals=0,
+            bytes_accessed=REACH * chans * comps * BS * 8,
+        ),
+        name="mix_near",
+    )(lists, place, sums, p, scale, *halo, prev)
+
+
 SPREAD = 2 * KMAX + 1
 WIDE = 16
 
@@ -551,7 +641,10 @@
     attention = mix("low", lists, place, values, p_in, scale_in, (), None)
     attention = mix("far", lists, place, values, p_out, scale_out, (far, far_big), attention)
     attention = mix("high", lists, place, values, p_in, scale_in, (), attention)
-    attention = mix("near", lists, place, values, p_out, scale_out, (near, near_big), attention)
+    sums = own_call(lists, place, values, p_out, heads)
+    attention = near_call(
+        lists, place, values.shape, sums, p_out, scale_out, (near, near_big), attention, heads, head_dim
+    )
     return (attention.transpose(1, 0, 2), potential, forces)
 
 

time: 73.6 us -> 73 us (level)
  waiting for transfers between devices: 30.5 us -> 28.9 us
  Pallas kernels: 25.9 us -> 26.8 us
    pallas_call x0 -> x2, Pallas kernels: none -> 3.51 us  [the longest x1 2.1 us: near_call(): pl.pallas_call(functools.partial(near_kernel, heads, head_dim, chans // h...]
    pallas_call x4 -> x3, Pallas kernels: 10 us -> 7.33 us  [mix_call(): pl.pallas_call(functools.partial(mix_kernel, heads, head_dim, chans // he...]
    ppermute x2, waiting for transfers between devices: 1.39 us -> 0.63 us  [halfway(): lax.ppermute(x, 'inner', [(i, i ^ last) for i in range(2 * last)])]
  transfers between devices with their start and end apart: 11 -> 11, of which waited for: 8 -> 7; matrix products, arithmetic and copies ran while one was open for 0% -> 0% of each run, Pallas kernels for 22% -> 24%
where the time goes in v9:
time: 73 us; the launch traced here: 72.4 us
  waiting for transfers between devices  28.9 us (40%)
  Pallas kernels  26.8 us (37%)
  starting transfers between devices  15.8 us (22%)
  between operations  0.76 us (1%)
    ppermute x4, waiting for transfers between devices, swap(): return lax.ppermute(x, 'seq', pairs)  16 us
    ppermute x5, waiting for transfers between devices, exchanged(): return x + lax.ppermute(x, axis, [(i, i ^ step) for i in range(size)])  12.2 us
    pallas_call x2, Pallas kernels, scores_call(): pl.pallas_call(functools.partial(score_kernel, heads, head_dim, head_chan...  8.13 us
    ppermute x4, starting transfers between devices, swap(): return lax.ppermute(x, 'seq', pairs)  7.44 us
    pallas_call x3, Pallas kernels, mix_call(): pl.pallas_call(functools.partial(mix_kernel, heads, head_dim, chans // he...  7.33 us
    ppermute x5, starting transfers between devices, exchanged(): return x + lax.ppermute(x, axis, [(i, i ^ step) for i in range(size)])  4.94 us
    ppermute x2, starting transfers between devices, halfway(): lax.ppermute(x, 'inner', [(i, i ^ last) for i in range(2 * last)])  3.46 us
    pallas_call x1, Pallas kernels, table_call(): pl.pallas_call(functools.partial(table_kernel, planes, step), grid_spec=p...  2.13 us
  transfers between devices with their start and end apart: 11, of which 7 were waited for; matrix products, arithmetic and copies ran while one was open for 0% of the time, Pallas kernels for 24%

profile of v9, /device:TPU:0, one launch (start us, length us, event | category | flops | bytes accessed | tf_op | source)
XLA Modules:
  0.0 72.4 jit_solution(4369791065432129034)
XLA Ops:
  0.6 0.1 pad_add_fusion.place
  0.7 2.1 %load.1 = (bf16[64,512]{1,0:T(8,128)(2,1)S(1)}, bf16[64,512]{1,0:T(8,128)(2,1)S(1)}, bf16[24,32,512]{2,1,0:T(8,128)(2,1)S(1)}, bf16[32,2048]{1,0:T(8,128)(2,1)S(...) custom-call(s32[2]{0:T(128)S(1)} %pad_add_fusion.place, ...), custom_call_target="tpu_custom_call" | custom-call | bytes 1048576 | tf_op jit(solution)/shard_map/load/pallas_call | solution.py:88
  2.8 0.7 collective-permute-start
  3.5 5.8 %collective-permute-start.1 = (bf16[64,512]{1,0:T(8,128)(2,1)S(1)}, bf16[64,512]{1,0:T(8,128)(2,1)S(1)}, u32[]{:S(2)}, u32[]{:S(2)}) collective-permute-start(bf16[64,512]{1,0:T(8,128)(2,1)S(1)} %get-tuple-element.30), channel_id=1, source_target_pairs={{0,4},{4,0},{8,12},{12,8},{16,20},{20,16},{24,28},{28,24},{1,5},{5... | collective-permute-start | bytes 196616 | tf_op jit(solution)/shard_map/ppermute | solution.py:605
  9.3 4.6 %shard_map.103 = (bf16[4,2,768,256]{3,2,1,0:T(8,128)(2,1)S(1)}, f32[4,2,256]{2,1,0:T(2,128)S(1)}, f32[16,2048]{1,0:T(8,128)S(1)}, bf16[24,32,512]{2,1,0:T(8,128)(2,1)S(1)}) custom-call(s32[3,8]{1,0:T(4,128)S(1)} %get-tuple-element.23.lists, s32[64]{0:T(128)S(1)} %get-tuple-element.24.counts, s32[2]{0:T(128)S(1)} %pad_add_fusion.place, ...), custom_call_target="tpu_custom_call" | custom-call | flops 314572800 | bytes 3145728 | tf_op jit(solution)/shard_map/pallas_call | solution.py:210
  13.9 0.0 collective-permute-done.refs_4_.refs_0_
  13.9 3.6 %shard_map.104 = (bf16[4,2,768,256]{3,2,1,0:T(8,128)(2,1)S(1)}, f32[4,2,256]{2,1,0:T(2,128)S(1)}, f32[16,2048]{1,0:T(8,128)S(1)}) custom-call(s32[3,8]{1,0:T(4,128)S(1)} %get-tuple-element.23.lists, s32[64]{0:T(128)S(1)} %get-tuple-element.24.counts, s32[2]{0:T(128)S(1)} %pad_add_fusion.place, bf16[32,2048]{1,0:T(8,128)(2,1)S(1)} %get-tuple-element.25.refs_0_, ...), custom_call_target="tpu_custom_call" | custom-call | flops 314572800 | bytes 3145728 | tf_op jit(solution)/shard_map/pallas_call | solution.py:210
  17.5 0.0 collective-permute-start.4
  17.5 1.4 %collective-permute-done.4 = f32[16,2048]{1,0:T(8,128)S(1)} collective-permute-done((f32[16,2048]{1,0:T(8,128)S(1)}, f32[16,2048]{1,0:T(8,128)S(1)}, u32[]{:S(2)}, u32[]{:S(2)}) %collective-permute-start.4) | collective-permute-done | bytes 131104 | tf_op jit(solution)/shard_map/ppermute | solution.py:571
  18.8 1.6 %collective-permute-start.5 = (bf16[16,2048]{1,0:T(8,128)(2,1)S(1)}, bf16[16,2048]{1,0:T(8,128)(2,1)S(1)}, u32[]{:S(2)}, u32[]{:S(2)}) collective-permute-start(bf16[16,2048]{1,0:T(8,128)(2,1)S(1)} %add_convert_fusion.1), channel_id=1, source_target_pairs={{0,2},{1,3},{2,0},{3,1},{4,6},{5,7},{6,4},{7,5},{8,10},{9,11},{10,... | collective-permute-start | bytes 196616 | tf_op jit(solution)/shard_map/ppermute | solution.py:630
  20.4 2.1 %table.1 = (bf16[2,480,2048]{2,1,0:T(8,128)(2,1)S(1)}, f32[1,480]{1,0:T(1,128)S(1)}) custom-call(s32[2]{0:T(128)S(1)} %pad_add_fusion.place, s32[3,2048]{1,0:T(4,128)S(1)} %copy-done.1, f32[3,2048]{1,0:T(4,128)S(1)} %copy-done.2), custom_call_target="tpu_custom_call" | custom-call | flops 39321600 | bytes 3932160 | tf_op jit(solution)/shard_map/table/pallas_call | solution.py:470
  22.5 0.6 collective-permute-done.5
  23.2 1.4 %structure.1 = f32[16,960]{1,0:T(8,128)S(1)} custom-call(f32[16,2048]{1,0:T(8,128)S(1)} %convert_add_fusion.c_ref, bf16[960,2048]{1,0:T(8,128)(2,1)S(1)} %bitcast.15), custom_call_target="tpu_custom_call" | custom-call | flops 1006632960 | bytes 3932160 | tf_op jit(solution)/shard_map/structure/pallas_call | solution.py:498
  24.6 0.1 collective-permute-start.6
  24.7 4.2 %collective-permute-done.6 = f32[16,960]{1,0:T(8,128)S(1)} collective-permute-done((f32[16,960]{1,0:T(8,128)S(1)}, f32[16,960]{1,0:T(8,128)S(1)}, u32[]{:S(2)}, u32[]{:S(2)}) %collective-permute-start.6) | collective-permute-done | bytes 61472 | tf_op jit(solution)/shard_map/ppermute | solution.py:571
  28.9 1.6 %collective-permute-start.7 = (f32[16,960]{1,0:T(8,128)S(1)}, f32[16,960]{1,0:T(8,128)S(1)}, u32[]{:S(2)}, u32[]{:S(2)}) collective-permute-start(f32[16,960]{1,0:T(8,128)S(1)} %add.20), channel_id=1, source_target_pairs={{0,8},{4,12},{8,0},{12,4},{16,24},{20,28},{24,16},{28,20},{1,9},{5... | collective-permute-start | bytes 184328 | tf_op jit(solution)/shard_map/ppermute | solution.py:571
  30.6 2.7 %collective-permute-done.7 = f32[16,960]{1,0:T(8,128)S(1)} collective-permute-done((f32[16,960]{1,0:T(8,128)S(1)}, f32[16,960]{1,0:T(8,128)S(1)}, u32[]{:S(2)}, u32[]{:S(2)}) %collective-permute-start.7) | collective-permute-done | bytes 61472 | tf_op jit(solution)/shard_map/ppermute | solution.py:571
  33.3 3.1 %collective-permute-start.8 = (f32[16,960]{1,0:T(8,128)S(1)}, f32[16,960]{1,0:T(8,128)S(1)}, u32[]{:S(2)}, u32[]{:S(2)}) collective-permute-start(f32[16,960]{1,0:T(8,128)S(1)} %add.21), channel_id=1, source_target_pairs={{0,16},{4,20},{8,24},{12,28},{16,0},{20,4},{24,8},{28,12},{1,17},{... | collective-permute-start | bytes 184328 | tf_op jit(solution)/shard_map/ppermute | solution.py:571
  36.4 0.9 %collective-permute-start.3 = (bf16[24,32,512]{2,1,0:T(8,128)(2,1)S(1)}, bf16[24,32,512]{2,1,0:T(8,128)(2,1)S(1)}, u32[]{:S(2)}, u32[]{:S(2)}) collective-permute-start(bf16[24,32,512]{2,1,0:T(8,128)(2,1)S(1)} %get-tuple-element.37), channel_id=1, source_target_pairs={{4,8},{8,4},{12,16},{16,12},{20,24},{24,20},{5,9},{9,5},{13,17},{1... | collective-permute-start | bytes 2359304 | tf_op jit(solution)/shard_map/ppermute | solution.py:605
  37.3 2.6 %collective-permute-done.8 = f32[16,960]{1,0:T(8,128)S(1)} collective-permute-done((f32[16,960]{1,0:T(8,128)S(1)}, f32[16,960]{1,0:T(8,128)S(1)}, u32[]{:S(2)}, u32[]{:S(2)}) %collective-permute-start.8) | collective-permute-done | bytes 61472 | tf_op jit(solution)/shard_map/ppermute | solution.py:571
  39.9 1.5 %fields.1 = f32[24,2048]{1,0:T(8,128)S(1)} custom-call(s32[2]{0:T(128)S(1)} %pad_add_fusion.place, f32[16,960]{1,0:T(8,128)S(1)} %add.22.s_ref, f32[1,480]{1,0:T(1,128)S(1)} %get-tuple-element.40.weight_ref, f32[16,2048]{1,0:T(8,128)S(1)} %convert_add_fusion.c_ref, bf16[2,480,2048]{2,1,0:T(8,128)(2,1)S(1)} %get-tuple-element.39.t_ref), custom_call_target="tpu_custom_call" | custom-call | flops 503316480 | bytes 1966080 | tf_op jit(solution)/shard_map/fields/pallas_call | solution.py:535
  41.4 0.1 collective-permute-start.9
  41.5 0.1 collective-permute-start.2
  41.5 1.3 %collective-permute-done.9 = f32[24,2048]{1,0:T(8,128)S(1)} collective-permute-done((f32[24,2048]{1,0:T(8,128)S(1)}, f32[24,2048]{1,0:T(8,128)S(1)}, u32[]{:S(2)}, u32[]{:S(2)}) %collective-permute-start.9) | collective-permute-done | bytes 196640 | tf_op jit(solution)/shard_map/ppermute | solution.py:571
  42.9 1.9 %collective-permute-start.10 = (bf16[24,2048]{1,0:T(8,128)(2,1)S(1)}, bf16[24,2048]{1,0:T(8,128)(2,1)S(1)}, u32[]{:S(2)}, u32[]{:S(2)}) collective-permute-start(bf16[24,2048]{1,0:T(8,128)(2,1)S(1)} %add_convert_fusion.mine_ref), channel_id=1, source_target_pairs={{0,2},{1,3},{2,0},{3,1},{4,6},{5,7},{6,4},{7,5},{8,10},{9,11},{10,... | collective-permute-start | bytes 294920 | tf_op jit(solution)/shard_map/ppermute | solution.py:630
  44.8 2.3 %shard_map.105.refs_2_ = bf16[25,32,2048]{2,1,0:T(8,128)(2,1)} custom-call(s32[3,8]{1,0:T(4,128)S(1)} %get-tuple-element.23.lists, s32[2]{0:T(128)S(1)} %pad_add_fusion.place, bf16[25,32,2048]{2,1,0:T(8,128)(2,1)S(1)} %bitcast.11, bf16[4,2,768,256]{3,2,1,0:T(8,128)(2,1)S(1)} %get-tuple-element.35.p_ref, f32[4,2,256]{2,1,0:T(2,128)S(1)} %get-tuple-element.36.scale_ref), custom_call_target="tpu_custom_call" | custom-call | flops 629145600 | bytes 3276800 | tf_op jit(solution)/shard_map/pallas_call | solution.py:288
  47.2 1.4 %near_own.1.sum_ref = f32[2,2,400,256]{3,2,1,0:T(8,128)S(1)} custom-call(s32[3,8]{1,0:T(4,128)S(1)} %get-tuple-element.23.lists, s32[2]{0:T(128)S(1)} %pad_add_fusion.place, bf16[25,32,2048]{2,1,0:T(8,128)(2,1)S(1)} %bitcast.12, bf16[4,2,768,256]{3,2,1,0:T(8,128)(2,1)S(1)} %get-tuple-element.32.p_ref), custom_call_target="tpu_custom_call" | custom-call | flops 629145600 | bytes 3276800 | tf_op jit(solution)/shard_map/near_own/pallas_call | solution.py:334
  48.6 0.7 finish.1
  49.3 2.7 %shard_map.106.refs_0_ = bf16[25,32,2048]{2,1,0:T(8,128)(2,1)} custom-call(s32[3,8]{1,0:T(4,128)S(1)} %get-tuple-element.23.lists, s32[2]{0:T(128)S(1)} %pad_add_fusion.place, bf16[25,32,2048]{2,1,0:T(8,128)(2,1)S(1)} %bitcast.13, bf16[4,2,768,256]{3,2,1,0:T(8,128)(2,1)S(1)} %get-tuple-element.32.p_ref, ...), custom_call_target="tpu_custom_call", output_to_operand_aliasing={{}: (7, {})} | custom-call | flops 629145600 | bytes 3276800 | tf_op jit(solution)/shard_map/pallas_call | solution.py:288
  51.9 2.3 %shard_map.107.prev = bf16[25,32,2048]{2,1,0:T(8,128)(2,1)} custom-call(s32[3,8]{1,0:T(4,128)S(1)} %get-tuple-element.23.lists, s32[2]{0:T(128)S(1)} %pad_add_fusion.place, bf16[25,32,2048]{2,1,0:T(8,128)(2,1)S(1)} %bitcast.14, bf16[4,2,768,256]{3,2,1,0:T(8,128)(2,1)S(1)} %get-tuple-element.35.p_ref, ...), custom_call_target="tpu_custom_call", output_to_operand_aliasing={{}: (5, {})} | custom-call | flops 629145600 | bytes 3276800 | tf_op jit(solution)/shard_map/pallas_call | solution.py:288
  54.3 16.0 %collective-permute-done.2.big = bf16[24,32,512]{2,1,0:T(8,128)(2,1)S(1)} collective-permute-done((bf16[24,32,512]{2,1,0:T(8,128)(2,1)S(1)}, bf16[24,32,512]{2,1,0:T(8,128)(2,1)S(1)}, u32[]{:S(2)}, u32[]{:S(2)}) %collective-permute-start.2) | collective-permute-done | bytes 786464 | tf_op jit(solution)/shard_map/ppermute | solution.py:605
  70.3 2.1 %mix_near.1 = bf16[25,32,2048]{2,1,0:T(8,128)(2,1)} custom-call(s32[3,8]{1,0:T(4,128)S(1)} %get-tuple-element.23.lists, s32[2]{0:T(128)S(1)} %pad_add_fusion.place, f32[2,2,400,256]{3,2,1,0:T(8,128)S(1)} %near_own.1.sum_ref, bf16[4,2,768,256]{3,2,1,0:T(8,128)(2,1)S(1)} %get-tuple-element.32.p_ref, ...), custom_call_target="tpu_custom_call", output_to_operand_aliasing={{}: (7, {})} | custom-call | flops 314572800 | bytes 3276800 | tf_op jit(solution)/shard_map/mix_near/pallas_call | solution.py:381
  (15 shorter events, 0.1 us)
Async XLA Ops:
  2.8 11.1 %collective-permute-start = (bf16[64,512]{1,0:T(8,128)(2,1)S(1)}, bf16[64,512]{1,0:T(8,128)(2,1)S(1)}, u32[]{:S(2)}, u32[]{:S(2)}) collective-permute-start(bf16[64,512]{1,0:T(8,128)(2,1)S(1)} %get-tuple-element.29), channel_id=1, source_target_pairs={{4,8},{8,4},{12,16},{16,12},{20,24},{24,20},{5,9},{9,5},{13,17},{1... | collective-permute-start | bytes 196616 | tf_op jit(solution)/shard_map/ppermute | solution.py:605
  3.5 10.4 %collective-permute-start.1 = (bf16[64,512]{1,0:T(8,128)(2,1)S(1)}, bf16[64,512]{1,0:T(8,128)(2,1)S(1)}, u32[]{:S(2)}, u32[]{:S(2)}) collective-permute-start(bf16[64,512]{1,0:T(8,128)(2,1)S(1)} %get-tuple-element.30), channel_id=1, source_target_pairs={{0,4},{4,0},{8,12},{12,8},{16,20},{20,16},{24,28},{28,24},{1,5},{5... | collective-permute-start | bytes 196616 | tf_op jit(solution)/shard_map/ppermute | solution.py:605
  9.3 11.1 %copy-start.1 = (s32[3,2048]{1,0:T(4,128)S(1)}, s32[3,2048]{1,0:T(4,128)}, u32[]{:S(2)}) copy-start(s32[3,2048]{1,0:T(4,128)} %n_ref.1) | copy-start | bytes 73732
  9.3 11.1 %copy-start.2 = (f32[3,2048]{1,0:T(4,128)S(1)}, f32[3,2048]{1,0:T(4,128)}, u32[]{:S(2)}) copy-start(f32[3,2048]{1,0:T(4,128)} %f_ref.1) | copy-start | bytes 73732
  17.5 1.4 %collective-permute-start.4 = (f32[16,2048]{1,0:T(8,128)S(1)}, f32[16,2048]{1,0:T(8,128)S(1)}, u32[]{:S(2)}, u32[]{:S(2)}) collective-permute-start(f32[16,2048]{1,0:T(8,128)S(1)} %get-tuple-element.38), channel_id=1, source_target_pairs={{0,1},{1,0},{2,3},{3,2},{4,5},{5,4},{6,7},{7,6},{8,9},{9,8},{10,11... | collective-permute-start | bytes 393224 | tf_op jit(solution)/shard_map/ppermute | solution.py:571
  18.8 4.3 %collective-permute-start.5 = (bf16[16,2048]{1,0:T(8,128)(2,1)S(1)}, bf16[16,2048]{1,0:T(8,128)(2,1)S(1)}, u32[]{:S(2)}, u32[]{:S(2)}) collective-permute-start(bf16[16,2048]{1,0:T(8,128)(2,1)S(1)} %add_convert_fusion.1), channel_id=1, source_target_pairs={{0,2},{1,3},{2,0},{3,1},{4,6},{5,7},{6,4},{7,5},{8,10},{9,11},{10,... | collective-permute-start | bytes 196616 | tf_op jit(solution)/shard_map/ppermute | solution.py:630
  24.6 20.2 %copy-start = (bf16[32,25,2048]{2,0,1:T(8,128)(2,1)S(1)}, bf16[32,25,2048]{2,0,1:T(8,128)(2,1)}, u32[]{:S(2)}) copy-start(bf16[32,25,2048]{2,0,1:T(8,128)(2,1)} %param.10) | copy-start | bytes 9830404
  24.6 4.3 %collective-permute-start.6 = (f32[16,960]{1,0:T(8,128)S(1)}, f32[16,960]{1,0:T(8,128)S(1)}, u32[]{:S(2)}, u32[]{:S(2)}) collective-permute-start(f32[16,960]{1,0:T(8,128)S(1)} %structure.1), channel_id=1, source_target_pairs={{0,4},{4,0},{8,12},{12,8},{16,20},{20,16},{24,28},{28,24},{1,5},{5... | collective-permute-start | bytes 184328 | tf_op jit(solution)/shard_map/ppermute | solution.py:571
  28.9 4.3 %collective-permute-start.7 = (f32[16,960]{1,0:T(8,128)S(1)}, f32[16,960]{1,0:T(8,128)S(1)}, u32[]{:S(2)}, u32[]{:S(2)}) collective-permute-start(f32[16,960]{1,0:T(8,128)S(1)} %add.20), channel_id=1, source_target_pairs={{0,8},{4,12},{8,0},{12,4},{16,24},{20,28},{24,16},{28,20},{1,9},{5... | collective-permute-start | bytes 184328 | tf_op jit(solution)/shard_map/ppermute | solution.py:571
  33.3 6.6 %collective-permute-start.8 = (f32[16,960]{1,0:T(8,128)S(1)}, f32[16,960]{1,0:T(8,128)S(1)}, u32[]{:S(2)}, u32[]{:S(2)}) collective-permute-start(f32[16,960]{1,0:T(8,128)S(1)} %add.21), channel_id=1, source_target_pairs={{0,16},{4,20},{8,24},{12,28},{16,0},{20,4},{24,8},{28,12},{1,17},{... | collective-permute-start | bytes 184328 | tf_op jit(solution)/shard_map/ppermute | solution.py:571
  36.4 12.9 %collective-permute-start.3 = (bf16[24,32,512]{2,1,0:T(8,128)(2,1)S(1)}, bf16[24,32,512]{2,1,0:T(8,128)(2,1)S(1)}, u32[]{:S(2)}, u32[]{:S(2)}) collective-permute-start(bf16[24,32,512]{2,1,0:T(8,128)(2,1)S(1)} %get-tuple-element.37), channel_id=1, source_target_pairs={{4,8},{8,4},{12,16},{16,12},{20,24},{24,20},{5,9},{9,5},{13,17},{1... | collective-permute-start | bytes 2359304 | tf_op jit(solution)/shard_map/ppermute | solution.py:605
  41.4 1.5 %collective-permute-start.9 = (f32[24,2048]{1,0:T(8,128)S(1)}, f32[24,2048]{1,0:T(8,128)S(1)}, u32[]{:S(2)}, u32[]{:S(2)}) collective-permute-start(f32[24,2048]{1,0:T(8,128)S(1)} %fields.1), channel_id=1, source_target_pairs={{0,1},{1,0},{2,3},{3,2},{4,5},{5,4},{6,7},{7,6},{8,9},{9,8},{10,11... | collective-permute-start | bytes 589832 | tf_op jit(solution)/shard_map/ppermute | solution.py:571
  41.5 28.8 %collective-permute-start.2 = (bf16[24,32,512]{2,1,0:T(8,128)(2,1)S(1)}, bf16[24,32,512]{2,1,0:T(8,128)(2,1)S(1)}, u32[]{:S(2)}, u32[]{:S(2)}) collective-permute-start(bf16[24,32,512]{2,1,0:T(8,128)(2,1)S(1)} %get-tuple-element.34), channel_id=1, source_target_pairs={{0,4},{4,0},{8,12},{12,8},{16,20},{20,16},{24,28},{28,24},{1,5},{5... | collective-permute-start | bytes 2359304 | tf_op jit(solution)/shard_map/ppermute | solution.py:605
  42.9 5.6 %collective-permute-start.10 = (bf16[24,2048]{1,0:T(8,128)(2,1)S(1)}, bf16[24,2048]{1,0:T(8,128)(2,1)S(1)}, u32[]{:S(2)}, u32[]{:S(2)}) collective-permute-start(bf16[24,2048]{1,0:T(8,128)(2,1)S(1)} %add_convert_fusion.mine_ref), channel_id=1, source_target_pairs={{0,2},{1,3},{2,0},{3,1},{4,6},{5,7},{6,4},{7,5},{8,10},{9,11},{10,... | collective-permute-start | bytes 294920 | tf_op jit(solution)/shard_map/ppermute | solution.py:630

commit v10 on v9

--- a/solution.py
+++ b/solution.py
@@ -626,15 +626,17 @@
     last = lax.axis_size("inner") // 2
 
     def halfway(x):
-        x = summed(x, "inner", stop=last).astype(BF)
-        return x, lax.ppermute(x, "inner", [(i, i ^ last) for i in range(2 * last)])
-
-    mine, theirs = halfway(part)
-    charges = mine.astype(F32) + theirs.astype(F32)
+        x = summed(x, "inner", stop=last)
+        low = x.astype(BF)
+        return x, low, lax.ppermute(low, "inner", [(i, i ^ last) for i in range(2 * last)])
+
+    mine, _, theirs = halfway(part)
+    charges = mine + theirs.astype(F32)
     structure = structure_call(charges, table.reshape(-1, atoms), inv_root)
-    structure = summed(structure, "seq")
+    structure = structure + lax.ppermute(structure.astype(BF), "seq", near_pairs).astype(F32)
+    structure = summed(structure, "seq", 2)
     fields = field_call(place, structure, wave_weight, charges, table, planes)
-    fields, others = halfway(fields)
+    _, fields, others = halfway(fields)
     potential, forces = finish_call(fields, others, nq)
 
     mix = functools.partial(mix_call, heads=heads, head_dim=head_dim)

time: 73 us -> 72.7 us (level)
    ppermute x5 -> x4, waiting for transfers between devices: 12.2 us -> 8 us  [exchanged(): return x + lax.ppermute(x, axis, [(i, i ^ step) for i in range(size)])]
    ppermute x2 -> x3, waiting for transfers between devices: 0.63 us -> 4.5 us  [the longest x1 3.87 us: whole_step(): lax.ppermute(structure.astype(BF), 'seq', near_pairs).astype(F32)]
    ppermute x2 -> x3, starting transfers between devices: 3.46 us -> 3.56 us  [the longest x2 3.45 us: halfway(): lax.ppermute(low, 'inner', [(i, i ^ last) for i in range(2 * last)])]
    ppermute x5 -> x4, starting transfers between devices: 4.94 us -> 4.86 us  [exchanged(): return x + lax.ppermute(x, axis, [(i, i ^ step) for i in range(size)])]
where the time goes in v10:
time: 72.7 us; the launch traced here: 72.1 us
  waiting for transfers between devices  28.5 us (39%)
  Pallas kernels  26.7 us (37%)
  starting transfers between devices  15.9 us (22%)
  between operations  0.77 us (1%)
    ppermute x4, waiting for transfers between devices, swap(): return lax.ppermute(x, 'seq', pairs)  16 us
    pallas_call x2, Pallas kernels, scores_call(): pl.pallas_call(functools.partial(score_kernel, heads, head_dim, head_chan...  8.13 us
    ppermute x4, waiting for transfers between devices, exchanged(): return x + lax.ppermute(x, axis, [(i, i ^ step) for i in range(size)])  8 us
    ppermute x4, starting transfers between devices, swap(): return lax.ppermute(x, 'seq', pairs)  7.44 us
    pallas_call x3, Pallas kernels, mix_call(): pl.pallas_call(functools.partial(mix_kernel, heads, head_dim, chans // he...  7.33 us
    ppermute x4, starting transfers between devices, exchanged(): return x + lax.ppermute(x, axis, [(i, i ^ step) for i in range(size)])  4.86 us
    ppermute x1, waiting for transfers between devices, whole_step(): lax.ppermute(structure.astype(BF), 'seq', near_pairs).astype(F32)  3.87 us
    ppermute x2, starting transfers between devices, halfway(): lax.ppermute(low, 'inner', [(i, i ^ last) for i in range(2 * last)])  3.45 us
  transfers between devices with their start and end apart: 11, of which 7 were waited for; matrix products, arithmetic and copies ran while one was open for 0% of the time, Pallas kernels for 24%

profile of v10, /device:TPU:0, one launch (start us, length us, event | category | flops | bytes accessed | tf_op | source)
XLA Modules:
  0.0 72.1 jit_solution(1886149783274975863)
XLA Ops:
  0.6 0.1 pad_add_fusion.place
  0.7 2.1 %load.1 = (bf16[64,512]{1,0:T(8,128)(2,1)S(1)}, bf16[64,512]{1,0:T(8,128)(2,1)S(1)}, bf16[24,32,512]{2,1,0:T(8,128)(2,1)S(1)}, bf16[32,2048]{1,0:T(8,128)(2,1)S(...) custom-call(s32[2]{0:T(128)S(1)} %pad_add_fusion.place, ...), custom_call_target="tpu_custom_call" | custom-call | bytes 1048576 | tf_op jit(solution)/shard_map/load/pallas_call | solution.py:88
  2.8 0.7 collective-permute-start
  3.5 5.8 %collective-permute-start.1 = (bf16[64,512]{1,0:T(8,128)(2,1)S(1)}, bf16[64,512]{1,0:T(8,128)(2,1)S(1)}, u32[]{:S(2)}, u32[]{:S(2)}) collective-permute-start(bf16[64,512]{1,0:T(8,128)(2,1)S(1)} %get-tuple-element.30), channel_id=1, source_target_pairs={{0,4},{4,0},{8,12},{12,8},{16,20},{20,16},{24,28},{28,24},{1,5},{5... | collective-permute-start | bytes 196616 | tf_op jit(solution)/shard_map/ppermute | solution.py:605
  9.3 4.6 %shard_map.103 = (bf16[4,2,768,256]{3,2,1,0:T(8,128)(2,1)S(1)}, f32[4,2,256]{2,1,0:T(2,128)S(1)}, f32[16,2048]{1,0:T(8,128)S(1)}, bf16[24,32,512]{2,1,0:T(8,128)(2,1)S(1)}) custom-call(s32[3,8]{1,0:T(4,128)S(1)} %get-tuple-element.23.lists, s32[64]{0:T(128)S(1)} %get-tuple-element.24.counts, s32[2]{0:T(128)S(1)} %pad_add_fusion.place, ...), custom_call_target="tpu_custom_call" | custom-call | flops 314572800 | bytes 3145728 | tf_op jit(solution)/shard_map/pallas_call | solution.py:210
  13.9 0.0 collective-permute-done.refs_4_.refs_0_
  13.9 3.6 %shard_map.104 = (bf16[4,2,768,256]{3,2,1,0:T(8,128)(2,1)S(1)}, f32[4,2,256]{2,1,0:T(2,128)S(1)}, f32[16,2048]{1,0:T(8,128)S(1)}) custom-call(s32[3,8]{1,0:T(4,128)S(1)} %get-tuple-element.23.lists, s32[64]{0:T(128)S(1)} %get-tuple-element.24.counts, s32[2]{0:T(128)S(1)} %pad_add_fusion.place, bf16[32,2048]{1,0:T(8,128)(2,1)S(1)} %get-tuple-element.25.refs_0_, ...), custom_call_target="tpu_custom_call" | custom-call | flops 314572800 | bytes 3145728 | tf_op jit(solution)/shard_map/pallas_call | solution.py:210
  17.5 0.0 collective-permute-start.4
  17.5 1.4 %collective-permute-done.4 = f32[16,2048]{1,0:T(8,128)S(1)} collective-permute-done((f32[16,2048]{1,0:T(8,128)S(1)}, f32[16,2048]{1,0:T(8,128)S(1)}, u32[]{:S(2)}, u32[]{:S(2)}) %collective-permute-start.4) | collective-permute-done | bytes 131104 | tf_op jit(solution)/shard_map/ppermute | solution.py:571
  18.9 1.6 %collective-permute-start.5 = (bf16[16,2048]{1,0:T(8,128)(2,1)S(1)}, bf16[16,2048]{1,0:T(8,128)(2,1)S(1)}, u32[]{:S(2)}, u32[]{:S(2)}) collective-permute-start(bf16[16,2048]{1,0:T(8,128)(2,1)S(1)} %get-tuple-element.43), channel_id=1, source_target_pairs={{0,2},{1,3},{2,0},{3,1},{4,6},{5,7},{6,4},{7,5},{8,10},{9,11},{10,... | collective-permute-start | bytes 196616 | tf_op jit(solution)/shard_map/ppermute | solution.py:631
  20.4 2.1 %table.1 = (bf16[2,480,2048]{2,1,0:T(8,128)(2,1)S(1)}, f32[1,480]{1,0:T(1,128)S(1)}) custom-call(s32[2]{0:T(128)S(1)} %pad_add_fusion.place, s32[3,2048]{1,0:T(4,128)S(1)} %copy-done.1, f32[3,2048]{1,0:T(4,128)S(1)} %copy-done.2), custom_call_target="tpu_custom_call" | custom-call | flops 39321600 | bytes 3932160 | tf_op jit(solution)/shard_map/table/pallas_call | solution.py:470
  22.6 0.6 collective-permute-done.5
  23.2 1.4 %structure.1 = f32[16,960]{1,0:T(8,128)S(1)} custom-call(f32[16,2048]{1,0:T(8,128)S(1)} %convert_add_fusion.c_ref, bf16[960,2048]{1,0:T(8,128)(2,1)S(1)} %bitcast.15), custom_call_target="tpu_custom_call" | custom-call | flops 1006632960 | bytes 3932160 | tf_op jit(solution)/shard_map/structure/pallas_call | solution.py:498
  24.6 0.1 collective-permute-start.6
  24.7 3.9 %collective-permute-done.6 = bf16[16,960]{1,0:T(8,128)(2,1)S(1)} collective-permute-done((bf16[16,960]{1,0:T(8,128)(2,1)S(1)}, bf16[16,960]{1,0:T(8,128)(2,1)S(1)}, u32[]{:S(2)}, u32[]{:S(2)}) %collective-permute-start.6) | collective-permute-done | bytes 30752 | tf_op jit(solution)/shard_map/ppermute | solution.py:636
  28.6 1.6 %collective-permute-start.7 = (f32[16,960]{1,0:T(8,128)S(1)}, f32[16,960]{1,0:T(8,128)S(1)}, u32[]{:S(2)}, u32[]{:S(2)}) collective-permute-start(f32[16,960]{1,0:T(8,128)S(1)} %convert_add_fusion.1), channel_id=1, source_target_pairs={{0,8},{4,12},{8,0},{12,4},{16,24},{20,28},{24,16},{28,20},{1,9},{5... | collective-permute-start | bytes 184328 | tf_op jit(solution)/shard_map/ppermute | solution.py:571
  30.3 2.7 %collective-permute-done.7 = f32[16,960]{1,0:T(8,128)S(1)} collective-permute-done((f32[16,960]{1,0:T(8,128)S(1)}, f32[16,960]{1,0:T(8,128)S(1)}, u32[]{:S(2)}, u32[]{:S(2)}) %collective-permute-start.7) | collective-permute-done | bytes 61472 | tf_op jit(solution)/shard_map/ppermute | solution.py:571
  33.0 3.1 %collective-permute-start.8 = (f32[16,960]{1,0:T(8,128)S(1)}, f32[16,960]{1,0:T(8,128)S(1)}, u32[]{:S(2)}, u32[]{:S(2)}) collective-permute-start(f32[16,960]{1,0:T(8,128)S(1)} %add.21), channel_id=1, source_target_pairs={{0,16},{4,20},{8,24},{12,28},{16,0},{20,4},{24,8},{28,12},{1,17},{... | collective-permute-start | bytes 184328 | tf_op jit(solution)/shard_map/ppermute | solution.py:571
  36.1 0.9 %collective-permute-start.3 = (bf16[24,32,512]{2,1,0:T(8,128)(2,1)S(1)}, bf16[24,32,512]{2,1,0:T(8,128)(2,1)S(1)}, u32[]{:S(2)}, u32[]{:S(2)}) collective-permute-start(bf16[24,32,512]{2,1,0:T(8,128)(2,1)S(1)} %get-tuple-element.37), channel_id=1, source_target_pairs={{4,8},{8,4},{12,16},{16,12},{20,24},{24,20},{5,9},{9,5},{13,17},{1... | collective-permute-start | bytes 2359304 | tf_op jit(solution)/shard_map/ppermute | solution.py:605
  37.0 2.6 %collective-permute-done.8 = f32[16,960]{1,0:T(8,128)S(1)} collective-permute-done((f32[16,960]{1,0:T(8,128)S(1)}, f32[16,960]{1,0:T(8,128)S(1)}, u32[]{:S(2)}, u32[]{:S(2)}) %collective-permute-start.8) | collective-permute-done | bytes 61472 | tf_op jit(solution)/shard_map/ppermute | solution.py:571
  39.6 1.5 %fields.1 = f32[24,2048]{1,0:T(8,128)S(1)} custom-call(s32[2]{0:T(128)S(1)} %pad_add_fusion.place, f32[16,960]{1,0:T(8,128)S(1)} %add.22.s_ref, f32[1,480]{1,0:T(1,128)S(1)} %get-tuple-element.40.weight_ref, f32[16,2048]{1,0:T(8,128)S(1)} %convert_add_fusion.c_ref, bf16[2,480,2048]{2,1,0:T(8,128)(2,1)S(1)} %get-tuple-element.39.t_ref), custom_call_target="tpu_custom_call" | custom-call | flops 503316480 | bytes 1966080 | tf_op jit(solution)/shard_map/fields/pallas_call | solution.py:535
  41.1 0.1 collective-permute-start.9
  41.2 0.1 collective-permute-start.2
  41.3 1.3 %collective-permute-done.9 = f32[24,2048]{1,0:T(8,128)S(1)} collective-permute-done((f32[24,2048]{1,0:T(8,128)S(1)}, f32[24,2048]{1,0:T(8,128)S(1)}, u32[]{:S(2)}, u32[]{:S(2)}) %collective-permute-start.9) | collective-permute-done | bytes 196640 | tf_op jit(solution)/shard_map/ppermute | solution.py:571
  42.6 1.9 %collective-permute-start.10 = (bf16[24,2048]{1,0:T(8,128)(2,1)S(1)}, bf16[24,2048]{1,0:T(8,128)(2,1)S(1)}, u32[]{:S(2)}, u32[]{:S(2)}) collective-permute-start(bf16[24,2048]{1,0:T(8,128)(2,1)S(1)} %add_convert_fusion.mine_ref), channel_id=1, source_target_pairs={{0,2},{1,3},{2,0},{3,1},{4,6},{5,7},{6,4},{7,5},{8,10},{9,11},{10,... | collective-permute-start | bytes 294920 | tf_op jit(solution)/shard_map/ppermute | solution.py:631
  44.5 2.3 %shard_map.105.refs_2_ = bf16[25,32,2048]{2,1,0:T(8,128)(2,1)} custom-call(s32[3,8]{1,0:T(4,128)S(1)} %get-tuple-element.23.lists, s32[2]{0:T(128)S(1)} %pad_add_fusion.place, bf16[25,32,2048]{2,1,0:T(8,128)(2,1)S(1)} %bitcast.11, bf16[4,2,768,256]{3,2,1,0:T(8,128)(2,1)S(1)} %get-tuple-element.35.p_ref, f32[4,2,256]{2,1,0:T(2,128)S(1)} %get-tuple-element.36.scale_ref), custom_call_target="tpu_custom_call" | custom-call | flops 629145600 | bytes 3276800 | tf_op jit(solution)/shard_map/pallas_call | solution.py:288
  46.9 1.4 %near_own.1.sum_ref = f32[2,2,400,256]{3,2,1,0:T(8,128)S(1)} custom-call(s32[3,8]{1,0:T(4,128)S(1)} %get-tuple-element.23.lists, s32[2]{0:T(128)S(1)} %pad_add_fusion.place, bf16[25,32,2048]{2,1,0:T(8,128)(2,1)S(1)} %bitcast.12, bf16[4,2,768,256]{3,2,1,0:T(8,128)(2,1)S(1)} %get-tuple-element.32.p_ref), custom_call_target="tpu_custom_call" | custom-call | flops 629145600 | bytes 3276800 | tf_op jit(solution)/shard_map/near_own/pallas_call | solution.py:334
  48.3 0.7 finish.1
  49.0 2.7 %shard_map.106.refs_0_ = bf16[25,32,2048]{2,1,0:T(8,128)(2,1)} custom-call(s32[3,8]{1,0:T(4,128)S(1)} %get-tuple-element.23.lists, s32[2]{0:T(128)S(1)} %pad_add_fusion.place, bf16[25,32,2048]{2,1,0:T(8,128)(2,1)S(1)} %bitcast.13, bf16[4,2,768,256]{3,2,1,0:T(8,128)(2,1)S(1)} %get-tuple-element.32.p_ref, ...), custom_call_target="tpu_custom_call", output_to_operand_aliasing={{}: (7, {})} | custom-call | flops 629145600 | bytes 3276800 | tf_op jit(solution)/shard_map/pallas_call | solution.py:288
  51.6 2.3 %shard_map.107.prev = bf16[25,32,2048]{2,1,0:T(8,128)(2,1)} custom-call(s32[3,8]{1,0:T(4,128)S(1)} %get-tuple-element.23.lists, s32[2]{0:T(128)S(1)} %pad_add_fusion.place, bf16[25,32,2048]{2,1,0:T(8,128)(2,1)S(1)} %bitcast.14, bf16[4,2,768,256]{3,2,1,0:T(8,128)(2,1)S(1)} %get-tuple-element.35.p_ref, ...), custom_call_target="tpu_custom_call", output_to_operand_aliasing={{}: (5, {})} | custom-call | flops 629145600 | bytes 3276800 | tf_op jit(solution)/shard_map/pallas_call | solution.py:288
  54.0 16.0 %collective-permute-done.2.big = bf16[24,32,512]{2,1,0:T(8,128)(2,1)S(1)} collective-permute-done((bf16[24,32,512]{2,1,0:T(8,128)(2,1)S(1)}, bf16[24,32,512]{2,1,0:T(8,128)(2,1)S(1)}, u32[]{:S(2)}, u32[]{:S(2)}) %collective-permute-start.2) | collective-permute-done | bytes 786464 | tf_op jit(solution)/shard_map/ppermute | solution.py:605
  70.0 2.1 %mix_near.1 = bf16[25,32,2048]{2,1,0:T(8,128)(2,1)} custom-call(s32[3,8]{1,0:T(4,128)S(1)} %get-tuple-element.23.lists, s32[2]{0:T(128)S(1)} %pad_add_fusion.place, f32[2,2,400,256]{3,2,1,0:T(8,128)S(1)} %near_own.1.sum_ref, bf16[4,2,768,256]{3,2,1,0:T(8,128)(2,1)S(1)} %get-tuple-element.32.p_ref, ...), custom_call_target="tpu_custom_call", output_to_operand_aliasing={{}: (7, {})} | custom-call | flops 314572800 | bytes 3276800 | tf_op jit(solution)/shard_map/mix_near/pallas_call | solution.py:381
  (16 shorter events, 0.1 us)
Async XLA Ops:
  2.8 11.1 %collective-permute-start = (bf16[64,512]{1,0:T(8,128)(2,1)S(1)}, bf16[64,512]{1,0:T(8,128)(2,1)S(1)}, u32[]{:S(2)}, u32[]{:S(2)}) collective-permute-start(bf16[64,512]{1,0:T(8,128)(2,1)S(1)} %get-tuple-element.29), channel_id=1, source_target_pairs={{4,8},{8,4},{12,16},{16,12},{20,24},{24,20},{5,9},{9,5},{13,17},{1... | collective-permute-start | bytes 196616 | tf_op jit(solution)/shard_map/ppermute | solution.py:605
  3.5 10.4 %collective-permute-start.1 = (bf16[64,512]{1,0:T(8,128)(2,1)S(1)}, bf16[64,512]{1,0:T(8,128)(2,1)S(1)}, u32[]{:S(2)}, u32[]{:S(2)}) collective-permute-start(bf16[64,512]{1,0:T(8,128)(2,1)S(1)} %get-tuple-element.30), channel_id=1, source_target_pairs={{0,4},{4,0},{8,12},{12,8},{16,20},{20,16},{24,28},{28,24},{1,5},{5... | collective-permute-start | bytes 196616 | tf_op jit(solution)/shard_map/ppermute | solution.py:605
  9.3 11.1 %copy-start.1 = (s32[3,2048]{1,0:T(4,128)S(1)}, s32[3,2048]{1,0:T(4,128)}, u32[]{:S(2)}) copy-start(s32[3,2048]{1,0:T(4,128)} %n_ref.1) | copy-start | bytes 73732
  9.3 11.1 %copy-start.2 = (f32[3,2048]{1,0:T(4,128)S(1)}, f32[3,2048]{1,0:T(4,128)}, u32[]{:S(2)}) copy-start(f32[3,2048]{1,0:T(4,128)} %f_ref.1) | copy-start | bytes 73732
  17.5 1.4 %collective-permute-start.4 = (f32[16,2048]{1,0:T(8,128)S(1)}, f32[16,2048]{1,0:T(8,128)S(1)}, u32[]{:S(2)}, u32[]{:S(2)}) collective-permute-start(f32[16,2048]{1,0:T(8,128)S(1)} %get-tuple-element.38), channel_id=1, source_target_pairs={{0,1},{1,0},{2,3},{3,2},{4,5},{5,4},{6,7},{7,6},{8,9},{9,8},{10,11... | collective-permute-start | bytes 393224 | tf_op jit(solution)/shard_map/ppermute | solution.py:571
  18.9 4.3 %collective-permute-start.5 = (bf16[16,2048]{1,0:T(8,128)(2,1)S(1)}, bf16[16,2048]{1,0:T(8,128)(2,1)S(1)}, u32[]{:S(2)}, u32[]{:S(2)}) collective-permute-start(bf16[16,2048]{1,0:T(8,128)(2,1)S(1)} %get-tuple-element.43), channel_id=1, source_target_pairs={{0,2},{1,3},{2,0},{3,1},{4,6},{5,7},{6,4},{7,5},{8,10},{9,11},{10,... | collective-permute-start | bytes 196616 | tf_op jit(solution)/shard_map/ppermute | solution.py:631
  24.6 19.9 %copy-start = (bf16[32,25,2048]{2,0,1:T(8,128)(2,1)S(1)}, bf16[32,25,2048]{2,0,1:T(8,128)(2,1)}, u32[]{:S(2)}) copy-start(bf16[32,25,2048]{2,0,1:T(8,128)(2,1)} %param.10) | copy-start | bytes 9830404
  24.6 4.0 %collective-permute-start.6 = (bf16[16,960]{1,0:T(8,128)(2,1)S(1)}, bf16[16,960]{1,0:T(8,128)(2,1)S(1)}, u32[]{:S(2)}, u32[]{:S(2)}) collective-permute-start(bf16[16,960]{1,0:T(8,128)(2,1)S(1)} %convert_element_type.17), channel_id=1, source_target_pairs={{0,4},{4,0},{8,12},{12,8},{16,20},{20,16},{24,28},{28,24},{1,5},{5... | collective-permute-start | bytes 92168 | tf_op jit(solution)/shard_map/ppermute | solution.py:636
  28.6 4.3 %collective-permute-start.7 = (f32[16,960]{1,0:T(8,128)S(1)}, f32[16,960]{1,0:T(8,128)S(1)}, u32[]{:S(2)}, u32[]{:S(2)}) collective-permute-start(f32[16,960]{1,0:T(8,128)S(1)} %convert_add_fusion.1), channel_id=1, source_target_pairs={{0,8},{4,12},{8,0},{12,4},{16,24},{20,28},{24,16},{28,20},{1,9},{5... | collective-permute-start | bytes 184328 | tf_op jit(solution)/shard_map/ppermute | solution.py:571
  33.0 6.6 %collective-permute-start.8 = (f32[16,960]{1,0:T(8,128)S(1)}, f32[16,960]{1,0:T(8,128)S(1)}, u32[]{:S(2)}, u32[]{:S(2)}) collective-permute-start(f32[16,960]{1,0:T(8,128)S(1)} %add.21), channel_id=1, source_target_pairs={{0,16},{4,20},{8,24},{12,28},{16,0},{20,4},{24,8},{28,12},{1,17},{... | collective-permute-start | bytes 184328 | tf_op jit(solution)/shard_map/ppermute | solution.py:571
  36.1 12.9 %collective-permute-start.3 = (bf16[24,32,512]{2,1,0:T(8,128)(2,1)S(1)}, bf16[24,32,512]{2,1,0:T(8,128)(2,1)S(1)}, u32[]{:S(2)}, u32[]{:S(2)}) collective-permute-start(bf16[24,32,512]{2,1,0:T(8,128)(2,1)S(1)} %get-tuple-element.37), channel_id=1, source_target_pairs={{4,8},{8,4},{12,16},{16,12},{20,24},{24,20},{5,9},{9,5},{13,17},{1... | collective-permute-start | bytes 2359304 | tf_op jit(solution)/shard_map/ppermute | solution.py:605
  41.1 1.5 %collective-permute-start.9 = (f32[24,2048]{1,0:T(8,128)S(1)}, f32[24,2048]{1,0:T(8,128)S(1)}, u32[]{:S(2)}, u32[]{:S(2)}) collective-permute-start(f32[24,2048]{1,0:T(8,128)S(1)} %fields.1), channel_id=1, source_target_pairs={{0,1},{1,0},{2,3},{3,2},{4,5},{5,4},{6,7},{7,6},{8,9},{9,8},{10,11... | collective-permute-start | bytes 589832 | tf_op jit(solution)/shard_map/ppermute | solution.py:571
  41.2 28.8 %collective-permute-start.2 = (bf16[24,32,512]{2,1,0:T(8,128)(2,1)S(1)}, bf16[24,32,512]{2,1,0:T(8,128)(2,1)S(1)}, u32[]{:S(2)}, u32[]{:S(2)}) collective-permute-start(bf16[24,32,512]{2,1,0:T(8,128)(2,1)S(1)} %get-tuple-element.34), channel_id=1, source_target_pairs={{0,4},{4,0},{8,12},{12,8},{16,20},{20,16},{24,28},{28,24},{1,5},{5... | collective-permute-start | bytes 2359304 | tf_op jit(solution)/shard_map/ppermute | solution.py:605
  42.6 5.6 %collective-permute-start.10 = (bf16[24,2048]{1,0:T(8,128)(2,1)S(1)}, bf16[24,2048]{1,0:T(8,128)(2,1)S(1)}, u32[]{:S(2)}, u32[]{:S(2)}) collective-permute-start(bf16[24,2048]{1,0:T(8,128)(2,1)S(1)} %add_convert_fusion.mine_ref), channel_id=1, source_target_pairs={{0,2},{1,3},{2,0},{3,1},{4,6},{5,7},{6,4},{7,5},{8,10},{9,11},{10,... | collective-permute-start | bytes 294920 | tf_op jit(solution)/shard_map/ppermute | solution.py:631
